TPU v7x, 32 devices: a whole 2x2x4 slice. The times are simulated.
32 devices in a mesh: rep: 4 (over z), fsdp: 8 (over y, x, core).
Axes of the slice: x: 2, y: 2, z: 4, core: 2. Of those that a mesh axis runs over, the one named last changes fastest.
Arguments:
- tokens: bfloat16 [64, 512, 768], P(('rep', 'fsdp')), may hold values from -6 to 6
- cotangent: bfloat16 [64, 512, 768], P(('rep', 'fsdp')), may hold values from -6 to 6
- lengths: int32 [64], P(('rep', 'fsdp')), may hold values from 256 to 512, as said below
- live_batches: int32 [32], P(('rep', 'fsdp')), may hold values from 1 to 2, as said below
- w_qkv: bfloat16 [2, 768, 2304], P(None, 'fsdp'), may hold values from -0.21875 to 0.21875
- w_out: bfloat16 [2, 768, 768], P(None, 'fsdp'), may hold values from -0.875 to 0.875
- w_up: bfloat16 [2, 768, 3072], P(None, 'fsdp'), may hold values from -0.21875 to 0.21875
- w_down: bfloat16 [2, 3072, 768], P(None, 'fsdp'), may hold values from -0.109375 to 0.109375
- up_bias: float32 [2, 3072], P(None, 'fsdp'), may hold values from -3 to 3
- biases: float32 [2, 6, 768], P(None, None, 'fsdp'), may hold values from -3 to 3
- norm_gains: float32 [2, 2, 768], P(None, None, 'fsdp'), may hold values from 0.5 to 1.5
Outputs:
- outputs: bfloat16 [64, 512, 768], P(('rep', 'fsdp'))
- grad_tokens: bfloat16 [64, 512, 768], P(('rep', 'fsdp'))
- grad_qkv: float32 [2, 768, 2304], P(None, 'fsdp')
- grad_out: float32 [2, 768, 768], P(None, 'fsdp')
- grad_up: float32 [2, 768, 3072], P(None, 'fsdp')
- grad_down: float32 [2, 3072, 768], P(None, 'fsdp')
- grad_up_bias: float32 [2, 3072], P(None, 'fsdp')
- grad_biases: float32 [2, 6, 768], P(None, None, 'fsdp')
- grad_gains: float32 [2, 2, 768], P(None, None, 'fsdp')
Inputs may be any that keep to these rules, and one draw needn't show every extreme that they name: `lengths`: positions from a sequence's length on are padding; 512 and 256 occur in every draw. `live_batches`: entry g counts the live sequences, from the first, among sequences g * 2 to g * 2 + 2 - 1 (the rows of one device); the others are empty; 1 and 2 occur in every draw.
All inputs are finite; a program needn't handle non-finite values.
Results may differ from a plain program's by a relative error of at most 0.035.
Values may be sent and summed in bfloat16 or wider, within the bound.
A program may use at most 384 MiB of HBM per device.

v0:
```python
import jax
import jax.numpy as jnp
from jax import lax
from jax.sharding import PartitionSpec as P

HEADS = 12
HEAD = 64
LAYERS = 2


epsilon = 1e-05
big_negative = -1000000000.0
root_half = 0.7071067811865476
inv_root_tau = 0.3989422804014327


def split_heads(rows):
    return rows.reshape(rows.shape[0], HEADS, HEAD)


def norm_rows(values, gain_row, shift_row):
    middle = jnp.mean(values, axis=-1, keepdims=True)
    centred = values - middle
    spread = jnp.mean(centred * centred, axis=-1, keepdims=True)
    scaling = lax.rsqrt(spread + epsilon)
    normed = centred * scaling
    return (normed * gain_row + shift_row, normed, scaling)


def norm_back(grad_rows, normed, scaling, gain_row):
    scaled = grad_rows * gain_row
    first_mean = jnp.mean(scaled, axis=-1, keepdims=True)
    second_mean = jnp.mean(scaled * normed, axis=-1, keepdims=True)
    return scaling * (scaled - first_mean - normed * second_mean)


def gelu_slope(pre_act):
    return 0.5 * (1.0 + lax.erf(pre_act * root_half)) + pre_act * inv_root_tau * jnp.exp(
        -0.5 * pre_act * pre_act
    )


def attention_scores(queries, key_rows, key_mask):
    scores = jnp.einsum(
        "qhe,khe->hqk",
        split_heads(queries),
        split_heads(key_rows),
        preferred_element_type=jnp.float32,
    )
    return scores + key_mask[None, None, :]


def layer_forward(hidden, key_mask, weights_full):
    w_qkv, w_out, w_up, w_down, up_bias, bias_rows, gain_rows = weights_full
    model_width = w_out.shape[0]
    base_low = hidden.astype(jnp.bfloat16)
    projected = jnp.dot(base_low, w_qkv, preferred_element_type=jnp.float32)
    queries = ((projected[:, :model_width] + bias_rows[0]) * HEAD ** (-0.5)).astype(jnp.bfloat16)
    key_rows = projected[:, model_width : 2 * model_width].astype(jnp.bfloat16)
    value_rows = (projected[:, 2 * model_width :] + bias_rows[1]).astype(jnp.bfloat16)
    scores = attention_scores(queries, key_rows, key_mask)
    row_peak = jnp.max(scores, axis=-1, keepdims=True)
    row_total = jnp.sum(jnp.exp(scores - row_peak), axis=-1, keepdims=True)
    log_total = row_peak + jnp.log(row_total)
    attention = jnp.exp(scores - log_total).astype(jnp.bfloat16)
    context = jnp.einsum(
        "hqk,khe->qhe", attention, split_heads(value_rows), preferred_element_type=jnp.float32
    )
    context = context.reshape(hidden.shape[0], model_width).astype(jnp.bfloat16)
    attn_out = jnp.dot(context, w_out, preferred_element_type=jnp.float32) + bias_rows[2]
    mid_rows, normed_first, scale_first = norm_rows(hidden + attn_out, gain_rows[0], bias_rows[4])
    mid_low = mid_rows.astype(jnp.bfloat16)
    pre_act = jnp.dot(mid_low, w_up, preferred_element_type=jnp.float32) + up_bias
    act_low = jax.nn.gelu(pre_act, approximate=False).astype(jnp.bfloat16)
    ffn_out = jnp.dot(act_low, w_down, preferred_element_type=jnp.float32) + bias_rows[3]
    result, normed_second, scale_second = norm_rows(mid_rows + ffn_out, gain_rows[1], bias_rows[5])
    stored = (
        base_low,
        queries,
        key_rows,
        value_rows,
        log_total,
        context,
        normed_first,
        scale_first,
        mid_low,
        pre_act,
        act_low,
        normed_second,
        scale_second,
    )
    return (result, stored)


def layer_backward(stored, grad_rows, key_mask, weights_full):
    (
        base_low,
        queries,
        key_rows,
        value_rows,
        log_total,
        context,
        normed_first,
        scale_first,
        mid_low,
        pre_act,
        act_low,
        normed_second,
        scale_second,
    ) = stored
    w_qkv, w_out, w_up, w_down, up_bias, bias_rows, gain_rows = weights_full
    seq_rows = grad_rows.shape[0]
    model_width = w_out.shape[0]
    grad_gain_second = jnp.sum(grad_rows * normed_second, axis=0)
    grad_shift_second = jnp.sum(grad_rows, axis=0)
    grad_sum_second = norm_back(grad_rows, normed_second, scale_second, gain_rows[1])
    grad_ffn = grad_sum_second.astype(jnp.bfloat16)
    grad_down_bias = jnp.sum(grad_ffn.astype(jnp.float32), axis=0)
    grad_down = jnp.dot(act_low.T, grad_ffn, preferred_element_type=jnp.float32)
    grad_act = jnp.dot(grad_ffn, w_down.T, preferred_element_type=jnp.float32)
    grad_pre = (grad_act * gelu_slope(pre_act)).astype(jnp.bfloat16)
    grad_up_bias = jnp.sum(grad_pre.astype(jnp.float32), axis=0)
    grad_up = jnp.dot(mid_low.T, grad_pre, preferred_element_type=jnp.float32)
    grad_mid = grad_sum_second + jnp.dot(grad_pre, w_up.T, preferred_element_type=jnp.float32)
    grad_gain_first = jnp.sum(grad_mid * normed_first, axis=0)
    grad_shift_first = jnp.sum(grad_mid, axis=0)
    grad_sum_first = norm_back(grad_mid, normed_first, scale_first, gain_rows[0])
    grad_attn = grad_sum_first.astype(jnp.bfloat16)
    grad_out_bias = jnp.sum(grad_attn.astype(jnp.float32), axis=0)
    grad_out = jnp.dot(context.T, grad_attn, preferred_element_type=jnp.float32)
    grad_context = jnp.dot(grad_attn, w_out.T, preferred_element_type=jnp.float32).astype(
        jnp.bfloat16
    )
    scores = attention_scores(queries, key_rows, key_mask)
    attention = jnp.exp(scores - log_total)
    grad_attention = jnp.einsum(
        "qhe,khe->hqk",
        split_heads(grad_context),
        split_heads(value_rows),
        preferred_element_type=jnp.float32,
    )
    row_inner = jnp.sum(attention * grad_attention, axis=-1, keepdims=True)
    grad_scores = (attention * (grad_attention - row_inner)).astype(jnp.bfloat16)
    grad_query = jnp.einsum(
        "hqk,khe->qhe", grad_scores, split_heads(key_rows), preferred_element_type=jnp.float32
    ).astype(jnp.bfloat16) * HEAD ** (-0.5)
    grad_key = jnp.einsum(
        "hqk,qhe->khe", grad_scores, split_heads(queries), preferred_element_type=jnp.float32
    ).astype(jnp.bfloat16)
    grad_value = jnp.einsum(
        "hqk,qhe->khe",
        attention.astype(jnp.bfloat16),
        split_heads(grad_context),
        preferred_element_type=jnp.float32,
    ).astype(jnp.bfloat16)
    query_rows = grad_query.reshape(seq_rows, model_width)
    value_grad_rows = grad_value.reshape(seq_rows, model_width)
    grad_proj = jnp.concatenate(
        [query_rows, grad_key.reshape(seq_rows, model_width), value_grad_rows], axis=1
    )
    grad_qkv = jnp.dot(base_low.T, grad_proj, preferred_element_type=jnp.float32)
    grad_hidden = grad_sum_first + jnp.dot(grad_proj, w_qkv.T, preferred_element_type=jnp.float32)
    grad_bias_rows = jnp.stack(
        [
            jnp.sum(query_rows.astype(jnp.float32), axis=0),
            jnp.sum(value_grad_rows.astype(jnp.float32), axis=0),
            grad_out_bias,
            grad_down_bias,
            grad_shift_first,
            grad_shift_second,
        ]
    )
    grad_gain_rows = jnp.stack([grad_gain_first, grad_gain_second])
    return (
        grad_hidden,
        (grad_qkv, grad_out, grad_up, grad_down, grad_up_bias, grad_bias_rows, grad_gain_rows),
    )


def empty_store(batches, seq_len, model_width, hidden_units):
    wide_shape = (batches, seq_len, model_width)
    unit_shape = (batches, seq_len, hidden_units)
    column_shape = (batches, seq_len, 1)
    return (
        jnp.zeros(wide_shape, jnp.bfloat16),
        jnp.zeros(wide_shape, jnp.bfloat16),
        jnp.zeros(wide_shape, jnp.bfloat16),
        jnp.zeros(wide_shape, jnp.bfloat16),
        jnp.zeros((batches, HEADS, seq_len, 1), jnp.float32),
        jnp.zeros(wide_shape, jnp.bfloat16),
        jnp.zeros(wide_shape, jnp.float32),
        jnp.zeros(column_shape, jnp.float32),
        jnp.zeros(wide_shape, jnp.bfloat16),
        jnp.zeros(unit_shape, jnp.float32),
        jnp.zeros(unit_shape, jnp.bfloat16),
        jnp.zeros(wide_shape, jnp.float32),
        jnp.zeros(column_shape, jnp.float32),
    )


def forward_plain(source, weights_full, key_masks, live_count):

    def advance(micro_idx, buffer):
        result, stored = layer_forward(
            source[micro_idx].astype(jnp.float32), key_masks[micro_idx], weights_full
        )
        return buffer.at[micro_idx].set(result)

    return lax.fori_loop(0, live_count, advance, jnp.zeros(source.shape, jnp.float32))


def forward_saving(source, weights_full, key_masks, live_count, hidden_units):
    batches, seq_len, model_width = source.shape

    def advance(micro_idx, loop_state):
        buffer, stores = loop_state
        result, stored = layer_forward(source[micro_idx], key_masks[micro_idx], weights_full)
        stores = tuple(
            (
                buffer_item.at[micro_idx].set(new_item)
                for buffer_item, new_item in zip(stores, stored)
            )
        )
        return (buffer.at[micro_idx].set(result), stores)

    initial = (
        jnp.zeros(source.shape, jnp.float32),
        empty_store(batches, seq_len, model_width, hidden_units),
    )
    return lax.fori_loop(0, live_count, advance, initial)


def zero_grads(weights_full):
    return tuple((jnp.zeros(weight_item.shape, jnp.float32) for weight_item in weights_full))


def reduce_grads(totals):
    slices = (
        lax.psum_scatter(
            totals[0].astype(jnp.bfloat16), "fsdp", scatter_dimension=0, tiled=True
        ).astype(jnp.float32),
        lax.psum_scatter(
            totals[1].astype(jnp.bfloat16), "fsdp", scatter_dimension=0, tiled=True
        ).astype(jnp.float32),
        lax.psum_scatter(
            totals[2].astype(jnp.bfloat16), "fsdp", scatter_dimension=0, tiled=True
        ).astype(jnp.float32),
        lax.psum_scatter(
            totals[3].astype(jnp.bfloat16), "fsdp", scatter_dimension=0, tiled=True
        ).astype(jnp.float32),
        lax.psum_scatter(
            totals[4].astype(jnp.bfloat16), "fsdp", scatter_dimension=0, tiled=True
        ).astype(jnp.float32),
        lax.psum_scatter(
            totals[5].astype(jnp.bfloat16), "fsdp", scatter_dimension=1, tiled=True
        ).astype(jnp.float32),
        lax.psum_scatter(
            totals[6].astype(jnp.bfloat16), "fsdp", scatter_dimension=1, tiled=True
        ).astype(jnp.float32),
    )
    return (
        lax.psum(slices[0].astype(jnp.bfloat16), "rep").astype(jnp.float32),
        lax.psum(slices[1].astype(jnp.bfloat16), "rep").astype(jnp.float32),
        lax.psum(slices[2].astype(jnp.bfloat16), "rep").astype(jnp.float32),
        lax.psum(slices[3].astype(jnp.bfloat16), "rep").astype(jnp.float32),
        lax.psum(slices[4].astype(jnp.bfloat16), "rep").astype(jnp.float32),
        lax.psum(slices[5].astype(jnp.bfloat16), "rep").astype(jnp.float32),
        lax.psum(slices[6].astype(jnp.bfloat16), "rep").astype(jnp.float32),
    )


def on_device(
    tokens,
    cotangent,
    lengths,
    live_batches,
    w_qkv,
    w_out,
    w_up,
    w_down,
    up_bias,
    biases,
    norm_gains,
):
    hidden_units = w_up.shape[2]
    live_count = live_batches[0]
    places = jnp.arange(tokens.shape[1], dtype=jnp.int32)
    inside = places[None, :] < lengths[:, None]
    key_masks = jnp.where(inside, 0.0, big_negative).astype(jnp.float32)
    valid_rows = jnp.where(inside, 1.0, 0.0).astype(jnp.float32)
    kept_weights = []
    layer_inputs = []
    current = tokens
    stored_all = None
    for layer_idx in range(LAYERS):
        weights_full = (
            lax.all_gather(w_qkv[layer_idx], "fsdp", axis=0, tiled=True),
            lax.all_gather(w_out[layer_idx], "fsdp", axis=0, tiled=True),
            lax.all_gather(w_up[layer_idx], "fsdp", axis=0, tiled=True),
            lax.all_gather(w_down[layer_idx], "fsdp", axis=0, tiled=True),
            lax.all_gather(
                up_bias[layer_idx].astype(jnp.bfloat16), "fsdp", axis=0, tiled=True
            ).astype(jnp.float32),
            lax.all_gather(
                biases[layer_idx].astype(jnp.bfloat16), "fsdp", axis=1, tiled=True
            ).astype(jnp.float32),
            lax.all_gather(
                norm_gains[layer_idx].astype(jnp.bfloat16), "fsdp", axis=1, tiled=True
            ).astype(jnp.float32),
        )
        kept_weights.append(weights_full)
        layer_inputs.append(current)
        if layer_idx + 1 < LAYERS:
            current = forward_plain(current, weights_full, key_masks, live_count)
        else:
            current, stored_all = forward_saving(
                current, weights_full, key_masks, live_count, hidden_units
            )
    outputs = (current * valid_rows[:, :, None]).astype(jnp.bfloat16)
    results = [None] * LAYERS
    last_weights = kept_weights[LAYERS - 1]

    def back_last(micro_idx, loop_state):
        grad_buffer, totals = loop_state
        stored = tuple((buffer_item[micro_idx] for buffer_item in stored_all))
        grad_rows = cotangent[micro_idx].astype(jnp.float32) * valid_rows[micro_idx][:, None]
        grad_hidden, layer_grads = layer_backward(
            stored, grad_rows, key_masks[micro_idx], last_weights
        )
        totals = tuple((running + increment for running, increment in zip(totals, layer_grads)))
        return (grad_buffer.at[micro_idx].set(grad_hidden), totals)

    grad_current, totals = lax.fori_loop(
        0, live_count, back_last, (jnp.zeros(tokens.shape, jnp.float32), zero_grads(last_weights))
    )
    results[LAYERS - 1] = reduce_grads(totals)
    layer_idx = 0
    weights_full = (
        lax.all_gather(w_qkv[layer_idx], "fsdp", axis=0, tiled=True),
        lax.all_gather(w_out[layer_idx], "fsdp", axis=0, tiled=True),
        lax.all_gather(w_up[layer_idx], "fsdp", axis=0, tiled=True),
        lax.all_gather(w_down[layer_idx], "fsdp", axis=0, tiled=True),
        lax.all_gather(up_bias[layer_idx].astype(jnp.bfloat16), "fsdp", axis=0, tiled=True).astype(
            jnp.float32
        ),
        lax.all_gather(biases[layer_idx].astype(jnp.bfloat16), "fsdp", axis=1, tiled=True).astype(
            jnp.float32
        ),
        lax.all_gather(
            norm_gains[layer_idx].astype(jnp.bfloat16), "fsdp", axis=1, tiled=True
        ).astype(jnp.float32),
    )
    source = layer_inputs[layer_idx]
    grad_later = grad_current

    def back_redo(micro_idx, loop_state):
        grad_buffer, totals = loop_state
        result, stored = layer_forward(
            source[micro_idx].astype(jnp.float32), key_masks[micro_idx], weights_full
        )
        grad_hidden, layer_grads = layer_backward(
            stored, grad_later[micro_idx], key_masks[micro_idx], weights_full
        )
        totals = tuple((running + increment for running, increment in zip(totals, layer_grads)))
        return (grad_buffer.at[micro_idx].set(grad_hidden), totals)

    grad_current, totals = lax.fori_loop(
        0, live_count, back_redo, (jnp.zeros(tokens.shape, jnp.float32), zero_grads(weights_full))
    )
    results[layer_idx] = reduce_grads(totals)
    grad_tokens = grad_current.astype(jnp.bfloat16)
    stacked = tuple(
        (
            jnp.stack([results[layer_idx][member] for layer_idx in range(LAYERS)])
            for member in range(7)
        )
    )
    return (
        outputs,
        grad_tokens,
        stacked[0],
        stacked[1],
        stacked[2],
        stacked[3],
        stacked[4],
        stacked[5],
        stacked[6],
    )


def solution(mesh):
    placed = (
        P(("rep", "fsdp"), None, None),
        P(("rep", "fsdp"), None, None),
        P(("rep", "fsdp")),
        P(("rep", "fsdp")),
        P(None, "fsdp", None),
        P(None, "fsdp", None),
        P(None, "fsdp", None),
        P(None, "fsdp", None),
        P(None, "fsdp"),
        P(None, None, "fsdp"),
        P(None, None, "fsdp"),
    )
    return jax.shard_map(
        on_device,
        mesh=mesh,
        in_specs=placed,
        out_specs=(
            P(("rep", "fsdp"), None, None),
            P(("rep", "fsdp"), None, None),
            P(None, "fsdp", None),
            P(None, "fsdp", None),
            P(None, "fsdp", None),
            P(None, "fsdp", None),
            P(None, "fsdp"),
            P(None, None, "fsdp"),
            P(None, None, "fsdp"),
        ),
        check_vma=False,
    )
```

profile of v0, /device:TPU:0, one launch (start us, length us, event | category | flops | bytes accessed | tf_op | source)
XLA Modules:
  0.0 1777.1 jit_solution(6857002041597758651)
XLA Ops:
  80.8 34.9 %all-gather.27.cloned.1.call-done = bf16[1,768,3072]{2,1,0:T(8,128)(2,1)} async-done(((bf16[1,96,3072]{2,1,0:T(8,128)(2,1)}), bf16[1,768,3072]{2,1,0:T(8,128)(2,1)}) %all-gather.27.cloned.1.call-update) | async-done | bytes 4718608 | tf_op jit(solution)/shard_map/all_gather | solution.py:299
  115.6 41.1 %all-gather.29.cloned.1.call-done = bf16[1,3072,768]{2,1,0:T(8,128)(2,1)} async-done(((bf16[1,384,768]{2,1,0:T(8,128)(2,1)}), bf16[1,3072,768]{2,1,0:T(8,128)(2,1)}) %all-gather.29.cloned.1.call-update) | async-done | bytes 4718608 | tf_op jit(solution)/shard_map/all_gather | solution.py:300
  158.6 73.0 %while.111 = (s32[]{:T(128)}, f32[2,512,768]{2,1,0:T(8,128)}, s32[]{:T(128)}, bf16[2,512,768]{2,1,0:T(8,128)(2,1)}, bf16[768,2304]{1,0:T(8,128)(2,1)}, /*index=5...) while((s32[]{:T(128)}, f32[2,512,768]{2,1,0:T(8,128)}, ...), condition=%wide.region_8.9_spmd, body=%wide.region_0.8_spmd.sunk | while | flops 8195009536 | bytes 159952688 | solution.py:209
  204.5 21.4 %fusion.397 = (f32[512]{0:T(512)S(1)}, f32[512,768]{1,0:T(8,128)S(1)}) fusion(f32[768]{0:T(1024)S(1)} %get-tuple-element.1798, bf16[3072,768]{1,0:T(8,128)(2,1)} %get-tuple-element.2033, bf16[768,3072]{1,0:T(8,128)(2,1)} %get-tuple-element.2031, f32[3072]{0:T(1024)S(1)} %get-tuple-element.2032, f32[512,768]{1,0:T(8,128)S(1)} %get-tuple-element.1806, ...), kind=kOutput, calls=%fused_computation.405.clone.1 | convolution fusion | flops 4940365312 | bytes 12610560 | tf_op jit(solution)/shard_map/while/body/dot_general | solution.py:75
  231.7 28.2 %all-gather.35.cloned.1.call-done = bf16[1,768,3072]{2,1,0:T(8,128)(2,1)} async-done(((bf16[1,96,3072]{2,1,0:T(8,128)(2,1)}), bf16[1,768,3072]{2,1,0:T(8,128)(2,1)}) %all-gather.35.cloned.1.call-update) | async-done | bytes 4718608 | tf_op jit(solution)/shard_map/all_gather | solution.py:299
  260.0 41.3 %all-gather.37.cloned.1.call-done = bf16[1,3072,768]{2,1,0:T(8,128)(2,1)} async-done(((bf16[1,384,768]{2,1,0:T(8,128)(2,1)}), bf16[1,3072,768]{2,1,0:T(8,128)(2,1)}) %all-gather.37.cloned.1.call-update) | async-done | bytes 4718608 | tf_op jit(solution)/shard_map/all_gather | solution.py:300
  322.4 128.3 %while.112 = (s32[]{:T(128)}, f32[2,512,768]{2,1,0:T(8,128)}, bf16[2,512,768]{2,1,0:T(8,128)(2,1)}, bf16[2,512,768]{2,1,0:T(8,128)(2,1)}, bf16[2,512,768]{2,1,0:...) while((s32[]{:T(128)}, f32[2,512,768]{2,1,0:T(8,128)}, ...), condition=%wide.region_18.0_spmd, body=%wide.region_9.18_spmd.sunk | while | flops 8205240320 | bytes 390526496 | solution.py:230
  382.9 20.0 %fusion.413 = (bf16[2,512,3072]{2,1,0:T(8,128)(2,1)S(1)}, bf16[512,3072]{1,0:T(8,128)(2,1)S(1)}, f32[512,3072]{1,0:T(8,128)S(1)}) fusion(bf16[2,512,3072]{2,1,0:T(8,128)(2,1)S(1)} %bitcast.598, s32[]{:T(128)} %select_n.55, pred[]{:T(512)} %and_reduce_fusion.11, f32[3072]{0:T(1024)S(1)} %get-tuple-element.2124, ...), kind=kOutput, calls=%fused_computation.122.clone.1 | convolution fusion | flops 2523267072 | bytes 22044676 | tf_op jit(solution)/shard_map/while/body/dot_general | solution.py:73
  466.5 109.5 %while.113 = (s32[]{:T(128)}, f32[2,512,768]{2,1,0:T(8,128)}, f32[768,2304]{1,0:T(8,128)}, f32[768,768]{1,0:T(8,128)}, f32[768,3072]{1,0:T(8,128)}, /*index=5*/f...) while((s32[]{:T(128)}, f32[2,512,768]{2,1,0:T(8,128)}, ...), condition=%wide.region_35.0_spmd, body=%wide.region_19.35_spmd.sunk | while | flops 16609045504 | bytes 501465280 | solution.py:333
  590.4 149.2 %while.114 = (s32[]{:T(128)}, bf16[2,512,768]{2,1,0:T(8,128)(2,1)}, f32[768,2304]{1,0:T(8,128)}, f32[768,768]{1,0:T(8,128)}, f32[768,3072]{1,0:T(8,128)}, /*inde...) while((s32[]{:T(128)}, bf16[2,512,768]{2,1,0:T(8,128)(2,1)}, ...), condition=%wide.region_58.59_spmd, body=%wide.region_36.58_spmd.sunk | while | flops 24392359936 | bytes 755007680 | solution.py:367
  632.5 16.4 fusion.480
  784.2 322.4 %reduce-scatter.25.cloned.1.call-done = bf16[96,768]{1,0:T(8,128)(2,1)} async-done(((bf16[768,768]{1,0:T(8,128)(2,1)}), bf16[96,768]{1,0:T(8,128)(2,1)}) %reduce-scatter.25.cloned.1.call-update) | async-done | bytes 147472 | tf_op jit(solution)/shard_map/reduce_scatter | solution.py:242
  1106.6 40.4 %reduce-scatter.27.cloned.1.call-done = bf16[96,768]{1,0:T(8,128)(2,1)} async-done(((bf16[768,768]{1,0:T(8,128)(2,1)}), bf16[96,768]{1,0:T(8,128)(2,1)}) %reduce-scatter.27.cloned.1.call-update) | async-done | bytes 147472 | tf_op jit(solution)/shard_map/reduce_scatter | solution.py:242
  1146.9 51.5 %reduce-scatter.21.cloned.1.call-done = bf16[96,2304]{1,0:T(8,128)(2,1)} async-done(((bf16[768,2304]{1,0:T(8,128)(2,1)}), bf16[96,2304]{1,0:T(8,128)(2,1)}) %reduce-scatter.21.cloned.1.call-update) | async-done | bytes 442384 | tf_op jit(solution)/shard_map/reduce_scatter | solution.py:239
  1198.4 51.3 %reduce-scatter.23.cloned.1.call-done = bf16[96,2304]{1,0:T(8,128)(2,1)} async-done(((bf16[768,2304]{1,0:T(8,128)(2,1)}), bf16[96,2304]{1,0:T(8,128)(2,1)}) %reduce-scatter.23.cloned.1.call-update) | async-done | bytes 442384 | tf_op jit(solution)/shard_map/reduce_scatter | solution.py:239
  1249.7 57.3 %reduce-scatter.29.cloned.1.call-done = bf16[96,3072]{1,0:T(8,128)(2,1)} async-done(((bf16[768,3072]{1,0:T(8,128)(2,1)}), bf16[96,3072]{1,0:T(8,128)(2,1)}) %reduce-scatter.29.cloned.1.call-update) | async-done | bytes 589840 | tf_op jit(solution)/shard_map/reduce_scatter | solution.py:245
  1306.9 57.1 %reduce-scatter.33.cloned.1.call-done = bf16[384,768]{1,0:T(8,128)(2,1)} async-done(((bf16[3072,768]{1,0:T(8,128)(2,1)}), bf16[384,768]{1,0:T(8,128)(2,1)}) %reduce-scatter.33.cloned.1.call-update) | async-done | bytes 589840 | tf_op jit(solution)/shard_map/reduce_scatter | solution.py:248
  1364.0 57.1 %reduce-scatter.31.cloned.1.call-done = bf16[96,3072]{1,0:T(8,128)(2,1)} async-done(((bf16[768,3072]{1,0:T(8,128)(2,1)}), bf16[96,3072]{1,0:T(8,128)(2,1)}) %reduce-scatter.31.cloned.1.call-update) | async-done | bytes 589840 | tf_op jit(solution)/shard_map/reduce_scatter | solution.py:245
  1421.1 57.1 %reduce-scatter.35.cloned.1.call-done = bf16[384,768]{1,0:T(8,128)(2,1)} async-done(((bf16[3072,768]{1,0:T(8,128)(2,1)}), bf16[384,768]{1,0:T(8,128)(2,1)}) %reduce-scatter.35.cloned.1.call-update) | async-done | bytes 589840 | tf_op jit(solution)/shard_map/reduce_scatter | solution.py:248
  1479.6 22.9 %all-reduce.2 = (bf16[3072]{0:T(1024)(128)(2,1)S(1)}, bf16[3072]{0:T(1024)(128)(2,1)S(1)}) all-reduce(bf16[3072]{0:T(1024)(128)(2,1)S(1)} %convert_element_type.373, bf16[3072]{0:T(1024)(128)(2,1)S(1)} %convert_element_type.372), channel_id=25, replica_groups=mesh['rep'=4,'fsdp'=8] {'fsdp'}, use_global_device_ids=true, to_apply=%region_77.0.clone | all-reduce | flops 6144 | bytes 24576
  1515.6 36.3 %reduce-scatter.43.cloned.1.call-done = bf16[96,2]{1,0:T(8,128)(2,1)} async-done(((bf16[768,2]{1,0:T(8,128)(2,1)}), bf16[96,2]{1,0:T(8,128)(2,1)}) %reduce-scatter.43.cloned.1.call-update) | async-done | bytes 400
  1552.7 36.5 %reduce-scatter.37.cloned.1.call-done = bf16[96,6]{1,0:T(8,128)(2,1)} async-done(((bf16[768,6]{1,0:T(8,128)(2,1)}), bf16[96,6]{1,0:T(8,128)(2,1)}) %reduce-scatter.37.cloned.1.call-update) | async-done | bytes 1168
  1590.0 36.3 %reduce-scatter.39.cloned.1.call-done = bf16[96,6]{1,0:T(8,128)(2,1)} async-done(((bf16[768,6]{1,0:T(8,128)(2,1)}), bf16[96,6]{1,0:T(8,128)(2,1)}) %reduce-scatter.39.cloned.1.call-update) | async-done | bytes 1168
  1640.9 122.4 %all-reduce.7.cloned.1.call-done = (bf16[1,96,2304]{2,1,0:T(8,128)(2,1)}, bf16[1,96,2304]{2,1,0:T(8,128)(2,1)}, bf16[1,96,768]{2,1,0:T(8,128)(2,1)}, bf16[1,96,7...) async-done(((bf16[1,96,2304]{2,1,0:T(8,128)(2,1)}, ...) | async-done | bytes 3538960 | tf_op jit(solution)/shard_map/psum | solution.py:262
  (568 shorter events, 522.7 us)
Async XLA Ops:
  7.2 73.6 %all-gather.25.cloned.1.call-start = ((), (), s32[]{:S(2)}) async-start(), calls=%async_computation.21 | async-start | bytes 1327104 | tf_op jit(solution)/shard_map/all_gather | solution.py:298
  9.1 71.7 %all-gather.23.cloned.1.call-start = ((), (), s32[]{:S(2)}) async-start(), calls=%async_computation.20 | async-start | bytes 3981312 | tf_op jit(solution)/shard_map/all_gather | solution.py:297
  11.3 104.3 %all-gather.27.cloned.1.call-start = ((), (), s32[]{:S(2)}) async-start(), calls=%async_computation.22 | async-start | bytes 5308416 | tf_op jit(solution)/shard_map/all_gather | solution.py:299
  12.5 144.3 %all-gather.29.cloned.1.call-start = ((), (), s32[]{:S(2)}) async-start(), calls=%async_computation.23 | async-start | bytes 5308416 | tf_op jit(solution)/shard_map/all_gather | solution.py:300
  13.7 218.0 %all-gather.33.cloned.1.call-start = ((), (), s32[]{:S(2)}) async-start(), calls=%async_computation.25 | async-start | bytes 1327104 | tf_op jit(solution)/shard_map/all_gather | solution.py:298
  14.3 217.4 %all-gather.31.cloned.1.call-start = ((), (), s32[]{:S(2)}) async-start(), calls=%async_computation.24 | async-start | bytes 3981312 | tf_op jit(solution)/shard_map/all_gather | solution.py:297
  14.9 245.1 %all-gather.35.cloned.1.call-start = ((), (), s32[]{:S(2)}) async-start(), calls=%async_computation.26 | async-start | bytes 5308416 | tf_op jit(solution)/shard_map/all_gather | solution.py:299
  15.6 285.6 %all-gather.37.cloned.1.call-start = ((), (), s32[]{:S(2)}) async-start(), calls=%async_computation.27 | async-start | bytes 5308416 | tf_op jit(solution)/shard_map/all_gather | solution.py:300
  16.4 1090.2 %reduce-scatter.25.cloned.1.call-start = ((), (), s32[]{:S(2)}) async-start(), calls=%async_computation.14 | async-start | bytes 1327104 | tf_op jit(solution)/shard_map/reduce_scatter | solution.py:242
  742.7 404.3 %reduce-scatter.27.cloned.1.call-start = ((), (), s32[]{:S(2)}) async-start(), calls=%async_computation.15 | async-start | bytes 1327104 | tf_op jit(solution)/shard_map/reduce_scatter | solution.py:242
  743.9 454.5 %reduce-scatter.21.cloned.1.call-start = ((), (), s32[]{:S(2)}) async-start(), calls=%async_computation.12 | async-start | bytes 3981312 | tf_op jit(solution)/shard_map/reduce_scatter | solution.py:239
  749.0 500.6 %reduce-scatter.23.cloned.1.call-start = ((), (), s32[]{:S(2)}) async-start(), calls=%async_computation.13 | async-start | bytes 3981312 | tf_op jit(solution)/shard_map/reduce_scatter | solution.py:239
  754.2 552.7 %reduce-scatter.29.cloned.1.call-start = ((), (), s32[]{:S(2)}) async-start(), calls=%async_computation.16 | async-start | bytes 5308416 | tf_op jit(solution)/shard_map/reduce_scatter | solution.py:245
  760.9 603.1 %reduce-scatter.33.cloned.1.call-start = ((), (), s32[]{:S(2)}) async-start(), calls=%async_computation.18 | async-start | bytes 5308416 | tf_op jit(solution)/shard_map/reduce_scatter | solution.py:248
  767.3 653.8 %reduce-scatter.31.cloned.1.call-start = ((), (), s32[]{:S(2)}) async-start(), calls=%async_computation.17 | async-start | bytes 5308416 | tf_op jit(solution)/shard_map/reduce_scatter | solution.py:245
  773.9 704.4 %reduce-scatter.35.cloned.1.call-start = ((), (), s32[]{:S(2)}) async-start(), calls=%async_computation.19 | async-start | bytes 5308416 | tf_op jit(solution)/shard_map/reduce_scatter | solution.py:248
  780.3 699.2 %copy-start.75 = (f32[3072]{0:T(1024)S(1)}, f32[3072]{0:T(1024)}, u32[]{:S(2)}) copy-start(f32[3072]{0:T(1024)} %copy-done.74) | copy-start | bytes 36868
  780.4 722.3 %copy-start.46 = (f32[2,512,768]{2,1,0:T(8,128)S(1)}, f32[2,512,768]{2,1,0:T(8,128)}, u32[]{:S(2)}) copy-start(f32[2,512,768]{2,1,0:T(8,128)} %get-tuple-element.693) | copy-start | bytes 9437188
  780.4 722.3 %copy-start.92 = (f32[2,512]{1,0:T(2,128)S(1)}, f32[2,512]{1,0:T(2,128)}, u32[]{:S(2)}) copy-start(f32[2,512]{1,0:T(2,128)} %get-tuple-element.2145) | copy-start | bytes 12292
  780.4 734.4 %reduce-scatter.41.cloned.1.call-start = ((), (), s32[]{:S(2)}) async-start(), calls=%async_computation.30 | async-start | bytes 221184
  781.3 770.6 %reduce-scatter.43.cloned.1.call-start = ((), (), s32[]{:S(2)}) async-start(), calls=%async_computation.31 | async-start | bytes 221184
  782.3 807.0 %reduce-scatter.37.cloned.1.call-start = ((), (), s32[]{:S(2)}) async-start(), calls=%async_computation.28 | async-start | bytes 221184
  783.2 843.2 %reduce-scatter.39.cloned.1.call-start = ((), (), s32[]{:S(2)}) async-start(), calls=%async_computation.29 | async-start | bytes 221184
  784.1 979.2 %all-reduce.7.cloned.1.call-start = ((), (), s32[]{:S(2)}) async-start(), calls=%async_computation.32 | async-start | bytes 7077888 | tf_op jit(solution)/shard_map/psum | solution.py:262
  (130 other events, 2541.3 us)
Sparse Core Ops, SparseCore 0:
  9.9 26.9 all-gather.24
  38.7 35.5 all-gather.22
  76.8 38.7 all-gather.26
  118.0 38.7 all-gather.28
  158.5 23.9 all-gather.32
  184.8 33.8 all-gather.30
  221.1 38.8 all-gather.34
  262.4 38.7 all-gather.36
  742.8 363.7 reduce-scatter.24
  1110.2 36.6 reduce-scatter.26
  1150.4 47.9 reduce-scatter.20
  1201.7 47.8 reduce-scatter.22
  1253.1 53.7 reduce-scatter.28
  1310.2 53.7 reduce-scatter.32
  1367.3 53.7 reduce-scatter.30
  1424.4 53.7 reduce-scatter.34
  1481.1 33.6 reduce-scatter.40
  1518.3 33.6 reduce-scatter.42
  1555.5 33.6 reduce-scatter.36
  1592.7 33.6 reduce-scatter.38
  1629.3 133.9 all-reduce.6
where the time goes:
time: 1790 us; the launch traced here: 1780 us
  waiting for transfers between devices  1080 us (60%)
  matrix products  245 us (14%)
  local copies, waits for them, and re-layouts  131 us (7%)
  other arithmetic  120 us (7%)
  blocking collectives  92.7 us (5%)
  loops' own time  86.7 us (5%)
    reduce_scatter x2, waiting for transfers between devices, reduce_grads(): lax.psum_scatter(totals[1].astype(jnp.bfloat16), 'fsdp', scatter_dimensio...  363 us
    unnamed x25, waiting for transfers between devices  123 us
    psum x1, waiting for transfers between devices, reduce_grads(): lax.psum(slices[0].astype(jnp.bfloat16), 'rep').astype(jnp.float32)  122 us
    reduce_scatter x2, waiting for transfers between devices, reduce_grads(): lax.psum_scatter(totals[2].astype(jnp.bfloat16), 'fsdp', scatter_dimensio...  114 us
    reduce_scatter x2, waiting for transfers between devices, reduce_grads(): lax.psum_scatter(totals[3].astype(jnp.bfloat16), 'fsdp', scatter_dimensio...  114 us
    reduce_scatter x2, waiting for transfers between devices, reduce_grads(): lax.psum_scatter(totals[0].astype(jnp.bfloat16), 'fsdp', scatter_dimensio...  103 us
    all_gather x2, waiting for transfers between devices, on_device(): lax.all_gather(w_down[layer_idx], 'fsdp', axis=0, tiled=True)  82.4 us
    all_gather x2, waiting for transfers between devices, on_device(): lax.all_gather(w_up[layer_idx], 'fsdp', axis=0, tiled=True)  63.1 us
  transfers between devices with their start and end apart: 21, of which 17 were waited for; matrix products, arithmetic and copies ran while one was open for 6% of the time, Pallas kernels for 0%

commit v1 on v0

v1 whole, which is shorter than its diff:
```python
import functools

import jax
import jax.numpy as jnp
from jax import lax
from jax.experimental import pallas as pl
from jax.experimental.pallas import tpu as pltpu
from jax.sharding import PartitionSpec as P

HEAD = 64
LAYERS = 2
GROUP = 256
ROWS = 256
VMEM_BYTES = 60 * 1024 * 1024

epsilon = 1e-05
big_negative = -1000000000.0
root_half = 0.7071067811865476
inv_root_tau = 0.3989422804014327
f32 = jnp.float32
bf16 = jnp.bfloat16


def dot_nn(a, b):
    return lax.dot_general(a, b, (((1,), (0,)), ((), ())), preferred_element_type=f32)


def dot_nt(a, b):
    return lax.dot_general(a, b, (((1,), (1,)), ((), ())), preferred_element_type=f32)


def whole(shape):
    zeros = (0,) * len(shape)
    return pl.BlockSpec(shape, lambda *_: zeros, pipeline_mode=pl.Buffered(1))


def column_block(rows, width):
    return pl.BlockSpec((rows, width), lambda j, *_: (0, j))


ANY = pl.BlockSpec(memory_space=pl.ANY)


def piece_copies(me, pieces, target, sems):
    depth = pieces[0].shape[0]
    copies = []
    for mask, piece in enumerate(pieces):
        start = pl.multiple_of((me ^ mask) * depth, 16)
        copies.append(pltpu.make_async_copy(piece, target.at[pl.ds(start, depth), :], sems.at[mask]))
    return copies


def norm_forward(total, gain, shift):
    middle = jnp.mean(total, axis=-1, keepdims=True)
    centred = total - middle
    spread = jnp.mean(centred * centred, axis=-1, keepdims=True)
    scaling = lax.rsqrt(spread + epsilon)
    normed = centred * scaling
    return normed * gain + shift, normed, scaling


def norm_backward(grad, normed, scaling, gain):
    scaled = grad * gain
    first = jnp.mean(scaled, axis=-1, keepdims=True)
    second = jnp.mean(scaled * normed, axis=-1, keepdims=True)
    return scaling * (scaled - first - normed * second)


def head_mask(shape, head):
    lanes = lax.broadcasted_iota(jnp.int32, shape, 1)
    return (lanes >= head * HEAD) & (lanes < (head + 1) * HEAD)


def attend_forward_kernel(n, seqs, me_ref, x_ref, small_ref, mask_ref, *refs):
    qkv_pieces, out_pieces = refs[:n], refs[n : 2 * n]
    q_ref, k_ref, v_ref, ctx_ref, lse_ref, mid_ref, low_ref, n1_ref, r1_ref = refs[2 * n : 2 * n + 9]
    base, w_qkv, w_out, acc, sems = refs[2 * n + 9 :]
    step, steps = pl.program_id(0), pl.num_programs(0)
    rows, width = x_ref.shape
    seq = rows // seqs
    heads = GROUP // HEAD
    qkv_copies = piece_copies(me_ref[0], qkv_pieces, w_qkv, sems.at[0])
    out_copies = piece_copies(me_ref[0], out_pieces, w_out, sems.at[1])

    @pl.when(step == 0)
    def _():
        for copy in qkv_copies:
            copy.start()
        for copy in out_copies:
            copy.start()
        base[...] = x_ref[...].astype(bf16)
        for copy in qkv_copies:
            copy.wait()
        for copy in out_copies:
            copy.wait()

    columns = pl.multiple_of(step * GROUP, GROUP)
    q_bias = small_ref[0:1, pl.ds(columns, GROUP)]
    v_bias = small_ref[1:2, pl.ds(columns, GROUP)]

    def project(block, carry):
        at = pl.ds(pl.multiple_of(block * ROWS, ROWS), ROWS)
        low = base[at, :]
        q = dot_nn(low, w_qkv[:, pl.ds(columns, GROUP)])
        q_ref[at, :] = ((q + q_bias) * HEAD ** (-0.5)).astype(bf16)
        k = dot_nn(low, w_qkv[:, pl.ds(pl.multiple_of(width + columns, GROUP), GROUP)])
        k_ref[at, :] = k.astype(bf16)
        v = dot_nn(low, w_qkv[:, pl.ds(pl.multiple_of(2 * width + columns, GROUP), GROUP)])
        v_ref[at, :] = (v + v_bias).astype(bf16)
        return carry

    lax.fori_loop(0, rows // ROWS, project, 0)

    def attend(s, carry):
        at = pl.ds(pl.multiple_of(s * seq, seq), seq)
        q, k = q_ref[at, :], k_ref[at, :]
        v_turned = v_ref[at, :].T
        key_mask = mask_ref[at, :]
        parts = []
        for head in range(heads):
            q_head = jnp.where(head_mask(q.shape, head), q, jnp.zeros_like(q))
            scores = dot_nt(k, q_head) + key_mask
            peak = jnp.max(scores, axis=0, keepdims=True)
            raised = jnp.exp(scores - peak)
            total = jnp.sum(raised, axis=0, keepdims=True)
            mixed = dot_nn(v_turned[head * HEAD : (head + 1) * HEAD, :], raised.astype(bf16))
            parts.append((mixed / total).astype(bf16))
            lse_ref[0, pl.ds(s * heads + head, 1), :] = peak + jnp.log(total)
        ctx_ref[at, :] = jnp.concatenate(parts, axis=0).T
        return carry

    lax.fori_loop(0, seqs, attend, 0)

    def mix(block, carry):
        at = pl.ds(pl.multiple_of(block * ROWS, ROWS), ROWS)
        term = dot_nn(ctx_ref[at, :], w_out[pl.ds(columns, GROUP), :])

        @pl.when(step == 0)
        def _():
            acc[at, :] = term

        @pl.when(step > 0)
        def _():
            acc[at, :] += term

        @pl.when(step == steps - 1)
        def _():
            total = x_ref[at, :].astype(f32) + acc[at, :] + small_ref[2:3, :]
            mid, normed, scaling = norm_forward(total, small_ref[6:7, :], small_ref[4:5, :])
            mid_ref[at, :] = mid
            low_ref[at, :] = mid.astype(bf16)
            n1_ref[at, :] = normed.astype(bf16)
            r1_ref[at, :] = scaling

        return carry

    lax.fori_loop(0, rows // ROWS, mix, 0)


def attend_forward(me, x, small, key_mask, qkv_pieces, out_pieces, seqs):
    n = len(qkv_pieces)
    rows, width = x.shape
    steps = width // GROUP
    seq = rows // seqs
    wide = jax.ShapeDtypeStruct((rows, width), bf16)
    heads = GROUP // HEAD
    return pl.pallas_call(
        functools.partial(attend_forward_kernel, n, seqs),
        out_shape=(
            wide,
            wide,
            wide,
            wide,
            jax.ShapeDtypeStruct((steps, seqs * heads, seq), f32),
            jax.ShapeDtypeStruct((rows, width), f32),
            wide,
            wide,
            jax.ShapeDtypeStruct((rows, 1), f32),
        ),
        grid_spec=pltpu.PrefetchScalarGridSpec(
            num_scalar_prefetch=1,
            grid=(steps,),
            in_specs=[whole((rows, width)), whole(small.shape), whole((rows, 1))] + [ANY] * (2 * n),
            out_specs=[column_block(rows, GROUP)] * 4
            + [
                pl.BlockSpec((1, seqs * heads, seq), lambda j, *_: (j, 0, 0)),
                whole((rows, width)),
                whole((rows, width)),
                whole((rows, width)),
                whole((rows, 1)),
            ],
            scratch_shapes=[
                pltpu.VMEM((rows, width), bf16),
                pltpu.VMEM((width, 3 * width), bf16),
                pltpu.VMEM((width, width), bf16),
                pltpu.VMEM((rows, width), f32),
                pltpu.SemaphoreType.DMA((2, n)),
            ],
        ),
        compiler_params=pltpu.CompilerParams(
            dimension_semantics=("arbitrary",), vmem_limit_bytes=VMEM_BYTES
        ),
        cost_estimate=cost(8 * rows * width * width + 16 * rows * seq * width, 20 * rows * width),
        name="attend_forward",
    )(me, x, small, key_mask, *qkv_pieces, *out_pieces)


def ffn_forward_kernel(n, last, me_ref, mid_ref, low_ref, small_ref, up_bias_ref, valid_ref, *refs):
    up_pieces, down_pieces = refs[:n], refs[n : 2 * n]
    outs = refs[2 * n :]
    act_ref, slope_ref, n2_ref, r2_ref, hid_ref = outs[:5]
    if last:
        w_up, w_down, acc, sems = outs[5:]
    else:
        hid_low_ref, w_up, w_down, acc, sems = outs[5:]
    step, steps = pl.program_id(0), pl.num_programs(0)
    rows, width = mid_ref.shape
    chunk = act_ref.shape[1]
    up_copies = piece_copies(me_ref[0], up_pieces, w_up, sems.at[0])
    down_copies = piece_copies(me_ref[0], down_pieces, w_down, sems.at[1])

    @pl.when(step == 0)
    def _():
        for copy in up_copies:
            copy.start()
        for copy in down_copies:
            copy.start()
        for copy in up_copies:
            copy.wait()
        for copy in down_copies:
            copy.wait()

    columns = pl.multiple_of(step * chunk, chunk)
    tile = 256

    def block_step(block, carry):
        at = pl.ds(pl.multiple_of(block * ROWS, ROWS), ROWS)
        low = low_ref[at, :]
        for part in range(chunk // tile):
            inside = slice(part * tile, (part + 1) * tile)
            at_units = pl.ds(pl.multiple_of(columns + part * tile, tile), tile)
            pre = dot_nn(low, w_up[:, at_units]) + up_bias_ref[:, inside]
            share = 0.5 * (1.0 + lax.erf(pre * root_half))
            act_ref[at, inside] = (pre * share).astype(bf16)
            density = inv_root_tau * jnp.exp(-0.5 * pre * pre)
            slope_ref[at, inside] = (share + pre * density).astype(bf16)
        term = dot_nn(act_ref[at, :], w_down[pl.ds(columns, chunk), :])

        @pl.when(step == 0)
        def _():
            acc[at, :] = term

        @pl.when(step > 0)
        def _():
            acc[at, :] += term

        @pl.when(step == steps - 1)
        def _():
            total = mid_ref[at, :] + acc[at, :] + small_ref[3:4, :]
            hidden, normed, scaling = norm_forward(total, small_ref[7:8, :], small_ref[5:6, :])
            n2_ref[at, :] = normed.astype(bf16)
            r2_ref[at, :] = scaling
            if last:
                hid_ref[at, :] = (hidden * valid_ref[at, :]).astype(bf16)
            else:
                hid_ref[at, :] = hidden
                hid_low_ref[at, :] = hidden.astype(bf16)

        return carry

    lax.fori_loop(0, rows // ROWS, block_step, 0)


def ffn_forward(me, mid, low, small, up_bias, valid, up_pieces, down_pieces, last):
    n = len(up_pieces)
    rows, width = mid.shape
    units = up_bias.shape[1]
    chunk = width
    steps = units // chunk
    out_shape = [
        jax.ShapeDtypeStruct((rows, units), bf16),
        jax.ShapeDtypeStruct((rows, units), bf16),
        jax.ShapeDtypeStruct((rows, width), bf16),
        jax.ShapeDtypeStruct((rows, 1), f32),
        jax.ShapeDtypeStruct((rows, width), bf16 if last else f32),
    ]
    out_specs = [column_block(rows, chunk)] * 2 + [
        whole((rows, width)),
        whole((rows, 1)),
        whole((rows, width)),
    ]
    if not last:
        out_shape.append(jax.ShapeDtypeStruct((rows, width), bf16))
        out_specs.append(whole((rows, width)))
    return pl.pallas_call(
        functools.partial(ffn_forward_kernel, n, last),
        out_shape=tuple(out_shape),
        grid_spec=pltpu.PrefetchScalarGridSpec(
            num_scalar_prefetch=1,
            grid=(steps,),
            in_specs=[
                whole((rows, width)),
                whole((rows, width)),
                whole(small.shape),
                column_block(1, chunk),
                whole((rows, 1)),
            ]
            + [ANY] * (2 * n),
            out_specs=out_specs,
            scratch_shapes=[
                pltpu.VMEM((width, units), bf16),
                pltpu.VMEM((units, width), bf16),
                pltpu.VMEM((rows, width), f32),
                pltpu.SemaphoreType.DMA((2, n)),
            ],
        ),
        compiler_params=pltpu.CompilerParams(
            dimension_semantics=("arbitrary",), vmem_limit_bytes=VMEM_BYTES
        ),
        cost_estimate=cost(8 * rows * width * units, 8 * rows * units),
        name="ffn_forward",
    )(me, mid, low, small, up_bias, valid, *up_pieces, *down_pieces)


def shard_copies(n, me, source_of, keep_of, send_of, sems):
    def each(start):
        for owner in range(n):
            mask = me ^ owner
            place = mask // 2

            @pl.when(mask % 2 == 0)
            def _():
                copy = pltpu.make_async_copy(source_of(owner), keep_of(place), sems.at[owner])
                copy.start() if start else copy.wait()

            @pl.when(mask % 2 == 1)
            def _():
                copy = pltpu.make_async_copy(source_of(owner), send_of(place), sems.at[owner])
                copy.start() if start else copy.wait()

    return each


def ffn_backward_kernel(n, me_ref, g_ref, valid_ref, n2_ref, r2_ref, low_ref, n1_ref, r1_ref, small_ref, act_ref, slope_ref, *refs):
    up_pieces, down_pieces = refs[:n], refs[n : 2 * n]
    gs1_ref, ga1_ref, sums_ref, up_sum_ref, down_keep, down_send, up_keep, up_send = refs[2 * n : 2 * n + 8]
    w_up, w_down, gs2, gffn, gpre, acc, low_turned, d_down, d_up, sems, out_sems = refs[2 * n + 8 :]
    step, steps = pl.program_id(0), pl.num_programs(0)
    me = me_ref[0]
    rows, width = gs2.shape
    chunk = act_ref.shape[1]
    per_down = down_keep.shape[1]
    per_up = up_keep.shape[2]
    tile = 256
    up_copies = piece_copies(me, up_pieces, w_up, sems.at[0])
    down_copies = piece_copies(me, down_pieces, w_down, sems.at[1])

    @pl.when(step == 0)
    def _():
        for copy in down_copies:
            copy.start()
        for copy in up_copies:
            copy.start()
        sums_ref[...] = jnp.zeros_like(sums_ref)

        def prepare(block, carry):
            at = pl.ds(pl.multiple_of(block * ROWS, ROWS), ROWS)
            grad = g_ref[at, :].astype(f32) * valid_ref[at, :]
            normed = n2_ref[at, :].astype(f32)
            summed = norm_backward(grad, normed, r2_ref[at, :], small_ref[7:8, :])
            gs2[at, :] = summed
            low = summed.astype(bf16)
            gffn[at, :] = low
            sums_ref[0:1, :] += jnp.sum(grad * normed, axis=0, keepdims=True)
            sums_ref[1:2, :] += jnp.sum(grad, axis=0, keepdims=True)
            sums_ref[2:3, :] += jnp.sum(low.astype(f32), axis=0, keepdims=True)
            low_turned[:, at] = low_ref[at, :].T
            return carry

        lax.fori_loop(0, rows // ROWS, prepare, 0)
        for copy in down_copies:
            copy.wait()
        for copy in up_copies:
            copy.wait()

    columns = pl.multiple_of(step * chunk, chunk)
    up_sum_ref[...] = jnp.zeros_like(up_sum_ref)

    def through(block, carry):
        at = pl.ds(pl.multiple_of(block * ROWS, ROWS), ROWS)
        grad = gffn[at, :]
        for part in range(chunk // tile):
            inside = slice(part * tile, (part + 1) * tile)
            at_units = pl.ds(pl.multiple_of(columns + part * tile, tile), tile)
            grad_act = dot_nt(grad, w_down[at_units, :])
            low = (grad_act * slope_ref[at, inside].astype(f32)).astype(bf16)
            gpre[at, inside] = low
            up_sum_ref[:, inside] += jnp.sum(low.astype(f32), axis=0, keepdims=True)
        term = dot_nt(gpre[at, :], w_up[:, pl.ds(columns, chunk)])

        @pl.when(step == 0)
        def _():
            acc[at, :] = term

        @pl.when(step > 0)
        def _():
            acc[at, :] += term

        return carry

    lax.fori_loop(0, rows // ROWS, through, 0)

    def down_out(which):
        def run(start):
            for local in range(chunk // per_down):
                owner = which * (chunk // per_down) + local
                mask = me ^ owner
                source = d_down.at[pl.ds(local * per_down, per_down), :]
                place = mask // 2

                @pl.when(mask % 2 == 0)
                def _():
                    copy = pltpu.make_async_copy(source, down_keep.at[place], out_sems.at[0, local])
                    copy.start() if start else copy.wait()

                @pl.when(mask % 2 == 1)
                def _():
                    copy = pltpu.make_async_copy(source, down_send.at[place], out_sems.at[0, local])
                    copy.start() if start else copy.wait()

        return run

    def up_out(which):
        return shard_copies(
            n,
            me,
            lambda owner: d_up.at[pl.ds(owner * per_up, per_up), :],
            lambda place: up_keep.at[place, which],
            lambda place: up_send.at[place, which],
            out_sems.at[1],
        )

    @pl.when(step > 0)
    def _():
        down_out(step - 1)(False)

    def down_part(part, carry):
        at = pl.ds(pl.multiple_of(part * tile, tile), tile)
        turned = act_ref[:, at].T
        d_down[at, :] = dot_nn(turned, gffn[...]).astype(bf16)
        return carry

    lax.fori_loop(0, chunk // tile, down_part, 0)
    down_out(step)(True)

    @pl.when(step > 0)
    def _():
        up_out(step - 1)(False)

    def up_part(part, carry):
        at = pl.ds(pl.multiple_of(part * tile, tile), tile)
        d_up[at, :] = dot_nn(low_turned[at, :], gpre[...]).astype(bf16)
        return carry

    lax.fori_loop(0, width // tile, up_part, 0)
    up_out(step)(True)

    @pl.when(step == steps - 1)
    def _():
        def finish(block, carry):
            at = pl.ds(pl.multiple_of(block * ROWS, ROWS), ROWS)
            grad = gs2[at, :] + acc[at, :]
            normed = n1_ref[at, :].astype(f32)
            summed = norm_backward(grad, normed, r1_ref[at, :], small_ref[6:7, :])
            gs1_ref[at, :] = summed
            low = summed.astype(bf16)
            ga1_ref[at, :] = low
            sums_ref[3:4, :] += jnp.sum(grad * normed, axis=0, keepdims=True)
            sums_ref[4:5, :] += jnp.sum(grad, axis=0, keepdims=True)
            sums_ref[5:6, :] += jnp.sum(low.astype(f32), axis=0, keepdims=True)
            return carry

        lax.fori_loop(0, rows // ROWS, finish, 0)
        down_out(step)(False)
        up_out(step)(False)


def ffn_backward(me, grad, valid, n2, r2, low, n1, r1, small, act, slope, up_pieces, down_pieces):
    n = len(up_pieces)
    rows, width = grad.shape
    units = act.shape[1]
    chunk = width
    steps = units // chunk
    chips = n // 2
    down_half = jax.ShapeDtypeStruct((chips, units // n, width), bf16)
    up_half = jax.ShapeDtypeStruct((chips, steps, width // n, chunk), bf16)
    return pl.pallas_call(
        functools.partial(ffn_backward_kernel, n),
        out_shape=(
            jax.ShapeDtypeStruct((rows, width), f32),
            jax.ShapeDtypeStruct((rows, width), bf16),
            jax.ShapeDtypeStruct((8, width), f32),
            jax.ShapeDtypeStruct((1, units), f32),
            down_half,
            down_half,
            up_half,
            up_half,
        ),
        grid_spec=pltpu.PrefetchScalarGridSpec(
            num_scalar_prefetch=1,
            grid=(steps,),
            in_specs=[
                whole((rows, width)),
                whole((rows, 1)),
                whole((rows, width)),
                whole((rows, 1)),
                whole((rows, width)),
                whole((rows, width)),
                whole((rows, 1)),
                whole(small.shape),
                column_block(rows, chunk),
                column_block(rows, chunk),
            ]
            + [ANY] * (2 * n),
            out_specs=[
                whole((rows, width)),
                whole((rows, width)),
                whole((8, width)),
                column_block(1, chunk),
            ]
            + [ANY] * 4,
            scratch_shapes=[
                pltpu.VMEM((width, units), bf16),
                pltpu.VMEM((units, width), bf16),
                pltpu.VMEM((rows, width), f32),
                pltpu.VMEM((rows, width), bf16),
                pltpu.VMEM((rows, chunk), bf16),
                pltpu.VMEM((rows, width), f32),
                pltpu.VMEM((width, rows), bf16),
                pltpu.VMEM((chunk, width), bf16),
                pltpu.VMEM((width, chunk), bf16),
                pltpu.SemaphoreType.DMA((2, n)),
                pltpu.SemaphoreType.DMA((2, n)),
            ],
        ),
        compiler_params=pltpu.CompilerParams(
            dimension_semantics=("arbitrary",), vmem_limit_bytes=VMEM_BYTES
        ),
        cost_estimate=cost(10 * rows * width * units, 8 * rows * units),
        name="ffn_backward",
    )(me, grad, valid, n2, r2, low, n1, r1, small, act, slope, *up_pieces, *down_pieces)


def attend_backward_kernel(n, seqs, me_ref, ga_ref, gs_ref, base_ref, mask_ref, q_ref, k_ref, v_ref, ctx_ref, lse_ref, *refs):
    qkv_pieces, out_pieces = refs[:n], refs[n : 2 * n]
    gh_ref, sums_ref, qkv_keep, qkv_send, out_keep, out_send = refs[2 * n : 2 * n + 6]
    w_qkv, w_out, acc, base_turned, gctx, gproj, d_qkv, d_out, p_all, ds_all, sems, out_sems = refs[2 * n + 6 :]
    step, steps = pl.program_id(0), pl.num_programs(0)
    me = me_ref[0]
    rows, width = ga_ref.shape
    seq = rows // seqs
    heads = GROUP // HEAD
    per = width // n
    tile = 256
    qkv_copies = piece_copies(me, qkv_pieces, w_qkv, sems.at[0])
    out_copies = piece_copies(me, out_pieces, w_out, sems.at[1])

    @pl.when(step == 0)
    def _():
        for copy in out_copies:
            copy.start()
        for copy in qkv_copies:
            copy.start()

        def turn(block, carry):
            at = pl.ds(pl.multiple_of(block * ROWS, ROWS), ROWS)
            base_turned[:, at] = base_ref[at, :].T
            return carry

        lax.fori_loop(0, rows // ROWS, turn, 0)
        for copy in out_copies:
            copy.wait()
        for copy in qkv_copies:
            copy.wait()

    columns = pl.multiple_of(step * GROUP, GROUP)

    def through(block, carry):
        at = pl.ds(pl.multiple_of(block * ROWS, ROWS), ROWS)
        gctx[at, :] = dot_nt(ga_ref[at, :], w_out[pl.ds(columns, GROUP), :]).astype(bf16)
        return carry

    lax.fori_loop(0, rows // ROWS, through, 0)
    d_out[pl.ds(columns, GROUP), :] = dot_nn(ctx_ref[...].T, ga_ref[...]).astype(bf16)

    def attend(s, carry):
        at = pl.ds(pl.multiple_of(s * seq, seq), seq)
        q, k, v, grad = q_ref[at, :], k_ref[at, :], v_ref[at, :], gctx[at, :]
        k_turned = k.T
        key_mask = mask_ref[at, :]
        parts, q_heads, g_heads = [], [], []
        for head in range(heads):
            inside = head_mask(q.shape, head)
            q_head = jnp.where(inside, q, jnp.zeros_like(q))
            g_head = jnp.where(inside, grad, jnp.zeros_like(grad))
            scores = dot_nt(k, q_head) + key_mask
            attention = jnp.exp(scores - lse_ref[0, pl.ds(s * heads + head, 1), :])
            weighted = attention * dot_nt(v, g_head)
            inner = jnp.sum(weighted, axis=0, keepdims=True)
            grad_scores = (weighted - attention * inner).astype(bf16)
            here = slice(head * seq, (head + 1) * seq)
            p_all[:, here] = attention.astype(bf16)
            ds_all[:, here] = grad_scores
            turned = dot_nn(k_turned[head * HEAD : (head + 1) * HEAD, :], grad_scores)
            parts.append(turned.astype(bf16) * HEAD ** (-0.5))
            q_heads.append(q_head)
            g_heads.append(g_head)
        gproj[at, 0:GROUP] = jnp.concatenate(parts, axis=0).T
        gproj[at, GROUP : 2 * GROUP] = dot_nn(ds_all[...], jnp.concatenate(q_heads, axis=0)).astype(bf16)
        gproj[at, 2 * GROUP : 3 * GROUP] = dot_nn(p_all[...], jnp.concatenate(g_heads, axis=0)).astype(bf16)
        return carry

    lax.fori_loop(0, seqs, attend, 0)
    sums_ref[...] = jnp.zeros_like(sums_ref)

    def onward(block, carry):
        at = pl.ds(pl.multiple_of(block * ROWS, ROWS), ROWS)
        term = dot_nt(gproj[at, 0:GROUP], w_qkv[:, pl.ds(columns, GROUP)])
        term += dot_nt(gproj[at, GROUP : 2 * GROUP], w_qkv[:, pl.ds(pl.multiple_of(width + columns, GROUP), GROUP)])
        term += dot_nt(gproj[at, 2 * GROUP : 3 * GROUP], w_qkv[:, pl.ds(pl.multiple_of(2 * width + columns, GROUP), GROUP)])
        sums_ref[0:1, :] += jnp.sum(gproj[at, 0:GROUP].astype(f32), axis=0, keepdims=True)
        sums_ref[1:2, :] += jnp.sum(gproj[at, 2 * GROUP : 3 * GROUP].astype(f32), axis=0, keepdims=True)

        @pl.when(step == 0)
        def _():
            acc[at, :] = gs_ref[at, :] + term

        @pl.when(step > 0)
        def _():
            acc[at, :] += term

        @pl.when(step == steps - 1)
        def _():
            gh_ref[at, :] = acc[at, :].astype(gh_ref.dtype)

        return carry

    lax.fori_loop(0, rows // ROWS, onward, 0)

    def qkv_out(which, start):
        for part in range(3):
            at = pl.ds(pl.multiple_of(which * GROUP, GROUP), GROUP)
            shard_copies(
                n,
                me,
                lambda owner: d_qkv.at[pl.ds(owner * per, per), pl.ds(part * GROUP, GROUP)],
                lambda place: qkv_keep.at[place, part, :, at],
                lambda place: qkv_send.at[place, part, :, at],
                out_sems.at[part],
            )(start)

    @pl.when(step > 0)
    def _():
        qkv_out(step - 1, False)

    def weight_part(part, carry):
        at = pl.ds(pl.multiple_of(part * tile, tile), tile)
        d_qkv[at, :] = dot_nn(base_turned[at, :], gproj[...]).astype(bf16)
        return carry

    lax.fori_loop(0, width // tile, weight_part, 0)
    qkv_out(step, True)

    @pl.when(step == steps - 1)
    def _():
        out_copy = shard_copies(
            n,
            me,
            lambda owner: d_out.at[pl.ds(owner * per, per), :],
            lambda place: out_keep.at[place],
            lambda place: out_send.at[place],
            out_sems.at[3],
        )
        out_copy(True)
        qkv_out(step, False)
        out_copy(False)


def attend_backward(me, ga, gs, base, key_mask, q, k, v, ctx, lse, qkv_pieces, out_pieces, seqs, out_type):
    n = len(qkv_pieces)
    rows, width = ga.shape
    steps = width // GROUP
    seq = rows // seqs
    heads = GROUP // HEAD
    chips = n // 2
    qkv_half = jax.ShapeDtypeStruct((chips, 3, width // n, width), bf16)
    out_half = jax.ShapeDtypeStruct((chips, width // n, width), bf16)
    return pl.pallas_call(
        functools.partial(attend_backward_kernel, n, seqs),
        out_shape=(
            jax.ShapeDtypeStruct((rows, width), out_type),
            jax.ShapeDtypeStruct((8, width), f32),
            qkv_half,
            qkv_half,
            out_half,
            out_half,
        ),
        grid_spec=pltpu.PrefetchScalarGridSpec(
            num_scalar_prefetch=1,
            grid=(steps,),
            in_specs=[whole((rows, width))] * 3
            + [whole((rows, 1))]
            + [column_block(rows, GROUP)] * 4
            + [pl.BlockSpec((1, seqs * heads, seq), lambda j, *_: (j, 0, 0))]
            + [ANY] * (2 * n),
            out_specs=[whole((rows, width)), column_block(8, GROUP)] + [ANY] * 4,
            scratch_shapes=[
                pltpu.VMEM((width, 3 * width), bf16),
                pltpu.VMEM((width, width), bf16),
                pltpu.VMEM((rows, width), f32),
                pltpu.VMEM((width, rows), bf16),
                pltpu.VMEM((rows, GROUP), bf16),
                pltpu.VMEM((rows, 3 * GROUP), bf16),
                pltpu.VMEM((width, 3 * GROUP), bf16),
                pltpu.VMEM((width, width), bf16),
                pltpu.VMEM((seq, heads * seq), bf16),
                pltpu.VMEM((seq, heads * seq), bf16),
                pltpu.SemaphoreType.DMA((2, n)),
                pltpu.SemaphoreType.DMA((4, n)),
            ],
        ),
        compiler_params=pltpu.CompilerParams(
            dimension_semantics=("arbitrary",), vmem_limit_bytes=VMEM_BYTES
        ),
        cost_estimate=cost(16 * rows * width * width + 40 * rows * seq * width, 20 * rows * width),
        name="attend_backward",
    )(me, ga, gs, base, key_mask, q, k, v, ctx, lse, *qkv_pieces, *out_pieces)


def cost(flops, moved):
    return pl.CostEstimate(flops=int(flops), bytes_accessed=int(moved), transcendentals=0)


def swap(array, axis, count, mask):
    return lax.ppermute(array, axis, [(i, i ^ mask) for i in range(count)])


def gather_pieces(own, n, bits):
    pieces = {0: own}
    for bit in bits:
        for mask, piece in list(pieces.items()):
            pieces[mask | bit] = swap(piece, "fsdp", n, bit)
    return [pieces[mask] for mask in range(n)]


def scatter_pieces(keep, send, n, bits):
    other = swap(send, "fsdp", n, 1)
    terms = {place: [keep[place], other[place]] for place in range(n // 2)}

    def total(items):
        return sum(item.astype(f32) for item in items)

    for bit in bits:
        half = bit // 2
        leaving = [place for place in sorted(terms) if place & half]
        packed = jnp.stack([total(terms[place]).astype(bf16) for place in leaving])
        arrived = swap(packed, "fsdp", n, bit)
        for slot, place in enumerate(leaving):
            terms[place ^ half].append(arrived[slot])
            del terms[place]
    return total(terms[0])


def sum_replicas(shards, rank, count):
    def parts_of(array, index):
        split = array.reshape((count, array.shape[0] // count) + array.shape[1:])
        return lax.dynamic_index_in_dim(split, index, 0, keepdims=False)

    def packed(index):
        return jnp.concatenate([parts_of(array, index) for array in shards], axis=0)

    total = packed(rank)
    for mask in range(1, count):
        total = total + swap(packed(rank ^ mask).astype(bf16), "rep", count, mask).astype(f32)
    low = total.astype(bf16)
    pieces = jnp.stack([low] + [swap(low, "rep", count, mask) for mask in range(1, count)])
    ordered = [lax.dynamic_index_in_dim(pieces, rank ^ place, 0, keepdims=False) for place in range(count)]
    results = []
    start = 0
    for array in shards:
        size = array.shape[0] // count
        rows = [piece[start : start + size] for piece in ordered]
        results.append(jnp.concatenate(rows, axis=0).astype(f32))
        start += size
    return results


def gather_small(own, n, me):
    array = own[None]
    bit = 1
    while bit < n:
        other = swap(array, "fsdp", n, bit)
        upper = (me // bit) % 2 == 1
        array = jnp.concatenate([jnp.where(upper, other, array), jnp.where(upper, array, other)], axis=0)
        bit *= 2
    return array


def on_device(n, reps, tokens, cotangent, lengths, live_batches, w_qkv, w_out, w_up, w_down, up_bias, biases, norm_gains):
    seqs, seq, width = tokens.shape
    rows = seqs * seq
    units = w_up.shape[2]
    per = width // n
    me = lax.axis_index("fsdp").astype(jnp.int32)
    rank = lax.axis_index("rep").astype(jnp.int32)
    me_row = me[None]

    places = jnp.arange(seq, dtype=jnp.int32)
    inside = places[None, :] < lengths[:, None]
    alive = jnp.arange(seqs, dtype=jnp.int32) < live_batches[0]
    key_mask = jnp.where(inside, 0.0, big_negative).astype(f32).reshape(rows, 1)
    valid = jnp.where(inside & alive[:, None], 1.0, 0.0).astype(f32).reshape(rows, 1)
    ones = jnp.ones((rows, 1), f32)

    own_small = jnp.concatenate([up_bias.reshape(-1), biases.reshape(-1), norm_gains.reshape(-1)])
    small_all = gather_small(own_small, n, me)
    cut_a = LAYERS * units // n
    cut_b = cut_a + LAYERS * 6 * per
    up_bias_all = small_all[:, :cut_a].reshape(n, LAYERS, units // n).transpose(1, 0, 2).reshape(LAYERS, 1, units)
    bias_all = small_all[:, cut_a:cut_b].reshape(n, LAYERS, 6, per).transpose(1, 2, 0, 3).reshape(LAYERS, 6, width)
    gain_all = small_all[:, cut_b:].reshape(n, LAYERS, 2, per).transpose(1, 2, 0, 3).reshape(LAYERS, 2, width)
    smalls = jnp.concatenate([bias_all, gain_all], axis=1)

    chip_bits = []
    bit = 2
    while bit < n:
        chip_bits.append(bit)
        bit *= 2
    upward = chip_bits + [1]
    downward = chip_bits[::-1] + [1]

    qkv, out, up, down = [], [], [], []
    for layer in range(LAYERS):
        qkv.append(gather_pieces(w_qkv[layer], n, upward))
        out.append(gather_pieces(w_out[layer], n, downward))
        up.append(gather_pieces(w_up[layer], n, downward))
        down.append(gather_pieces(w_down[layer], n, upward))

    current = tokens.reshape(rows, width)
    base = current
    saved = []
    for layer in range(LAYERS):
        last = layer == LAYERS - 1
        q, k, v, ctx, lse, mid, low, n1, r1 = attend_forward(
            me_row, current, smalls[layer], key_mask, qkv[layer], out[layer], seqs
        )
        results = ffn_forward(
            me_row, mid, low, smalls[layer], up_bias_all[layer], valid, up[layer], down[layer], last
        )
        act, slope, n2, r2, current = results[:5]
        saved.append((base, q, k, v, ctx, lse, low, n1, r1, act, slope, n2, r2))
        if not last:
            base = results[5]
    outputs = current.reshape(seqs, seq, width)

    grad = cotangent.reshape(rows, width)
    grad_valid = valid
    shard_sums = [None] * LAYERS
    small_sums = [None] * LAYERS
    for layer in range(LAYERS - 1, -1, -1):
        base, q, k, v, ctx, lse, low, n1, r1, act, slope, n2, r2 = saved[layer]
        gs1, ga1, sums, up_sum, down_keep, down_send, up_keep, up_send = ffn_backward(
            me_row, grad, grad_valid, n2, r2, low, n1, r1, smalls[layer], act, slope, up[layer], down[layer]
        )
        grad, proj_sums, qkv_keep, qkv_send, out_keep, out_send = attend_backward(
            me_row, ga1, gs1, base, key_mask, q, k, v, ctx, lse, qkv[layer], out[layer], seqs,
            f32 if layer else bf16,
        )
        grad_valid = ones
        d_down = scatter_pieces(down_keep, down_send, n, chip_bits[::-1])
        d_up = scatter_pieces(up_keep, up_send, n, chip_bits)
        d_down, d_up = sum_replicas([d_down, d_up.reshape(-1, width)], rank, reps)
        d_qkv = scatter_pieces(qkv_keep, qkv_send, n, chip_bits[::-1])
        d_out = scatter_pieces(out_keep, out_send, n, chip_bits)
        d_qkv, d_out = sum_replicas([d_qkv.reshape(-1, width), d_out], rank, reps)
        d_up = d_up.reshape(units // width, per, width).transpose(1, 0, 2).reshape(per, units)
        d_qkv = d_qkv.reshape(3, per, width).transpose(1, 0, 2).reshape(per, 3 * width)
        shard_sums[layer] = (d_qkv, d_out, d_up, d_down)
        bias_sums = jnp.stack([proj_sums[0], proj_sums[1], sums[5], sums[2], sums[4], sums[1]])
        gain_sums = jnp.stack([sums[3], sums[0]])
        small_sums[layer] = (up_sum.reshape(n, units // n), bias_sums, gain_sums)
    grad_tokens = grad.reshape(seqs, seq, width)

    ups = jnp.stack([small_sums[layer][0] for layer in range(LAYERS)], axis=1).reshape(n, -1)
    bias_rows = jnp.stack([small_sums[layer][1] for layer in range(LAYERS)])
    bias_rows = bias_rows.reshape(LAYERS * 6, n, per).transpose(1, 0, 2).reshape(n, -1)
    gain_rows = jnp.stack([small_sums[layer][2] for layer in range(LAYERS)])
    gain_rows = gain_rows.reshape(LAYERS * 2, n, per).transpose(1, 0, 2).reshape(n, -1)
    small_total = jnp.concatenate([ups, bias_rows, gain_rows], axis=1)
    bit = 1
    while bit < n:
        small_total = small_total + swap(small_total, "fsdp", n, bit)
        bit *= 2
    mine = lax.dynamic_index_in_dim(small_total, me, 0, keepdims=True)
    bit = 1
    while bit < reps:
        mine = mine + swap(mine, "rep", reps, bit)
        bit *= 2
    mine = mine[0]
    grad_up_bias = mine[:cut_a].reshape(LAYERS, units // n)
    grad_biases = mine[cut_a:cut_b].reshape(LAYERS, 6, per)
    grad_gains = mine[cut_b:].reshape(LAYERS, 2, per)

    stacked = [jnp.stack([shard_sums[layer][member] for layer in range(LAYERS)]) for member in range(4)]
    return (outputs, grad_tokens, *stacked, grad_up_bias, grad_biases, grad_gains)


def solution(mesh):
    both = ("rep", "fsdp")
    placed = (
        P(both, None, None),
        P(both, None, None),
        P(both),
        P(both),
        P(None, "fsdp", None),
        P(None, "fsdp", None),
        P(None, "fsdp", None),
        P(None, "fsdp", None),
        P(None, "fsdp"),
        P(None, None, "fsdp"),
        P(None, None, "fsdp"),
    )
    return jax.shard_map(
        functools.partial(on_device, mesh.shape["fsdp"], mesh.shape["rep"]),
        mesh=mesh,
        in_specs=placed,
        out_specs=(
            P(both, None, None),
            P(both, None, None),
            P(None, "fsdp", None),
            P(None, "fsdp", None),
            P(None, "fsdp", None),
            P(None, "fsdp", None),
            P(None, "fsdp"),
            P(None, None, "fsdp"),
            P(None, None, "fsdp"),
        ),
        check_vma=False,
    )
```

time: 1790 us -> 797 us (0.45)
  waiting for transfers between devices: 1080 us -> 253 us
  Pallas kernels: 0 us -> 324 us
  matrix products: 245 us -> 0 us
  starting transfers between devices: 0.86 us -> 140 us
  local copies, waits for them, and re-layouts: 131 us -> 30.4 us
  blocking collectives: 92.7 us -> 0 us
  loops' own time: 86.7 us -> 0 us
  other arithmetic: 120 us -> 41.4 us
    reduce_scatter x8 -> x0, waiting for transfers between devices: 694 us -> none  [the longest x2 363 us: reduce_grads(): lax.psum_scatter(totals[1].astype(jnp.bfloat16), 'fsdp', scatter_dimensio...]
    pallas_call x0 -> x8, Pallas kernels: none -> 324 us  [the longest x2 104 us: attend_backward(): pl.pallas_call(functools.partial(attend_backward_kernel, n, seqs), out_sh...]
    ppermute x0 -> x112, waiting for transfers between devices: none -> 253 us  [swap(): return lax.ppermute(array, axis, [(i, i ^ mask) for i in range(count)])]
    dot_general x42 -> x0, matrix products: 245 us -> none  [the longest x2 36.4 us: layer_forward(): jnp.dot(mid_low, w_up, preferred_element_type=jnp.float32) + up_bias]
    all_gather x8 -> x0, waiting for transfers between devices: 146 us -> none  [the longest x2 82.4 us: on_device(): lax.all_gather(w_down[layer_idx], 'fsdp', axis=0, tiled=True)]
    ppermute x0 -> x112, starting transfers between devices: none -> 140 us  [swap(): return lax.ppermute(array, axis, [(i, i ^ mask) for i in range(count)])]
    unnamed x25 -> x0, waiting for transfers between devices: 123 us -> none
    psum x1 -> x0, waiting for transfers between devices: 122 us -> none  [reduce_grads(): lax.psum(slices[0].astype(jnp.bfloat16), 'rep').astype(jnp.float32)]
  transfers between devices with their start and end apart: 21 -> 112, of which waited for: 17 -> 45; matrix products, arithmetic and copies ran while one was open for 6% -> 7% of each run, Pallas kernels for 0% -> 12%
where the time goes in v1:
time: 797 us; the launch traced here: 792 us
  Pallas kernels  324 us (41%)
  waiting for transfers between devices  253 us (32%)
  starting transfers between devices  140 us (18%)
  other arithmetic  41.4 us (5%)
  local copies, waits for them, and re-layouts  30.4 us (4%)
    ppermute x112, waiting for transfers between devices, swap(): return lax.ppermute(array, axis, [(i, i ^ mask) for i in range(count)])  253 us
    ppermute x112, starting transfers between devices, swap(): return lax.ppermute(array, axis, [(i, i ^ mask) for i in range(count)])  140 us
    pallas_call x2, Pallas kernels, attend_backward(): pl.pallas_call(functools.partial(attend_backward_kernel, n, seqs), out_sh...  104 us
    pallas_call x2, Pallas kernels, ffn_backward(): pl.pallas_call(functools.partial(ffn_backward_kernel, n), out_shape=(jax....  90.2 us
    pallas_call x2, Pallas kernels, attend_forward(): pl.pallas_call(functools.partial(attend_forward_kernel, n, seqs), out_sha...  66.8 us
    pallas_call x2, Pallas kernels, ffn_forward(): pl.pallas_call(functools.partial(ffn_forward_kernel, n, last), out_shape=...  63.1 us
    convert_element_type x16, other arithmetic, scatter_pieces(): packed = jnp.stack([total(terms[place]).astype(bf16) for place in leaving])  17 us
  transfers between devices with their start and end apart: 112, of which 45 were waited for; matrix products, arithmetic and copies ran while one was open for 7% of the time, Pallas kernels for 12%

profile of v1, /device:TPU:0, one launch (start us, length us, event | category | flops | bytes accessed | tf_op | source)
XLA Modules:
  0.0 791.9 jit_solution(4616665369115087251)
XLA Ops:
  28.0 10.0 %collective-permute-done.43.refs_14_ = bf16[96,768]{1,0:T(8,128)(2,1)S(1)} collective-permute-done((bf16[96,768]{1,0:T(8,128)(2,1)S(1)}, bf16[96,768]{1,0:T(8,128)(2,1)S(1)}, u32[]{:S(2)}, u32[]{:S(2)}) %collective-permute-start.43) | collective-permute-done | bytes 147488 | tf_op jit(solution)/shard_map/ppermute | solution.py:745
  55.2 8.6 %collective-permute-done.18.refs_2_ = bf16[96,3072]{1,0:T(8,128)(2,1)S(1)} collective-permute-done((bf16[96,3072]{1,0:T(8,128)(2,1)S(1)}, bf16[96,3072]{1,0:T(8,128)(2,1)S(1)}, u32[]{:S(2)}, u32[]{:S(2)}) %collective-permute-start.18) | collective-permute-done | bytes 589856 | tf_op jit(solution)/shard_map/ppermute | solution.py:745
  119.1 16.6 %collective-permute-done.36.refs_6_ = bf16[96,2304]{1,0:T(8,128)(2,1)S(1)} collective-permute-done((bf16[96,2304]{1,0:T(8,128)(2,1)}, bf16[96,2304]{1,0:T(8,128)(2,1)S(1)}, u32[]{:S(2)}, u32[]{:S(2)}) %collective-permute-start.36) | collective-permute-done | bytes 442400 | tf_op jit(solution)/shard_map/ppermute | solution.py:745
  137.8 33.3 %attend_forward.2 = (bf16[1024,768]{1,0:T(8,128)(2,1)}, bf16[1024,768]{1,0:T(8,128)(2,1)}, bf16[1024,768]{1,0:T(8,128)(2,1)}, bf16[1024,768]{1,0:T(8,128)(2,1)},...) custom-call(s32[1]{0:T(128)} %bitcast.me_ref, ...), custom_call_target="tpu_custom_call" | custom-call | flops 11274289152 | bytes 15728640 | tf_op jit(solution)/shard_map/attend_forward/pallas_call | solution.py:167
  175.1 32.0 %ffn_forward.2 = (bf16[1024,3072]{1,0:T(8,128)(2,1)}, bf16[1024,3072]{1,0:T(8,128)(2,1)}, bf16[1024,768]{1,0:T(8,128)(2,1)}, f32[1024,1]{1,0:T(8,128)}, f32[1024,768]{1,0:T(8,128)}, /*index=5*/bf16[1024,768]{1,0:T(8,128)(2,1)}) custom-call(s32[1]{0:T(128)} %bitcast.me_ref, f32[1024,768]{1,0:T(8,128)} %get-tuple-element.66.mid_ref, ...), custom_call_target="tpu_custom_call" | custom-call | flops 19327352832 | bytes 25165824 | tf_op jit(solution)/shard_map/ffn_forward/pallas_call | solution.py:295
  208.8 33.5 %attend_forward.3 = (bf16[1024,768]{1,0:T(8,128)(2,1)}, bf16[1024,768]{1,0:T(8,128)(2,1)}, bf16[1024,768]{1,0:T(8,128)(2,1)}, bf16[1024,768]{1,0:T(8,128)(2,1)},...) custom-call(s32[1]{0:T(128)} %bitcast.me_ref, ...), custom_call_target="tpu_custom_call" | custom-call | flops 11274289152 | bytes 15728640 | tf_op jit(solution)/shard_map/attend_forward/pallas_call | solution.py:167
  243.7 31.1 %ffn_forward.3 = (bf16[1024,3072]{1,0:T(8,128)(2,1)}, bf16[1024,3072]{1,0:T(8,128)(2,1)}, bf16[1024,768]{1,0:T(8,128)(2,1)}, f32[1024,1]{1,0:T(8,128)}, bf16[1024,768]{1,0:T(8,128)(2,1)}) custom-call(s32[1]{0:T(128)} %bitcast.me_ref, f32[1024,768]{1,0:T(8,128)} %get-tuple-element.69.mid_ref, bf16[1024,768]{1,0:T(8,128)(2,1)} %get-tuple-element.70.low_ref, ...), custom_call_target="tpu_custom_call" | custom-call | flops 19327352832 | bytes 25165824 | tf_op jit(solution)/shard_map/ffn_forward/pallas_call | solution.py:295
  274.8 45.0 %ffn_backward.2 = (f32[1024,768]{1,0:T(8,128)}, bf16[1024,768]{1,0:T(8,128)(2,1)}, f32[8,768]{1,0:T(8,128)}, f32[1,3072]{1,0:T(1,128)}, bf16[4,384,768]{2,1,0:T(...) custom-call(s32[1]{0:T(128)} %bitcast.me_ref, ...), custom_call_target="tpu_custom_call" | custom-call | flops 24159191040 | bytes 25165824 | tf_op jit(solution)/shard_map/ffn_backward/pallas_call | solution.py:497
  319.9 52.3 %attend_backward.2 = (f32[1024,768]{1,0:T(8,128)}, f32[8,768]{1,0:T(8,128)}, bf16[4,3,96,768]{3,2,1,0:T(8,128)(2,1)}, bf16[4,3,96,768]{3,2,1,0:T(8,128)(2,1)}, b...) custom-call(s32[1]{0:T(128)} %bitcast.me_ref, bf16[1024,768]{1,0:T(8,128)(2,1)} %get-tuple-element.78.ga_ref, ...), custom_call_target="tpu_custom_call" | custom-call | flops 25769803776 | bytes 15728640 | tf_op jit(solution)/shard_map/attend_backward/pallas_call | solution.py:698
  373.0 45.2 %ffn_backward.3 = (f32[1024,768]{1,0:T(8,128)}, bf16[1024,768]{1,0:T(8,128)(2,1)}, f32[8,768]{1,0:T(8,128)}, f32[1,3072]{1,0:T(1,128)}, bf16[4,384,768]{2,1,0:T(...) custom-call(s32[1]{0:T(128)} %bitcast.me_ref, ...), custom_call_target="tpu_custom_call" | custom-call | flops 24159191040 | bytes 25165824 | tf_op jit(solution)/shard_map/ffn_backward/pallas_call | solution.py:497
  420.2 51.8 %attend_backward.3 = (bf16[1024,768]{1,0:T(8,128)(2,1)}, f32[8,768]{1,0:T(8,128)}, bf16[4,3,96,768]{3,2,1,0:T(8,128)(2,1)}, bf16[4,3,96,768]{3,2,1,0:T(8,128)(2,...) custom-call(s32[1]{0:T(128)} %bitcast.me_ref, bf16[1024,768]{1,0:T(8,128)(2,1)} %get-tuple-element.93.ga_ref, ...), custom_call_target="tpu_custom_call" | custom-call | flops 25769803776 | bytes 15728640 | tf_op jit(solution)/shard_map/attend_backward/pallas_call | solution.py:698
  528.5 9.1 %collective-permute-done.72 = bf16[2,3,96,768]{3,2,1,0:T(8,128)(2,1)S(1)} collective-permute-done((bf16[2,3,96,768]{3,2,1,0:T(8,128)(2,1)S(1)}, bf16[2,3,96,768]{3,2,1,0:T(8,128)(2,1)S(1)}, u32[]{:S(2)}, u32[]{:S(2)}) %collective-permute-start.72) | collective-permute-done | bytes 884768 | tf_op jit(solution)/shard_map/ppermute | solution.py:745
  539.4 16.7 %collective-permute-done.60 = bf16[2,3,96,768]{3,2,1,0:T(8,128)(2,1)S(1)} collective-permute-done((bf16[2,3,96,768]{3,2,1,0:T(8,128)(2,1)S(1)}, bf16[2,3,96,768]{3,2,1,0:T(8,128)(2,1)S(1)}, u32[]{:S(2)}, u32[]{:S(2)}) %collective-permute-start.60) | collective-permute-done | bytes 884768 | tf_op jit(solution)/shard_map/ppermute | solution.py:745
  558.2 9.9 %collective-permute-done.61 = bf16[1,3,96,768]{3,2,1,0:T(8,128)(2,1)S(1)} collective-permute-done((bf16[1,3,96,768]{3,2,1,0:T(8,128)(2,1)S(1)}, bf16[1,3,96,768]{3,2,1,0:T(8,128)(2,1)S(1)}, u32[]{:S(2)}, u32[]{:S(2)}) %collective-permute-start.61) | collective-permute-done | bytes 442400 | tf_op jit(solution)/shard_map/ppermute | solution.py:745
  577.0 9.2 %collective-permute-start.65 = (bf16[96,768]{1,0:T(8,128)(2,1)S(1)}, bf16[96,768]{1,0:T(8,128)(2,1)S(1)}, u32[]{:S(2)}, u32[]{:S(2)}) collective-permute-start(bf16[96,768]{1,0:T(8,128)(2,1)S(1)} %pad_maximum_fusion.22), channel_id=1, source_target_pairs={{0,8},{8,0},{16,24},{24,16},{1,9},{9,1},{17,25},{25,17},{2,10},{10... | collective-permute-start | bytes 442376 | tf_op jit(solution)/shard_map/ppermute | solution.py:745
  635.0 10.8 %collective-permute-done.96 = bf16[2,384,768]{2,1,0:T(8,128)(2,1)} collective-permute-done((bf16[2,384,768]{2,1,0:T(8,128)(2,1)}, bf16[2,384,768]{2,1,0:T(8,128)(2,1)}, u32[]{:S(2)}, u32[]{:S(2)}) %collective-permute-start.96) | collective-permute-done | bytes 1179680 | tf_op jit(solution)/shard_map/ppermute | solution.py:745
  652.3 18.3 %collective-permute-done.87 = bf16[2,4,96,768]{3,2,1,0:T(8,128)(2,1)} collective-permute-done((bf16[2,4,96,768]{3,2,1,0:T(8,128)(2,1)}, bf16[2,4,96,768]{3,2,1,0:T(8,128)(2,1)}, u32[]{:S(2)}, u32[]{:S(2)}) %collective-permute-start.87) | collective-permute-done | bytes 1179680 | tf_op jit(solution)/shard_map/ppermute | solution.py:745
  675.8 7.3 collective-permute-done.97
  703.6 12.5 %collective-permute-start.89 = (bf16[192,768]{1,0:T(8,128)(2,1)S(1)}, bf16[192,768]{1,0:T(8,128)(2,1)S(1)}, u32[]{:S(2)}, u32[]{:S(2)}) collective-permute-start(bf16[192,768]{1,0:T(8,128)(2,1)S(1)} %pad_maximum_fusion.16), channel_id=1, source_target_pairs={{0,8},{8,0},{16,24},{24,16},{1,9},{9,1},{17,25},{25,17},{2,10},{10... | collective-permute-start | bytes 884744 | tf_op jit(solution)/shard_map/ppermute | solution.py:745
  716.1 18.4 %collective-permute-done.102 = bf16[192,768]{1,0:T(8,128)(2,1)S(1)} collective-permute-done((bf16[192,768]{1,0:T(8,128)(2,1)S(1)}, bf16[192,768]{1,0:T(8,128)(2,1)S(1)}, u32[]{:S(2)}, u32[]{:S(2)}) %collective-permute-start.102) | collective-permute-done | bytes 294944 | tf_op jit(solution)/shard_map/ppermute | solution.py:745
  742.2 17.6 %collective-permute-done.90 = bf16[192,768]{1,0:T(8,128)(2,1)S(1)} collective-permute-done((bf16[192,768]{1,0:T(8,128)(2,1)S(1)}, bf16[192,768]{1,0:T(8,128)(2,1)S(1)}, u32[]{:S(2)}, u32[]{:S(2)}) %collective-permute-start.90) | collective-permute-done | bytes 294944 | tf_op jit(solution)/shard_map/ppermute | solution.py:745
  760.1 7.3 collective-permute-start.92
  767.4 11.4 %collective-permute-done.105 = bf16[192,768]{1,0:T(8,128)(2,1)S(1)} collective-permute-done((bf16[192,768]{1,0:T(8,128)(2,1)S(1)}, bf16[192,768]{1,0:T(8,128)(2,1)S(1)}, u32[]{:S(2)}, u32[]{:S(2)}) %collective-permute-start.105) | collective-permute-done | bytes 294944 | tf_op jit(solution)/shard_map/ppermute | solution.py:745
  780.0 7.4 collective-permute-done.93
  (521 shorter events, 273.5 us)
Async XLA Ops:
  135.6 35.5 %collective-permute-start.21 = (bf16[96,3072]{1,0:T(8,128)(2,1)}, bf16[96,3072]{1,0:T(8,128)(2,1)S(1)}, u32[]{:S(2)}, u32[]{:S(2)}) collective-permute-start(bf16[96,3072]{1,0:T(8,128)(2,1)} %copy-done.42), channel_id=1, source_target_pairs={{0,1},{1,0},{2,3},{3,2},{4,5},{5,4},{6,7},{7,6},{8,9},{9,8},{10,11... | collective-permute-start | bytes 1769480 | tf_op jit(solution)/shard_map/ppermute | solution.py:745
  136.4 35.3 %collective-permute-start.26 = (bf16[384,768]{1,0:T(8,128)(2,1)}, bf16[384,768]{1,0:T(8,128)(2,1)S(1)}, u32[]{:S(2)}, u32[]{:S(2)}) collective-permute-start(bf16[384,768]{1,0:T(8,128)(2,1)} %copy-done.44), channel_id=1, source_target_pairs={{0,1},{1,0},{2,3},{3,2},{4,5},{5,4},{6,7},{7,6},{8,9},{9,8},{10,11... | collective-permute-start | bytes 1769480 | tf_op jit(solution)/shard_map/ppermute | solution.py:745
  136.4 35.4 %collective-permute-start.28 = (bf16[384,768]{1,0:T(8,128)(2,1)}, bf16[384,768]{1,0:T(8,128)(2,1)S(1)}, u32[]{:S(2)}, u32[]{:S(2)}) collective-permute-start(bf16[384,768]{1,0:T(8,128)(2,1)} %copy-done.45), channel_id=1, source_target_pairs={{0,1},{1,0},{2,3},{3,2},{4,5},{5,4},{6,7},{7,6},{8,9},{9,8},{10,11... | collective-permute-start | bytes 1769480 | tf_op jit(solution)/shard_map/ppermute | solution.py:745
  136.9 36.4 %collective-permute-start.23 = (bf16[96,3072]{1,0:T(8,128)(2,1)}, bf16[96,3072]{1,0:T(8,128)(2,1)}, u32[]{:S(2)}, u32[]{:S(2)}) collective-permute-start(bf16[96,3072]{1,0:T(8,128)(2,1)} %collective-permute-done.22.refs_6_), channel_id=1, source_target_pairs={{0,1},{1,0},{2,3},{3,2},{4,5},{5,4},{6,7},{7,6},{8,9},{9,8},{10,11... | collective-permute-start | bytes 1769480 | tf_op jit(solution)/shard_map/ppermute | solution.py:745
  137.0 38.1 %collective-permute-start.30 = (bf16[384,768]{1,0:T(8,128)(2,1)}, bf16[384,768]{1,0:T(8,128)(2,1)}, u32[]{:S(2)}, u32[]{:S(2)}) collective-permute-start(bf16[384,768]{1,0:T(8,128)(2,1)} %collective-permute-done.29.refs_14_), channel_id=1, source_target_pairs={{0,1},{1,0},{2,3},{3,2},{4,5},{5,4},{6,7},{7,6},{8,9},{9,8},{10,11... | collective-permute-start | bytes 1769480 | tf_op jit(solution)/shard_map/ppermute | solution.py:745
  171.2 36.0 %collective-permute-start.35 = (bf16[96,2304]{1,0:T(8,128)(2,1)S(1)}, bf16[96,2304]{1,0:T(8,128)(2,1)}, u32[]{:S(2)}, u32[]{:S(2)}) collective-permute-start(bf16[96,2304]{1,0:T(8,128)(2,1)S(1)} %copy-done.64), channel_id=1, source_target_pairs={{0,1},{1,0},{2,3},{3,2},{4,5},{5,4},{6,7},{7,6},{8,9},{9,8},{10,11... | collective-permute-start | bytes 1327112 | tf_op jit(solution)/shard_map/ppermute | solution.py:745
  171.7 36.0 %collective-permute-start.47 = (bf16[96,3072]{1,0:T(8,128)(2,1)S(1)}, bf16[96,3072]{1,0:T(8,128)(2,1)S(1)}, u32[]{:S(2)}, u32[]{:S(2)}) collective-permute-start(bf16[96,3072]{1,0:T(8,128)(2,1)S(1)} %copy-done.47), channel_id=1, source_target_pairs={{0,1},{1,0},{2,3},{3,2},{4,5},{5,4},{6,7},{7,6},{8,9},{9,8},{10,11... | collective-permute-start | bytes 1769480 | tf_op jit(solution)/shard_map/ppermute | solution.py:745
  171.8 36.0 %collective-permute-start.50 = (bf16[96,3072]{1,0:T(8,128)(2,1)}, bf16[96,3072]{1,0:T(8,128)(2,1)S(1)}, u32[]{:S(2)}, u32[]{:S(2)}) collective-permute-start(bf16[96,3072]{1,0:T(8,128)(2,1)} %collective-permute-done.48.refs_4_), channel_id=1, source_target_pairs={{0,2},{1,3},{2,0},{3,1},{4,6},{5,7},{6,4},{7,5},{8,10},{9,11},{10,... | collective-permute-start | bytes 1769480 | tf_op jit(solution)/shard_map/ppermute | solution.py:745
  173.3 34.9 %collective-permute-start.57 = (bf16[384,768]{1,0:T(8,128)(2,1)}, bf16[384,768]{1,0:T(8,128)(2,1)}, u32[]{:S(2)}, u32[]{:S(2)}) collective-permute-start(bf16[384,768]{1,0:T(8,128)(2,1)} %collective-permute-done.53.refs_10_), channel_id=1, source_target_pairs={{0,4},{1,5},{2,6},{3,7},{4,0},{5,1},{6,2},{7,3},{8,12},{9,13},{10,... | collective-permute-start | bytes 1769480 | tf_op jit(solution)/shard_map/ppermute | solution.py:745
  207.2 35.1 %collective-permute-start.49 = (bf16[96,3072]{1,0:T(8,128)(2,1)}, bf16[96,3072]{1,0:T(8,128)(2,1)S(1)}, u32[]{:S(2)}, u32[]{:S(2)}) collective-permute-start(bf16[96,3072]{1,0:T(8,128)(2,1)} %collective-permute-done.48.refs_4_), channel_id=1, source_target_pairs={{0,1},{1,0},{2,3},{3,2},{4,5},{5,4},{6,7},{7,6},{8,9},{9,8},{10,11... | collective-permute-start | bytes 1769480 | tf_op jit(solution)/shard_map/ppermute | solution.py:745
  207.7 34.6 %collective-permute-start.54 = (bf16[384,768]{1,0:T(8,128)(2,1)}, bf16[384,768]{1,0:T(8,128)(2,1)S(1)}, u32[]{:S(2)}, u32[]{:S(2)}) collective-permute-start(bf16[384,768]{1,0:T(8,128)(2,1)} %collective-permute-done.53.refs_10_), channel_id=1, source_target_pairs={{0,1},{1,0},{2,3},{3,2},{4,5},{5,4},{6,7},{7,6},{8,9},{9,8},{10,11... | collective-permute-start | bytes 1769480 | tf_op jit(solution)/shard_map/ppermute | solution.py:745
  207.8 34.5 %collective-permute-start.56 = (bf16[384,768]{1,0:T(8,128)(2,1)}, bf16[384,768]{1,0:T(8,128)(2,1)S(1)}, u32[]{:S(2)}, u32[]{:S(2)}) collective-permute-start(bf16[384,768]{1,0:T(8,128)(2,1)} %collective-permute-done.55.refs_12_), channel_id=1, source_target_pairs={{0,1},{1,0},{2,3},{3,2},{4,5},{5,4},{6,7},{7,6},{8,9},{9,8},{10,11... | collective-permute-start | bytes 1769480 | tf_op jit(solution)/shard_map/ppermute | solution.py:745
  475.7 37.0 %collective-permute-start.71 = (bf16[4,3,96,768]{3,2,1,0:T(8,128)(2,1)}, bf16[4,3,96,768]{3,2,1,0:T(8,128)(2,1)S(1)}, u32[]{:S(2)}, u32[]{:S(2)}) collective-permute-start(bf16[4,3,96,768]{3,2,1,0:T(8,128)(2,1)} %get-tuple-element.106), channel_id=1, source_target_pairs={{0,1},{1,0},{2,3},{3,2},{4,5},{5,4},{6,7},{7,6},{8,9},{9,8},{10,11... | collective-permute-start | bytes 5308424 | tf_op jit(solution)/shard_map/ppermute | solution.py:745
  518.6 37.5 %collective-permute-start.60 = (bf16[2,3,96,768]{3,2,1,0:T(8,128)(2,1)S(1)}, bf16[2,3,96,768]{3,2,1,0:T(8,128)(2,1)S(1)}, u32[]{:S(2)}, u32[]{:S(2)}) collective-permute-start(bf16[2,3,96,768]{3,2,1,0:T(8,128)(2,1)S(1)} %pad_maximum_fusion.6), channel_id=1, source_target_pairs={{0,4},{1,5},{2,6},{3,7},{4,0},{5,1},{6,2},{7,3},{8,12},{9,13},{10,... | collective-permute-start | bytes 2654216 | tf_op jit(solution)/shard_map/ppermute | solution.py:745
  618.5 52.1 %collective-permute-start.87 = (bf16[2,4,96,768]{3,2,1,0:T(8,128)(2,1)}, bf16[2,4,96,768]{3,2,1,0:T(8,128)(2,1)}, u32[]{:S(2)}, u32[]{:S(2)}) collective-permute-start(bf16[2,4,96,768]{3,2,1,0:T(8,128)(2,1)} %pad_maximum_fusion.1), channel_id=1, source_target_pairs={{0,2},{1,3},{2,0},{3,1},{4,6},{5,7},{6,4},{7,5},{8,10},{9,11},{10,... | collective-permute-start | bytes 3538952 | tf_op jit(solution)/shard_map/ppermute | solution.py:745
  621.5 52.3 %collective-permute-start.84 = (bf16[2,384,768]{2,1,0:T(8,128)(2,1)}, bf16[2,384,768]{2,1,0:T(8,128)(2,1)}, u32[]{:S(2)}, u32[]{:S(2)}) collective-permute-start(bf16[2,384,768]{2,1,0:T(8,128)(2,1)} %pad_maximum_fusion), channel_id=1, source_target_pairs={{0,4},{1,5},{2,6},{3,7},{4,0},{5,1},{6,2},{7,3},{8,12},{9,13},{10,... | collective-permute-start | bytes 3538952 | tf_op jit(solution)/shard_map/ppermute | solution.py:745
  647.5 35.6 %collective-permute-start.97 = (bf16[1,384,768]{2,1,0:T(8,128)(2,1)S(1)}, bf16[1,384,768]{2,1,0:T(8,128)(2,1)S(1)}, u32[]{:S(2)}, u32[]{:S(2)}) collective-permute-start(bf16[1,384,768]{2,1,0:T(8,128)(2,1)S(1)} %add_convert_fusion.3), channel_id=1, source_target_pairs={{0,2},{1,3},{2,0},{3,1},{4,6},{5,7},{6,4},{7,5},{8,10},{9,11},{10,... | collective-permute-start | bytes 1769480 | tf_op jit(solution)/shard_map/ppermute | solution.py:745
  692.9 41.6 %collective-permute-start.102 = (bf16[192,768]{1,0:T(8,128)(2,1)S(1)}, bf16[192,768]{1,0:T(8,128)(2,1)S(1)}, u32[]{:S(2)}, u32[]{:S(2)}) collective-permute-start(bf16[192,768]{1,0:T(8,128)(2,1)S(1)} %pad_maximum_fusion.20), channel_id=1, source_target_pairs={{0,16},{8,24},{16,0},{24,8},{1,17},{9,25},{17,1},{25,9},{2,18},{10... | collective-permute-start | bytes 884744 | tf_op jit(solution)/shard_map/ppermute | solution.py:745
  693.0 41.5 %collective-permute-start.101 = (bf16[192,768]{1,0:T(8,128)(2,1)S(1)}, bf16[192,768]{1,0:T(8,128)(2,1)S(1)}, u32[]{:S(2)}, u32[]{:S(2)}) collective-permute-start(bf16[192,768]{1,0:T(8,128)(2,1)S(1)} %pad_maximum_fusion.19), channel_id=1, source_target_pairs={{0,8},{8,0},{16,24},{24,16},{1,9},{9,1},{17,25},{25,17},{2,10},{10... | collective-permute-start | bytes 884744 | tf_op jit(solution)/shard_map/ppermute | solution.py:745
  697.9 37.1 %collective-permute-start.91 = (bf16[192,768]{1,0:T(8,128)(2,1)S(1)}, bf16[192,768]{1,0:T(8,128)(2,1)S(1)}, u32[]{:S(2)}, u32[]{:S(2)}) collective-permute-start(bf16[192,768]{1,0:T(8,128)(2,1)S(1)} %pad_maximum_fusion.18), channel_id=1, source_target_pairs={{0,24},{8,16},{16,8},{24,0},{1,25},{9,17},{17,9},{25,1},{2,26},{10... | collective-permute-start | bytes 884744 | tf_op jit(solution)/shard_map/ppermute | solution.py:745
  699.1 60.8 %collective-permute-start.90 = (bf16[192,768]{1,0:T(8,128)(2,1)S(1)}, bf16[192,768]{1,0:T(8,128)(2,1)S(1)}, u32[]{:S(2)}, u32[]{:S(2)}) collective-permute-start(bf16[192,768]{1,0:T(8,128)(2,1)S(1)} %pad_maximum_fusion.17), channel_id=1, source_target_pairs={{0,16},{8,24},{16,0},{24,8},{1,17},{9,25},{17,1},{25,9},{2,18},{10... | collective-permute-start | bytes 884744 | tf_op jit(solution)/shard_map/ppermute | solution.py:745
  703.6 56.2 %collective-permute-start.89 = (bf16[192,768]{1,0:T(8,128)(2,1)S(1)}, bf16[192,768]{1,0:T(8,128)(2,1)S(1)}, u32[]{:S(2)}, u32[]{:S(2)}) collective-permute-start(bf16[192,768]{1,0:T(8,128)(2,1)S(1)} %pad_maximum_fusion.16), channel_id=1, source_target_pairs={{0,8},{8,0},{16,24},{24,16},{1,9},{9,1},{17,25},{25,17},{2,10},{10... | collective-permute-start | bytes 884744 | tf_op jit(solution)/shard_map/ppermute | solution.py:745
  735.0 43.7 %collective-permute-start.105 = (bf16[192,768]{1,0:T(8,128)(2,1)S(1)}, bf16[192,768]{1,0:T(8,128)(2,1)S(1)}, u32[]{:S(2)}, u32[]{:S(2)}) collective-permute-start(bf16[192,768]{1,0:T(8,128)(2,1)S(1)} %fusion.5), channel_id=1, source_target_pairs={{0,16},{8,24},{16,0},{24,8},{1,17},{9,25},{17,1},{25,9},{2,18},{10... | collective-permute-start | bytes 884744 | tf_op jit(solution)/shard_map/ppermute | solution.py:745
  735.0 43.7 %collective-permute-start.104 = (bf16[192,768]{1,0:T(8,128)(2,1)S(1)}, bf16[192,768]{1,0:T(8,128)(2,1)S(1)}, u32[]{:S(2)}, u32[]{:S(2)}) collective-permute-start(bf16[192,768]{1,0:T(8,128)(2,1)S(1)} %fusion.5), channel_id=1, source_target_pairs={{0,8},{8,0},{16,24},{24,16},{1,9},{9,1},{17,25},{25,17},{2,10},{10... | collective-permute-start | bytes 884744 | tf_op jit(solution)/shard_map/ppermute | solution.py:745
  (168 other events, 2759.4 us)

commit v2 on v1

--- a/solution.py
+++ b/solution.py
@@ -41,13 +41,129 @@
 ANY = pl.BlockSpec(memory_space=pl.ANY)
 
 
-def piece_copies(me, pieces, target, sems):
-    depth = pieces[0].shape[0]
-    copies = []
-    for mask, piece in enumerate(pieces):
-        start = pl.multiple_of((me ^ mask) * depth, 16)
-        copies.append(pltpu.make_async_copy(piece, target.at[pl.ds(start, depth), :], sems.at[mask]))
-    return copies
+def flip(index, mask):
+    bit = 1
+    while bit <= mask:
+        if mask & bit:
+            index = index + bit - 2 * bit * ((index // bit) % 2)
+        bit *= 2
+    return index
+
+
+def greet(n, bits):
+    me = lax.axis_index("fsdp")
+    barrier = pltpu.get_barrier_semaphore()
+    for bit in bits:
+        pl.semaphore_signal(barrier, inc=1, device_id={"fsdp": flip(me, bit)}, device_id_type=pl.DeviceIdType.MESH)
+    pl.semaphore_wait(barrier, len(bits))
+
+
+class Gather:
+    def __init__(self, own, full, order, send_sems, recv_sems, local_sem):
+        self.own, self.full, self.order = own, full, order
+        self.send_sems, self.recv_sems, self.local_sem = send_sems, recv_sems, local_sem
+        self.me = lax.axis_index("fsdp")
+        self.depth = own.shape[0]
+
+    def rows(self, mask):
+        return self.full.at[pl.ds(pl.multiple_of(flip(self.me, mask) * self.depth, 16), self.depth), :]
+
+    def round_masks(self, round_at):
+        earlier = self.order[:round_at]
+        masks = [0]
+        for bit in earlier:
+            masks += [mask | bit for mask in masks]
+        return [mask | self.order[round_at] for mask in masks]
+
+    def copy(self, mask):
+        bit = [bit for bit in self.order if bit & mask][-1]
+        held = mask ^ bit
+        return pltpu.make_async_remote_copy(
+            src_ref=self.own if held == 0 else self.rows(held),
+            dst_ref=self.rows(held),
+            send_sem=self.send_sems.at[mask],
+            recv_sem=self.recv_sems.at[mask],
+            device_id={"fsdp": flip(self.me, bit)},
+            device_id_type=pl.DeviceIdType.MESH,
+        )
+
+    def begin(self, round_at):
+        if round_at == 0:
+            pltpu.make_async_copy(self.own, self.rows(0), self.local_sem).start()
+        self.copy(self.order[round_at]).start()
+
+    def onward(self, round_at):
+        masks = self.round_masks(round_at)
+        for mask in masks:
+            self.copy(mask).wait_recv()
+        for bit in self.order[round_at + 1 :]:
+            for mask in masks:
+                self.copy(mask | bit).start()
+
+    def end(self):
+        pltpu.make_async_copy(self.own, self.rows(0), self.local_sem).wait()
+        for round_at in range(len(self.order)):
+            for mask in self.round_masks(round_at):
+                self.copy(mask).wait_send()
+
+
+def begin_all(n, gathers):
+    rounds = len(gathers[0].order)
+    greet(n, gathers[0].order)
+    for round_at in range(rounds):
+        for gather in gathers:
+            gather.begin(round_at)
+
+
+def onward_all(gathers, round_at):
+    for gather in gathers:
+        gather.onward(round_at)
+
+
+def end_all(gathers):
+    for gather in gathers:
+        gather.end()
+
+
+def make_gathers(n, layer, shards, wholes, orders, sems):
+    send_sems, recv_sems, local_sems = sems
+    return [
+        Gather(own.at[layer], full, order, send_sems.at[at], recv_sems.at[at], local_sems.at[at])
+        for at, (own, full, order) in enumerate(zip(shards, wholes, orders))
+    ]
+
+
+def gather_sems(n, count):
+    return [
+        pltpu.SemaphoreType.DMA((count, n)),
+        pltpu.SemaphoreType.DMA((count, n)),
+        pltpu.SemaphoreType.DMA((count,)),
+    ]
+
+
+def whole_of(n, shard):
+    return jax.ShapeDtypeStruct((shard.shape[1] * n, shard.shape[2]), shard.dtype)
+
+
+def gather_kernel(n, layer, orders, *refs):
+    count = len(orders)
+    gathers = make_gathers(n, layer, refs[:count], refs[count : 2 * count], orders, refs[2 * count :])
+    begin_all(n, gathers)
+    for round_at in range(len(orders[0])):
+        onward_all(gathers, round_at)
+    end_all(gathers)
+
+
+def gather_weights(n, layer, shards, orders, collective_id):
+    return pl.pallas_call(
+        functools.partial(gather_kernel, n, layer, orders),
+        out_shape=tuple(whole_of(n, shard) for shard in shards),
+        in_specs=[ANY] * len(shards),
+        out_specs=tuple([ANY] * len(shards)),
+        scratch_shapes=gather_sems(n, len(shards)),
+        compiler_params=pltpu.CompilerParams(collective_id=collective_id, has_side_effects=True),
+        name="gather_weights",
+    )(*shards)
 
 
 def norm_forward(total, gain, shift):
@@ -71,28 +187,28 @@
     return (lanes >= head * HEAD) & (lanes < (head + 1) * HEAD)
 
 
-def attend_forward_kernel(n, seqs, me_ref, x_ref, small_ref, mask_ref, *refs):
-    qkv_pieces, out_pieces = refs[:n], refs[n : 2 * n]
-    q_ref, k_ref, v_ref, ctx_ref, lse_ref, mid_ref, low_ref, n1_ref, r1_ref = refs[2 * n : 2 * n + 9]
-    base, w_qkv, w_out, acc, sems = refs[2 * n + 9 :]
+def attend_forward_kernel(n, seqs, layer, orders, x_ref, small_ref, mask_ref, qkv_ref, out_ref, *refs):
+    count = len(orders)
+    shards, refs = refs[:count], refs[count:]
+    q_ref, k_ref, v_ref, ctx_ref, lse_ref, mid_ref, low_ref, n1_ref, r1_ref = refs[:9]
+    wholes, refs = refs[9 : 9 + count], refs[9 + count :]
+    base, w_qkv, w_out, acc, sems = refs[:5]
+    gathers = make_gathers(n, layer, shards, wholes, orders, refs[5:])
     step, steps = pl.program_id(0), pl.num_programs(0)
     rows, width = x_ref.shape
     seq = rows // seqs
     heads = GROUP // HEAD
-    qkv_copies = piece_copies(me_ref[0], qkv_pieces, w_qkv, sems.at[0])
-    out_copies = piece_copies(me_ref[0], out_pieces, w_out, sems.at[1])
+    qkv_copy = pltpu.make_async_copy(qkv_ref, w_qkv, sems.at[0])
+    out_copy = pltpu.make_async_copy(out_ref, w_out, sems.at[1])
 
     @pl.when(step == 0)
     def _():
-        for copy in qkv_copies:
-            copy.start()
-        for copy in out_copies:
-            copy.start()
+        qkv_copy.start()
+        out_copy.start()
+        begin_all(n, gathers)
         base[...] = x_ref[...].astype(bf16)
-        for copy in qkv_copies:
-            copy.wait()
-        for copy in out_copies:
-            copy.wait()
+        qkv_copy.wait()
+        out_copy.wait()
 
     columns = pl.multiple_of(step * GROUP, GROUP)
     q_bias = small_ref[0:1, pl.ds(columns, GROUP)]
@@ -131,6 +247,10 @@
 
     lax.fori_loop(0, seqs, attend, 0)
 
+    @pl.when(step == 1)
+    def _():
+        onward_all(gathers, 0)
+
     def mix(block, carry):
         at = pl.ds(pl.multiple_of(block * ROWS, ROWS), ROWS)
         term = dot_nn(ctx_ref[at, :], w_out[pl.ds(columns, GROUP), :])
@@ -156,16 +276,21 @@
 
     lax.fori_loop(0, rows // ROWS, mix, 0)
 
-
-def attend_forward(me, x, small, key_mask, qkv_pieces, out_pieces, seqs):
-    n = len(qkv_pieces)
+    @pl.when(step == steps - 1)
+    def _():
+        for round_at in range(1, len(orders[0])):
+            onward_all(gathers, round_at)
+        end_all(gathers)
+
+
+def attend_forward(n, x, small, key_mask, w_qkv, w_out, seqs, layer, shards, orders, collective_id):
     rows, width = x.shape
     steps = width // GROUP
     seq = rows // seqs
     wide = jax.ShapeDtypeStruct((rows, width), bf16)
     heads = GROUP // HEAD
     return pl.pallas_call(
-        functools.partial(attend_forward_kernel, n, seqs),
+        functools.partial(attend_forward_kernel, n, seqs, layer, orders),
         out_shape=(
             wide,
             wide,
@@ -176,11 +301,12 @@
             wide,
             wide,
             jax.ShapeDtypeStruct((rows, 1), f32),
-        ),
+        )
+        + tuple(whole_of(n, shard) for shard in shards),
         grid_spec=pltpu.PrefetchScalarGridSpec(
-            num_scalar_prefetch=1,
+            num_scalar_prefetch=0,
             grid=(steps,),
-            in_specs=[whole((rows, width)), whole(small.shape), whole((rows, 1))] + [ANY] * (2 * n),
+            in_specs=[whole((rows, width)), whole(small.shape), whole((rows, 1))] + [ANY] * (2 + len(shards)),
             out_specs=[column_block(rows, GROUP)] * 4
             + [
                 pl.BlockSpec((1, seqs * heads, seq), lambda j, *_: (j, 0, 0)),
@@ -188,47 +314,62 @@
                 whole((rows, width)),
                 whole((rows, width)),
                 whole((rows, 1)),
-            ],
+            ]
+            + [ANY] * len(shards),
             scratch_shapes=[
                 pltpu.VMEM((rows, width), bf16),
                 pltpu.VMEM((width, 3 * width), bf16),
                 pltpu.VMEM((width, width), bf16),
                 pltpu.VMEM((rows, width), f32),
-                pltpu.SemaphoreType.DMA((2, n)),
-            ],
+                pltpu.SemaphoreType.DMA((2,)),
+            ]
+            + gather_sems(n, len(shards)),
         ),
         compiler_params=pltpu.CompilerParams(
-            dimension_semantics=("arbitrary",), vmem_limit_bytes=VMEM_BYTES
+            dimension_semantics=("arbitrary",),
+            vmem_limit_bytes=VMEM_BYTES,
+            collective_id=collective_id,
+            has_side_effects=True,
         ),
         cost_estimate=cost(8 * rows * width * width + 16 * rows * seq * width, 20 * rows * width),
         name="attend_forward",
-    )(me, x, small, key_mask, *qkv_pieces, *out_pieces)
-
-
-def ffn_forward_kernel(n, last, me_ref, mid_ref, low_ref, small_ref, up_bias_ref, valid_ref, *refs):
-    up_pieces, down_pieces = refs[:n], refs[n : 2 * n]
-    outs = refs[2 * n :]
-    act_ref, slope_ref, n2_ref, r2_ref, hid_ref = outs[:5]
-    if last:
-        w_up, w_down, acc, sems = outs[5:]
-    else:
-        hid_low_ref, w_up, w_down, acc, sems = outs[5:]
+    )(x, small, key_mask, w_qkv, w_out, *shards)
+
+
+def ffn_forward_kernel(n, last, layer, orders, mid_ref, low_ref, small_ref, up_bias_ref, valid_ref, up_ref, down_ref, *refs):
+    count = len(orders)
+    shards, refs = refs[:count], refs[count:]
+    act_ref, slope_ref, n2_ref, r2_ref, hid_ref = refs[:5]
+    refs = refs[5:]
+    if not last:
+        hid_low_ref, refs = refs[0], refs[1:]
+    wholes, refs = refs[:count], refs[count:]
+    w_up, w_down, acc, sems = refs[:4]
+    gathers = make_gathers(n, layer, shards, wholes, orders, refs[4:]) if count else []
     step, steps = pl.program_id(0), pl.num_programs(0)
     rows, width = mid_ref.shape
     chunk = act_ref.shape[1]
-    up_copies = piece_copies(me_ref[0], up_pieces, w_up, sems.at[0])
-    down_copies = piece_copies(me_ref[0], down_pieces, w_down, sems.at[1])
+    up_copy = pltpu.make_async_copy(up_ref, w_up, sems.at[0])
+    down_copy = pltpu.make_async_copy(down_ref, w_down, sems.at[1])
 
     @pl.when(step == 0)
     def _():
-        for copy in up_copies:
-            copy.start()
-        for copy in down_copies:
-            copy.start()
-        for copy in up_copies:
-            copy.wait()
-        for copy in down_copies:
-            copy.wait()
+        up_copy.start()
+        down_copy.start()
+        if gathers:
+            begin_all(n, gathers)
+        up_copy.wait()
+        down_copy.wait()
+
+    if gathers:
+
+        @pl.when(step == 1)
+        def _():
+            onward_all(gathers, 0)
+
+        @pl.when(step == 3)
+        def _():
+            onward_all(gathers, 1)
 
     columns = pl.multiple_of(step * chunk, chunk)
     tile = 256
@@ -270,9 +411,16 @@
 
     lax.fori_loop(0, rows // ROWS, block_step, 0)
 
-
-def ffn_forward(me, mid, low, small, up_bias, valid, up_pieces, down_pieces, last):
-    n = len(up_pieces)
+    if gathers:
+
+        @pl.when(step == steps - 1)
+        def _():
+            for round_at in range(2, len(orders[0])):
+                onward_all(gathers, round_at)
+            end_all(gathers)
+
+
+def ffn_forward(n, mid, low, small, up_bias, valid, w_up, w_down, last, layer, shards, orders, collective_id):
     rows, width = mid.shape
     units = up_bias.shape[1]
     chunk = width
@@ -292,11 +440,22 @@
     if not last:
         out_shape.append(jax.ShapeDtypeStruct((rows, width), bf16))
         out_specs.append(whole((rows, width)))
+    out_shape += [whole_of(n, shard) for shard in shards]
+    out_specs += [ANY] * len(shards)
+    if shards:
+        params = pltpu.CompilerParams(
+            dimension_semantics=("arbitrary",),
+            vmem_limit_bytes=VMEM_BYTES,
+            collective_id=collective_id,
+            has_side_effects=True,
+        )
+    else:
+        params = pltpu.CompilerParams(dimension_semantics=("arbitrary",), vmem_limit_bytes=VMEM_BYTES)
     return pl.pallas_call(
-        functools.partial(ffn_forward_kernel, n, last),
+        functools.partial(ffn_forward_kernel, n, last, layer, orders),
         out_shape=tuple(out_shape),
         grid_spec=pltpu.PrefetchScalarGridSpec(
-            num_scalar_prefetch=1,
+            num_scalar_prefetch=0,
             grid=(steps,),
             in_specs=[
                 whole((rows, width)),
@@ -305,21 +464,20 @@
                 column_block(1, chunk),
                 whole((rows, 1)),
             ]
-            + [ANY] * (2 * n),
+            + [ANY] * (2 + len(shards)),
             out_specs=out_specs,
             scratch_shapes=[
                 pltpu.VMEM((width, units), bf16),
                 pltpu.VMEM((units, width), bf16),
                 pltpu.VMEM((rows, width), f32),
-                pltpu.SemaphoreType.DMA((2, n)),
-            ],
+                pltpu.SemaphoreType.DMA((2,)),
+            ]
+            + (gather_sems(n, len(shards)) if shards else []),
         ),
-        compiler_params=pltpu.CompilerParams(
-            dimension_semantics=("arbitrary",), vmem_limit_bytes=VMEM_BYTES
-        ),
+        compiler_params=params,
         cost_estimate=cost(8 * rows * width * units, 8 * rows * units),
         name="ffn_forward",
-    )(me, mid, low, small, up_bias, valid, *up_pieces, *down_pieces)
+    )(mid, low, small, up_bias, valid, w_up, w_down, *shards)
 
 
 def shard_copies(n, me, source_of, keep_of, send_of, sems):
@@ -342,9 +500,9 @@
 
 
 def ffn_backward_kernel(n, me_ref, g_ref, valid_ref, n2_ref, r2_ref, low_ref, n1_ref, r1_ref, small_ref, act_ref, slope_ref, *refs):
-    up_pieces, down_pieces = refs[:n], refs[n : 2 * n]
-    gs1_ref, ga1_ref, sums_ref, up_sum_ref, down_keep, down_send, up_keep, up_send = refs[2 * n : 2 * n + 8]
-    w_up, w_down, gs2, gffn, gpre, acc, low_turned, d_down, d_up, sems, out_sems = refs[2 * n + 8 :]
+    up_ref, down_ref = refs[:2]
+    gs1_ref, ga1_ref, sums_ref, up_sum_ref, down_keep, down_send, up_keep, up_send = refs[2:10]
+    w_up, w_down, gs2, gffn, gpre, acc, low_turned, d_down, d_up, sems, out_sems = refs[10:]
     step, steps = pl.program_id(0), pl.num_programs(0)
     me = me_ref[0]
     rows, width = gs2.shape
@@ -352,8 +510,8 @@
     per_down = down_keep.shape[1]
     per_up = up_keep.shape[2]
     tile = 256
-    up_copies = piece_copies(me, up_pieces, w_up, sems.at[0])
-    down_copies = piece_copies(me, down_pieces, w_down, sems.at[1])
+    up_copies = [pltpu.make_async_copy(up_ref, w_up, sems.at[0])]
+    down_copies = [pltpu.make_async_copy(down_ref, w_down, sems.at[1])]
 
     @pl.when(step == 0)
     def _():
@@ -485,8 +643,7 @@
         up_out(step)(False)
 
 
-def ffn_backward(me, grad, valid, n2, r2, low, n1, r1, small, act, slope, up_pieces, down_pieces):
-    n = len(up_pieces)
+def ffn_backward(me, grad, valid, n2, r2, low, n1, r1, small, act, slope, w_up, w_down, n):
     rows, width = grad.shape
     units = act.shape[1]
     chunk = width
@@ -521,7 +678,7 @@
                 column_block(rows, chunk),
                 column_block(rows, chunk),
             ]
-            + [ANY] * (2 * n),
+            + [ANY] * 2,
             out_specs=[
                 whole((rows, width)),
                 whole((rows, width)),
@@ -539,7 +696,7 @@
                 pltpu.VMEM((width, rows), bf16),
                 pltpu.VMEM((chunk, width), bf16),
                 pltpu.VMEM((width, chunk), bf16),
-                pltpu.SemaphoreType.DMA((2, n)),
+                pltpu.SemaphoreType.DMA((2,)),
                 pltpu.SemaphoreType.DMA((2, n)),
             ],
         ),
@@ -548,13 +705,13 @@
         ),
         cost_estimate=cost(10 * rows * width * units, 8 * rows * units),
         name="ffn_backward",
-    )(me, grad, valid, n2, r2, low, n1, r1, small, act, slope, *up_pieces, *down_pieces)
+    )(me, grad, valid, n2, r2, low, n1, r1, small, act, slope, w_up, w_down)
 
 
 def attend_backward_kernel(n, seqs, me_ref, ga_ref, gs_ref, base_ref, mask_ref, q_ref, k_ref, v_ref, ctx_ref, lse_ref, *refs):
-    qkv_pieces, out_pieces = refs[:n], refs[n : 2 * n]
-    gh_ref, sums_ref, qkv_keep, qkv_send, out_keep, out_send = refs[2 * n : 2 * n + 6]
-    w_qkv, w_out, acc, base_turned, gctx, gproj, d_qkv, d_out, p_all, ds_all, sems, out_sems = refs[2 * n + 6 :]
+    qkv_ref, out_ref = refs[:2]
+    gh_ref, sums_ref, qkv_keep, qkv_send, out_keep, out_send = refs[2:8]
+    w_qkv, w_out, acc, base_turned, gctx, gproj, d_qkv, d_out, p_all, ds_all, sems, out_sems = refs[8:]
     step, steps = pl.program_id(0), pl.num_programs(0)
     me = me_ref[0]
     rows, width = ga_ref.shape
@@ -562,8 +719,8 @@
     heads = GROUP // HEAD
     per = width // n
     tile = 256
-    qkv_copies = piece_copies(me, qkv_pieces, w_qkv, sems.at[0])
-    out_copies = piece_copies(me, out_pieces, w_out, sems.at[1])
+    qkv_copies = [pltpu.make_async_copy(qkv_ref, w_qkv, sems.at[0])]
+    out_copies = [pltpu.make_async_copy(out_ref, w_out, sems.at[1])]
 
     @pl.when(step == 0)
     def _():
@@ -686,8 +843,7 @@
         out_copy(False)
 
 
-def attend_backward(me, ga, gs, base, key_mask, q, k, v, ctx, lse, qkv_pieces, out_pieces, seqs, out_type):
-    n = len(qkv_pieces)
+def attend_backward(me, ga, gs, base, key_mask, q, k, v, ctx, lse, w_qkv, w_out, seqs, out_type, n):
     rows, width = ga.shape
     steps = width // GROUP
     seq = rows // seqs
@@ -712,7 +868,7 @@
             + [whole((rows, 1))]
             + [column_block(rows, GROUP)] * 4
             + [pl.BlockSpec((1, seqs * heads, seq), lambda j, *_: (j, 0, 0))]
-            + [ANY] * (2 * n),
+            + [ANY] * 2,
             out_specs=[whole((rows, width)), column_block(8, GROUP)] + [ANY] * 4,
             scratch_shapes=[
                 pltpu.VMEM((width, 3 * width), bf16),
@@ -725,7 +881,7 @@
                 pltpu.VMEM((width, width), bf16),
                 pltpu.VMEM((seq, heads * seq), bf16),
                 pltpu.VMEM((seq, heads * seq), bf16),
-                pltpu.SemaphoreType.DMA((2, n)),
+                pltpu.SemaphoreType.DMA((2,)),
                 pltpu.SemaphoreType.DMA((4, n)),
             ],
         ),
@@ -734,7 +890,7 @@
         ),
         cost_estimate=cost(16 * rows * width * width + 40 * rows * seq * width, 20 * rows * width),
         name="attend_backward",
-    )(me, ga, gs, base, key_mask, q, k, v, ctx, lse, *qkv_pieces, *out_pieces)
+    )(me, ga, gs, base, key_mask, q, k, v, ctx, lse, w_qkv, w_out)
 
 
 def cost(flops, moved):
@@ -743,14 +899,6 @@
 
 def swap(array, axis, count, mask):
     return lax.ppermute(array, axis, [(i, i ^ mask) for i in range(count)])
-
-
-def gather_pieces(own, n, bits):
-    pieces = {0: own}
-    for bit in bits:
-        for mask, piece in list(pieces.items()):
-            pieces[mask | bit] = swap(piece, "fsdp", n, bit)
-    return [pieces[mask] for mask in range(n)]
 
 
 def scatter_pieces(keep, send, n, bits):
@@ -836,31 +984,30 @@
     while bit < n:
         chip_bits.append(bit)
         bit *= 2
-    upward = chip_bits + [1]
-    downward = chip_bits[::-1] + [1]
-
-    qkv, out, up, down = [], [], [], []
-    for layer in range(LAYERS):
-        qkv.append(gather_pieces(w_qkv[layer], n, upward))
-        out.append(gather_pieces(w_out[layer], n, downward))
-        up.append(gather_pieces(w_up[layer], n, downward))
-        down.append(gather_pieces(w_down[layer], n, upward))
+    upward = tuple(chip_bits + [1])
+    downward = tuple(chip_bits[::-1] + [1])
+
+    attend_orders, ffn_orders = (upward, downward), (downward, upward)
+    qkv, out, up, down = [None] * LAYERS, [None] * LAYERS, [None] * LAYERS, [None] * LAYERS
+    qkv[0], out[0] = gather_weights(n, 0, (w_qkv, w_out), attend_orders, 0)
 
     current = tokens.reshape(rows, width)
     base = current
     saved = []
     for layer in range(LAYERS):
         last = layer == LAYERS - 1
-        q, k, v, ctx, lse, mid, low, n1, r1 = attend_forward(
-            me_row, current, smalls[layer], key_mask, qkv[layer], out[layer], seqs
+        q, k, v, ctx, lse, mid, low, n1, r1, up[layer], down[layer] = attend_forward(
+            n, current, smalls[layer], key_mask, qkv[layer], out[layer], seqs,
+            layer, (w_up, w_down), ffn_orders, 1 + 2 * layer,
         )
         results = ffn_forward(
-            me_row, mid, low, smalls[layer], up_bias_all[layer], valid, up[layer], down[layer], last
+            n, mid, low, smalls[layer], up_bias_all[layer], valid, up[layer], down[layer], last,
+            layer + 1, () if last else (w_qkv, w_out), () if last else attend_orders, 2 + 2 * layer,
         )
         act, slope, n2, r2, current = results[:5]
         saved.append((base, q, k, v, ctx, lse, low, n1, r1, act, slope, n2, r2))
         if not last:
-            base = results[5]
+            base, qkv[layer + 1], out[layer + 1] = results[5:]
     outputs = current.reshape(seqs, seq, width)
 
     grad = cotangent.reshape(rows, width)
@@ -870,11 +1017,11 @@
     for layer in range(LAYERS - 1, -1, -1):
         base, q, k, v, ctx, lse, low, n1, r1, act, slope, n2, r2 = saved[layer]
         gs1, ga1, sums, up_sum, down_keep, down_send, up_keep, up_send = ffn_backward(
-            me_row, grad, grad_valid, n2, r2, low, n1, r1, smalls[layer], act, slope, up[layer], down[layer]
+            me_row, grad, grad_valid, n2, r2, low, n1, r1, smalls[layer], act, slope, up[layer], down[layer], n
         )
         grad, proj_sums, qkv_keep, qkv_send, out_keep, out_send = attend_backward(
             me_row, ga1, gs1, base, key_mask, q, k, v, ctx, lse, qkv[layer], out[layer], seqs,
-            f32 if layer else bf16,
+            f32 if layer else bf16, n,
         )
         grad_valid = ones
         d_down = scatter_pieces(down_keep, down_send, n, chip_bits[::-1])

time: 797 us -> 747 us (0.937)
  Pallas kernels: 324 us -> 404 us
  waiting for transfers between devices: 253 us -> 175 us
  starting transfers between devices: 140 us -> 92.5 us
    ppermute x112 -> x56, waiting for transfers between devices: 253 us -> 175 us  [swap(): return lax.ppermute(array, axis, [(i, i ^ mask) for i in range(count)])]
    pallas_call x4 -> x5, Pallas kernels: 130 us -> 200 us  [the longest x2 103 us: attend_forward(): pl.pallas_call(functools.partial(attend_forward_kernel, n, seqs, layer, o...]
    ppermute x112 -> x56, starting transfers between devices: 140 us -> 92.5 us  [swap(): return lax.ppermute(array, axis, [(i, i ^ mask) for i in range(count)])]
    pallas_call x2, Pallas kernels: 90.2 us -> 100 us  [ffn_backward(): pl.pallas_call(functools.partial(ffn_backward_kernel, n), out_shape=(jax....]
  transfers between devices with their start and end apart: 112 -> 56, of which waited for: 45 -> 27; matrix products, arithmetic and copies ran while one was open for 7% -> 7% of each run, Pallas kernels for 12% -> 4%
where the time goes in v2:
time: 747 us; the launch traced here: 743 us
  Pallas kernels  404 us (54%)
  waiting for transfers between devices  175 us (23%)
  starting transfers between devices  92.5 us (12%)
  other arithmetic  43.1 us (6%)
  local copies, waits for them, and re-layouts  26.6 us (4%)
    ppermute x56, waiting for transfers between devices, swap(): return lax.ppermute(array, axis, [(i, i ^ mask) for i in range(count)])  175 us
    pallas_call x2, Pallas kernels, attend_backward(): pl.pallas_call(functools.partial(attend_backward_kernel, n, seqs), out_sh...  104 us
    pallas_call x2, Pallas kernels, attend_forward(): pl.pallas_call(functools.partial(attend_forward_kernel, n, seqs, layer, o...  103 us
    pallas_call x2, Pallas kernels, ffn_backward(): pl.pallas_call(functools.partial(ffn_backward_kernel, n), out_shape=(jax....  100 us
    ppermute x56, starting transfers between devices, swap(): return lax.ppermute(array, axis, [(i, i ^ mask) for i in range(count)])  92.5 us
    pallas_call x2, Pallas kernels, ffn_forward(): pl.pallas_call(functools.partial(ffn_forward_kernel, n, last, layer, orde...  69.4 us
    pallas_call x1, Pallas kernels, gather_weights(): pl.pallas_call(functools.partial(gather_kernel, n, layer, orders), out_sh...  26.9 us
    convert_element_type x16, other arithmetic, scatter_pieces(): packed = jnp.stack([total(terms[place]).astype(bf16) for place in leaving])  17.6 us
  transfers between devices with their start and end apart: 56, of which 27 were waited for; matrix products, arithmetic and copies ran while one was open for 7% of the time, Pallas kernels for 4%

profile of v2, /device:TPU:0, one launch (start us, length us, event | category | flops | bytes accessed | tf_op | source)
XLA Modules:
  0.0 742.9 jit_solution(12996438785020540077)
XLA Ops:
  13.9 26.9 %gather_weights.1 = (bf16[768,2304]{1,0:T(8,128)(2,1)}, bf16[768,768]{1,0:T(8,128)(2,1)}) custom-call(bf16[2,96,2304]{2,1,0:T(8,128)(2,1)} %refs_0_.6, bf16[2,96,768]{2,1,0:T(8,128)(2,1)} %refs_1_.6), custom_call_target="tpu_custom_call" | custom-call | tf_op jit(solution)/shard_map/gather_weights/pallas_call | solution.py:158
  43.2 52.5 %attend_forward.2 = (bf16[1024,768]{1,0:T(8,128)(2,1)}, bf16[1024,768]{1,0:T(8,128)(2,1)}, bf16[1024,768]{1,0:T(8,128)(2,1)}, bf16[1024,768]{1,0:T(8,128)(2,1)},...) custom-call(bf16[1024,768]{1,0:T(8,128)(2,1)} %bitcast.248, ...), custom_call_target="tpu_custom_call" | custom-call | flops 11274289152 | bytes 15728640 | tf_op jit(solution)/shard_map/attend_forward/pallas_call | solution.py:292
  95.7 38.4 %ffn_forward.2 = (bf16[1024,3072]{1,0:T(8,128)(2,1)}, bf16[1024,3072]{1,0:T(8,128)(2,1)}, bf16[1024,768]{1,0:T(8,128)(2,1)}, f32[1024,1]{1,0:T(8,128)}, f32[1024...) custom-call(f32[1024,768]{1,0:T(8,128)} %get-tuple-element.76.mid_ref, ...), custom_call_target="tpu_custom_call" | custom-call | flops 19327352832 | bytes 25165824 | tf_op jit(solution)/shard_map/ffn_forward/pallas_call | solution.py:454
  134.1 50.8 %attend_forward.3 = (bf16[1024,768]{1,0:T(8,128)(2,1)}, bf16[1024,768]{1,0:T(8,128)(2,1)}, bf16[1024,768]{1,0:T(8,128)(2,1)}, bf16[1024,768]{1,0:T(8,128)(2,1)},...) custom-call(f32[1024,768]{1,0:T(8,128)} %get-tuple-element.80.x_ref,, ...), custom_call_target="tpu_custom_call" | custom-call | flops 11274289152 | bytes 15728640 | tf_op jit(solution)/shard_map/attend_forward/pallas_call | solution.py:292
  184.9 30.9 %ffn_forward.3 = (bf16[1024,3072]{1,0:T(8,128)(2,1)}, bf16[1024,3072]{1,0:T(8,128)(2,1)}, bf16[1024,768]{1,0:T(8,128)(2,1)}, f32[1024,1]{1,0:T(8,128)}, bf16[1024,768]{1,0:T(8,128)(2,1)}) custom-call(f32[1024,768]{1,0:T(8,128)} %get-tuple-element.83.mid_ref, bf16[1024,768]{1,0:T(8,128)(2,1)} %get-tuple-element.84.low_ref, ...), custom_call_target="tpu_custom_call" | custom-call | flops 19327352832 | bytes 25165824 | tf_op jit(solution)/shard_map/ffn_forward/pallas_call | solution.py:454
  215.8 44.6 %ffn_backward.2 = (f32[1024,768]{1,0:T(8,128)}, bf16[1024,768]{1,0:T(8,128)(2,1)}, f32[8,768]{1,0:T(8,128)}, f32[1,3072]{1,0:T(1,128)}, bf16[4,384,768]{2,1,0:T(...) custom-call(s32[1]{0:T(128)} %bitcast.10.me_ref, ...), custom_call_target="tpu_custom_call" | custom-call | flops 24159191040 | bytes 25165824 | tf_op jit(solution)/shard_map/ffn_backward/pallas_call | solution.py:654
  260.5 52.2 %attend_backward.2 = (f32[1024,768]{1,0:T(8,128)}, f32[8,768]{1,0:T(8,128)}, bf16[4,3,96,768]{3,2,1,0:T(8,128)(2,1)}, bf16[4,3,96,768]{3,2,1,0:T(8,128)(2,1)}, b...) custom-call(s32[1]{0:T(128)} %bitcast.10.me_ref, bf16[1024,768]{1,0:T(8,128)(2,1)} %get-tuple-element.94.ga_ref, ...), custom_call_target="tpu_custom_call" | custom-call | flops 25769803776 | bytes 15728640 | tf_op jit(solution)/shard_map/attend_backward/pallas_call | solution.py:854
  313.5 55.6 %ffn_backward.3 = (f32[1024,768]{1,0:T(8,128)}, bf16[1024,768]{1,0:T(8,128)(2,1)}, f32[8,768]{1,0:T(8,128)}, f32[1,3072]{1,0:T(1,128)}, bf16[4,384,768]{2,1,0:T(...) custom-call(s32[1]{0:T(128)} %bitcast.10.me_ref, ...), custom_call_target="tpu_custom_call" | custom-call | flops 24159191040 | bytes 25165824 | tf_op jit(solution)/shard_map/ffn_backward/pallas_call | solution.py:654
  371.1 51.7 %attend_backward.3 = (bf16[1024,768]{1,0:T(8,128)(2,1)}, f32[8,768]{1,0:T(8,128)}, bf16[4,3,96,768]{3,2,1,0:T(8,128)(2,1)}, bf16[4,3,96,768]{3,2,1,0:T(8,128)(2,...) custom-call(s32[1]{0:T(128)} %bitcast.10.me_ref, bf16[1024,768]{1,0:T(8,128)(2,1)} %get-tuple-element.109.ga_ref, ...), custom_call_target="tpu_custom_call" | custom-call | flops 25769803776 | bytes 15728640 | tf_op jit(solution)/shard_map/attend_backward/pallas_call | solution.py:854
  476.8 11.0 %collective-permute-done.16 = bf16[2,3,96,768]{3,2,1,0:T(8,128)(2,1)S(1)} collective-permute-done((bf16[2,3,96,768]{3,2,1,0:T(8,128)(2,1)S(1)}, bf16[2,3,96,768]{3,2,1,0:T(8,128)(2,1)S(1)}, u32[]{:S(2)}, u32[]{:S(2)}) %collective-permute-start.16) | collective-permute-done | bytes 884768 | tf_op jit(solution)/shard_map/ppermute | solution.py:901
  491.0 14.8 %collective-permute-done.4 = bf16[2,3,96,768]{3,2,1,0:T(8,128)(2,1)S(1)} collective-permute-done((bf16[2,3,96,768]{3,2,1,0:T(8,128)(2,1)S(1)}, bf16[2,3,96,768]{3,2,1,0:T(8,128)(2,1)S(1)}, u32[]{:S(2)}, u32[]{:S(2)}) %collective-permute-start.4) | collective-permute-done | bytes 884768 | tf_op jit(solution)/shard_map/ppermute | solution.py:901
  510.1 8.1 %collective-permute-done.5 = bf16[1,3,96,768]{3,2,1,0:T(8,128)(2,1)S(1)} collective-permute-done((bf16[1,3,96,768]{3,2,1,0:T(8,128)(2,1)S(1)}, bf16[1,3,96,768]{3,2,1,0:T(8,128)(2,1)S(1)}, u32[]{:S(2)}, u32[]{:S(2)}) %collective-permute-start.5) | collective-permute-done | bytes 442400 | tf_op jit(solution)/shard_map/ppermute | solution.py:901
  528.2 8.2 %collective-permute-start.9 = (bf16[96,768]{1,0:T(8,128)(2,1)S(1)}, bf16[96,768]{1,0:T(8,128)(2,1)S(1)}, u32[]{:S(2)}, u32[]{:S(2)}) collective-permute-start(bf16[96,768]{1,0:T(8,128)(2,1)S(1)} %pad_maximum_fusion.22), channel_id=1, source_target_pairs={{0,8},{8,0},{16,24},{24,16},{1,9},{9,1},{17,25},{25,17},{2,10},{10... | collective-permute-start | bytes 442376 | tf_op jit(solution)/shard_map/ppermute | solution.py:901
  541.6 6.8 collective-permute-start.26
  584.8 12.0 %collective-permute-done.40 = bf16[2,384,768]{2,1,0:T(8,128)(2,1)} collective-permute-done((bf16[2,384,768]{2,1,0:T(8,128)(2,1)}, bf16[2,384,768]{2,1,0:T(8,128)(2,1)}, u32[]{:S(2)}, u32[]{:S(2)}) %collective-permute-start.40) | collective-permute-done | bytes 1179680 | tf_op jit(solution)/shard_map/ppermute | solution.py:901
  601.9 19.4 %collective-permute-done.31 = bf16[2,4,96,768]{3,2,1,0:T(8,128)(2,1)} collective-permute-done((bf16[2,4,96,768]{3,2,1,0:T(8,128)(2,1)}, bf16[2,4,96,768]{3,2,1,0:T(8,128)(2,1)}, u32[]{:S(2)}, u32[]{:S(2)}) %collective-permute-start.31) | collective-permute-done | bytes 1179680 | tf_op jit(solution)/shard_map/ppermute | solution.py:901
  626.2 7.6 %collective-permute-done.41 = bf16[1,384,768]{2,1,0:T(8,128)(2,1)S(1)} collective-permute-done((bf16[1,384,768]{2,1,0:T(8,128)(2,1)S(1)}, bf16[1,384,768]{2,1,0:T(8,128)(2,1)S(1)}, u32[]{:S(2)}, u32[]{:S(2)}) %collective-permute-start.41) | collective-permute-done | bytes 589856 | tf_op jit(solution)/shard_map/ppermute | solution.py:901
  654.5 12.5 %collective-permute-start.33 = (bf16[192,768]{1,0:T(8,128)(2,1)S(1)}, bf16[192,768]{1,0:T(8,128)(2,1)S(1)}, u32[]{:S(2)}, u32[]{:S(2)}) collective-permute-start(bf16[192,768]{1,0:T(8,128)(2,1)S(1)} %pad_maximum_fusion.16), channel_id=1, source_target_pairs={{0,8},{8,0},{16,24},{24,16},{1,9},{9,1},{17,25},{25,17},{2,10},{10... | collective-permute-start | bytes 884744 | tf_op jit(solution)/shard_map/ppermute | solution.py:901
  667.0 18.4 %collective-permute-done.46 = bf16[192,768]{1,0:T(8,128)(2,1)S(1)} collective-permute-done((bf16[192,768]{1,0:T(8,128)(2,1)S(1)}, bf16[192,768]{1,0:T(8,128)(2,1)S(1)}, u32[]{:S(2)}, u32[]{:S(2)}) %collective-permute-start.46) | collective-permute-done | bytes 294944 | tf_op jit(solution)/shard_map/ppermute | solution.py:901
  685.9 7.1 collective-permute-start.48
  693.1 17.6 %collective-permute-done.34 = bf16[192,768]{1,0:T(8,128)(2,1)S(1)} collective-permute-done((bf16[192,768]{1,0:T(8,128)(2,1)S(1)}, bf16[192,768]{1,0:T(8,128)(2,1)S(1)}, u32[]{:S(2)}, u32[]{:S(2)}) %collective-permute-start.34) | collective-permute-done | bytes 294944 | tf_op jit(solution)/shard_map/ppermute | solution.py:901
  711.0 7.3 collective-permute-start.36
  718.4 11.3 %collective-permute-done.49 = bf16[192,768]{1,0:T(8,128)(2,1)S(1)} collective-permute-done((bf16[192,768]{1,0:T(8,128)(2,1)S(1)}, bf16[192,768]{1,0:T(8,128)(2,1)S(1)}, u32[]{:S(2)}, u32[]{:S(2)}) %collective-permute-start.49) | collective-permute-done | bytes 294944 | tf_op jit(solution)/shard_map/ppermute | solution.py:901
  730.9 7.4 collective-permute-done.37
  (298 shorter events, 167.1 us)
Async XLA Ops:
  9.0 31.9 %collective-permute-start.2 = (f32[4,2304]{1,0:T(4,128)S(1)}, f32[4,2304]{1,0:T(4,128)S(1)}, u32[]{:S(2)}, u32[]{:S(2)}) collective-permute-start(f32[4,2304]{1,0:T(4,128)S(1)} %pad_maximum_fusion.30), channel_id=1, source_target_pairs={{0,4},{1,5},{2,6},{3,7},{4,0},{5,1},{6,2},{7,3},{8,12},{9,13},{10,... | collective-permute-start | bytes 110600 | tf_op jit(solution)/shard_map/ppermute | solution.py:901
  426.7 35.2 %collective-permute-start.15 = (bf16[4,3,96,768]{3,2,1,0:T(8,128)(2,1)}, bf16[4,3,96,768]{3,2,1,0:T(8,128)(2,1)}, u32[]{:S(2)}, u32[]{:S(2)}) collective-permute-start(bf16[4,3,96,768]{3,2,1,0:T(8,128)(2,1)} %get-tuple-element.122), channel_id=1, source_target_pairs={{0,1},{1,0},{2,3},{3,2},{4,5},{5,4},{6,7},{7,6},{8,9},{9,8},{10,11... | collective-permute-start | bytes 5308424 | tf_op jit(solution)/shard_map/ppermute | solution.py:901
  436.0 29.1 %collective-permute-start.3 = (bf16[4,3,96,768]{3,2,1,0:T(8,128)(2,1)}, bf16[4,3,96,768]{3,2,1,0:T(8,128)(2,1)}, u32[]{:S(2)}, u32[]{:S(2)}) collective-permute-start(bf16[4,3,96,768]{3,2,1,0:T(8,128)(2,1)} %get-tuple-element.118), channel_id=1, source_target_pairs={{0,1},{1,0},{2,3},{3,2},{4,5},{5,4},{6,7},{7,6},{8,9},{9,8},{10,11... | collective-permute-start | bytes 5308424 | tf_op jit(solution)/shard_map/ppermute | solution.py:901
  438.1 30.0 %collective-permute-start.42 = (bf16[4,4,96,768]{3,2,1,0:T(8,128)(2,1)}, bf16[4,4,96,768]{3,2,1,0:T(8,128)(2,1)S(1)}, u32[]{:S(2)}, u32[]{:S(2)}) collective-permute-start(bf16[4,4,96,768]{3,2,1,0:T(8,128)(2,1)} %get-tuple-element.132), channel_id=1, source_target_pairs={{0,1},{1,0},{2,3},{3,2},{4,5},{5,4},{6,7},{7,6},{8,9},{9,8},{10,11... | collective-permute-start | bytes 7077896 | tf_op jit(solution)/shard_map/ppermute | solution.py:901
  468.2 37.6 %collective-permute-start.4 = (bf16[2,3,96,768]{3,2,1,0:T(8,128)(2,1)S(1)}, bf16[2,3,96,768]{3,2,1,0:T(8,128)(2,1)S(1)}, u32[]{:S(2)}, u32[]{:S(2)}) collective-permute-start(bf16[2,3,96,768]{3,2,1,0:T(8,128)(2,1)S(1)} %pad_maximum_fusion.6), channel_id=1, source_target_pairs={{0,4},{1,5},{2,6},{3,7},{4,0},{5,1},{6,2},{7,3},{8,12},{9,13},{10,... | collective-permute-start | bytes 2654216 | tf_op jit(solution)/shard_map/ppermute | solution.py:901
  524.3 24.1 %collective-permute-start.11 = (bf16[96,768]{1,0:T(8,128)(2,1)S(1)}, bf16[96,768]{1,0:T(8,128)(2,1)S(1)}, u32[]{:S(2)}, u32[]{:S(2)}) collective-permute-start(bf16[96,768]{1,0:T(8,128)(2,1)S(1)} %pad_maximum_fusion.24), channel_id=1, source_target_pairs={{0,24},{8,16},{16,8},{24,0},{1,25},{9,17},{17,9},{25,1},{2,26},{10... | collective-permute-start | bytes 442376 | tf_op jit(solution)/shard_map/ppermute | solution.py:901
  527.9 27.1 %collective-permute-start.10 = (bf16[96,768]{1,0:T(8,128)(2,1)S(1)}, bf16[96,768]{1,0:T(8,128)(2,1)S(1)}, u32[]{:S(2)}, u32[]{:S(2)}) collective-permute-start(bf16[96,768]{1,0:T(8,128)(2,1)S(1)} %pad_maximum_fusion.23), channel_id=1, source_target_pairs={{0,16},{8,24},{16,0},{24,8},{1,17},{9,25},{17,1},{25,9},{2,18},{10... | collective-permute-start | bytes 442376 | tf_op jit(solution)/shard_map/ppermute | solution.py:901
  528.2 26.8 %collective-permute-start.9 = (bf16[96,768]{1,0:T(8,128)(2,1)S(1)}, bf16[96,768]{1,0:T(8,128)(2,1)S(1)}, u32[]{:S(2)}, u32[]{:S(2)}) collective-permute-start(bf16[96,768]{1,0:T(8,128)(2,1)S(1)} %pad_maximum_fusion.22), channel_id=1, source_target_pairs={{0,8},{8,0},{16,24},{24,16},{1,9},{9,1},{17,25},{25,17},{2,10},{10... | collective-permute-start | bytes 442376 | tf_op jit(solution)/shard_map/ppermute | solution.py:901
  566.8 32.7 %collective-permute-start.43 = (bf16[2,4,96,768]{3,2,1,0:T(8,128)(2,1)}, bf16[2,4,96,768]{3,2,1,0:T(8,128)(2,1)}, u32[]{:S(2)}, u32[]{:S(2)}) collective-permute-start(bf16[2,4,96,768]{3,2,1,0:T(8,128)(2,1)} %pad_maximum_fusion.4), channel_id=1, source_target_pairs={{0,2},{1,3},{2,0},{3,1},{4,6},{5,7},{6,4},{7,5},{8,10},{9,11},{10,... | collective-permute-start | bytes 3538952 | tf_op jit(solution)/shard_map/ppermute | solution.py:901
  567.6 29.2 %collective-permute-start.40 = (bf16[2,384,768]{2,1,0:T(8,128)(2,1)}, bf16[2,384,768]{2,1,0:T(8,128)(2,1)}, u32[]{:S(2)}, u32[]{:S(2)}) collective-permute-start(bf16[2,384,768]{2,1,0:T(8,128)(2,1)} %pad_maximum_fusion.3), channel_id=1, source_target_pairs={{0,4},{1,5},{2,6},{3,7},{4,0},{5,1},{6,2},{7,3},{8,12},{9,13},{10,... | collective-permute-start | bytes 3538952 | tf_op jit(solution)/shard_map/ppermute | solution.py:901
  568.9 52.3 %collective-permute-start.31 = (bf16[2,4,96,768]{3,2,1,0:T(8,128)(2,1)}, bf16[2,4,96,768]{3,2,1,0:T(8,128)(2,1)}, u32[]{:S(2)}, u32[]{:S(2)}) collective-permute-start(bf16[2,4,96,768]{3,2,1,0:T(8,128)(2,1)} %pad_maximum_fusion.1), channel_id=1, source_target_pairs={{0,2},{1,3},{2,0},{3,1},{4,6},{5,7},{6,4},{7,5},{8,10},{9,11},{10,... | collective-permute-start | bytes 3538952 | tf_op jit(solution)/shard_map/ppermute | solution.py:901
  572.2 51.3 %collective-permute-start.28 = (bf16[2,384,768]{2,1,0:T(8,128)(2,1)}, bf16[2,384,768]{2,1,0:T(8,128)(2,1)}, u32[]{:S(2)}, u32[]{:S(2)}) collective-permute-start(bf16[2,384,768]{2,1,0:T(8,128)(2,1)} %pad_maximum_fusion), channel_id=1, source_target_pairs={{0,4},{1,5},{2,6},{3,7},{4,0},{5,1},{6,2},{7,3},{8,12},{9,13},{10,... | collective-permute-start | bytes 3538952 | tf_op jit(solution)/shard_map/ppermute | solution.py:901
  598.3 35.6 %collective-permute-start.41 = (bf16[1,384,768]{2,1,0:T(8,128)(2,1)S(1)}, bf16[1,384,768]{2,1,0:T(8,128)(2,1)S(1)}, u32[]{:S(2)}, u32[]{:S(2)}) collective-permute-start(bf16[1,384,768]{2,1,0:T(8,128)(2,1)S(1)} %add_convert_fusion.3), channel_id=1, source_target_pairs={{0,2},{1,3},{2,0},{3,1},{4,6},{5,7},{6,4},{7,5},{8,10},{9,11},{10,... | collective-permute-start | bytes 1769480 | tf_op jit(solution)/shard_map/ppermute | solution.py:901
  601.1 34.3 %collective-permute-start.44 = (bf16[1,4,96,768]{3,2,1,0:T(8,128)(2,1)S(1)}, bf16[1,4,96,768]{3,2,1,0:T(8,128)(2,1)S(1)}, u32[]{:S(2)}, u32[]{:S(2)}) collective-permute-start(bf16[1,4,96,768]{3,2,1,0:T(8,128)(2,1)S(1)} %add_convert_fusion), channel_id=1, source_target_pairs={{0,4},{1,5},{2,6},{3,7},{4,0},{5,1},{6,2},{7,3},{8,12},{9,13},{10,... | collective-permute-start | bytes 1769480 | tf_op jit(solution)/shard_map/ppermute | solution.py:901
  643.8 41.6 %collective-permute-start.46 = (bf16[192,768]{1,0:T(8,128)(2,1)S(1)}, bf16[192,768]{1,0:T(8,128)(2,1)S(1)}, u32[]{:S(2)}, u32[]{:S(2)}) collective-permute-start(bf16[192,768]{1,0:T(8,128)(2,1)S(1)} %pad_maximum_fusion.20), channel_id=1, source_target_pairs={{0,16},{8,24},{16,0},{24,8},{1,17},{9,25},{17,1},{25,9},{2,18},{10... | collective-permute-start | bytes 884744 | tf_op jit(solution)/shard_map/ppermute | solution.py:901
  644.0 41.5 %collective-permute-start.45 = (bf16[192,768]{1,0:T(8,128)(2,1)S(1)}, bf16[192,768]{1,0:T(8,128)(2,1)S(1)}, u32[]{:S(2)}, u32[]{:S(2)}) collective-permute-start(bf16[192,768]{1,0:T(8,128)(2,1)S(1)} %pad_maximum_fusion.19), channel_id=1, source_target_pairs={{0,8},{8,0},{16,24},{24,16},{1,9},{9,1},{17,25},{25,17},{2,10},{10... | collective-permute-start | bytes 884744 | tf_op jit(solution)/shard_map/ppermute | solution.py:901
  648.9 37.1 %collective-permute-start.35 = (bf16[192,768]{1,0:T(8,128)(2,1)S(1)}, bf16[192,768]{1,0:T(8,128)(2,1)S(1)}, u32[]{:S(2)}, u32[]{:S(2)}) collective-permute-start(bf16[192,768]{1,0:T(8,128)(2,1)S(1)} %pad_maximum_fusion.18), channel_id=1, source_target_pairs={{0,24},{8,16},{16,8},{24,0},{1,25},{9,17},{17,9},{25,1},{2,26},{10... | collective-permute-start | bytes 884744 | tf_op jit(solution)/shard_map/ppermute | solution.py:901
  650.0 60.7 %collective-permute-start.34 = (bf16[192,768]{1,0:T(8,128)(2,1)S(1)}, bf16[192,768]{1,0:T(8,128)(2,1)S(1)}, u32[]{:S(2)}, u32[]{:S(2)}) collective-permute-start(bf16[192,768]{1,0:T(8,128)(2,1)S(1)} %pad_maximum_fusion.17), channel_id=1, source_target_pairs={{0,16},{8,24},{16,0},{24,8},{1,17},{9,25},{17,1},{25,9},{2,18},{10... | collective-permute-start | bytes 884744 | tf_op jit(solution)/shard_map/ppermute | solution.py:901
  654.5 56.2 %collective-permute-start.33 = (bf16[192,768]{1,0:T(8,128)(2,1)S(1)}, bf16[192,768]{1,0:T(8,128)(2,1)S(1)}, u32[]{:S(2)}, u32[]{:S(2)}) collective-permute-start(bf16[192,768]{1,0:T(8,128)(2,1)S(1)} %pad_maximum_fusion.16), channel_id=1, source_target_pairs={{0,8},{8,0},{16,24},{24,16},{1,9},{9,1},{17,25},{25,17},{2,10},{10... | collective-permute-start | bytes 884744 | tf_op jit(solution)/shard_map/ppermute | solution.py:901
  685.6 25.4 %collective-permute-start.50 = (bf16[192,768]{1,0:T(8,128)(2,1)S(1)}, bf16[192,768]{1,0:T(8,128)(2,1)S(1)}, u32[]{:S(2)}, u32[]{:S(2)}) collective-permute-start(bf16[192,768]{1,0:T(8,128)(2,1)S(1)} %fusion.5), channel_id=1, source_target_pairs={{0,24},{8,16},{16,8},{24,0},{1,25},{9,17},{17,9},{25,1},{2,26},{10... | collective-permute-start | bytes 884744 | tf_op jit(solution)/shard_map/ppermute | solution.py:901
  685.9 43.7 %collective-permute-start.49 = (bf16[192,768]{1,0:T(8,128)(2,1)S(1)}, bf16[192,768]{1,0:T(8,128)(2,1)S(1)}, u32[]{:S(2)}, u32[]{:S(2)}) collective-permute-start(bf16[192,768]{1,0:T(8,128)(2,1)S(1)} %fusion.5), channel_id=1, source_target_pairs={{0,16},{8,24},{16,0},{24,8},{1,17},{9,25},{17,1},{25,9},{2,18},{10... | collective-permute-start | bytes 884744 | tf_op jit(solution)/shard_map/ppermute | solution.py:901
  685.9 43.7 %collective-permute-start.48 = (bf16[192,768]{1,0:T(8,128)(2,1)S(1)}, bf16[192,768]{1,0:T(8,128)(2,1)S(1)}, u32[]{:S(2)}, u32[]{:S(2)}) collective-permute-start(bf16[192,768]{1,0:T(8,128)(2,1)S(1)} %fusion.5), channel_id=1, source_target_pairs={{0,8},{8,0},{16,24},{24,16},{1,9},{9,1},{17,25},{25,17},{2,10},{10... | collective-permute-start | bytes 884744 | tf_op jit(solution)/shard_map/ppermute | solution.py:901
  710.9 27.3 %collective-permute-start.37 = (bf16[192,768]{1,0:T(8,128)(2,1)S(1)}, bf16[192,768]{1,0:T(8,128)(2,1)S(1)}, u32[]{:S(2)}, u32[]{:S(2)}) collective-permute-start(bf16[192,768]{1,0:T(8,128)(2,1)S(1)} %fusion.2), channel_id=1, source_target_pairs={{0,16},{8,24},{16,0},{24,8},{1,17},{9,25},{17,1},{25,9},{2,18},{10... | collective-permute-start | bytes 884744 | tf_op jit(solution)/shard_map/ppermute | solution.py:901
  711.0 27.2 %collective-permute-start.36 = (bf16[192,768]{1,0:T(8,128)(2,1)S(1)}, bf16[192,768]{1,0:T(8,128)(2,1)S(1)}, u32[]{:S(2)}, u32[]{:S(2)}) collective-permute-start(bf16[192,768]{1,0:T(8,128)(2,1)S(1)} %fusion.2), channel_id=1, source_target_pairs={{0,8},{8,0},{16,24},{24,16},{1,9},{9,1},{17,25},{25,17},{2,10},{10... | collective-permute-start | bytes 884744 | tf_op jit(solution)/shard_map/ppermute | solution.py:901
  (58 other events, 737.2 us)

commit v3 on v2

--- a/solution.py
+++ b/solution.py
@@ -48,6 +48,14 @@
             index = index + bit - 2 * bit * ((index // bit) % 2)
         bit *= 2
     return index
+
+
+def exclusive_or(a, b, count):
+    total, bit = 0, 1
+    while bit < count:
+        total = total + bit * ((a // bit + b // bit) % 2)
+        bit *= 2
+    return total
 
 
 def greet(n, bits):
@@ -164,6 +172,241 @@
         compiler_params=pltpu.CompilerParams(collective_id=collective_id, has_side_effects=True),
         name="gather_weights",
     )(*shards)
+
+
+BLOCK = 96
+
+
+def add_rows(rows, target, sources):
+    def step(block, carry):
+        at = pl.ds(pl.multiple_of(block * BLOCK, BLOCK), BLOCK)
+        total = None
+        for ref, lead in sources:
+            value = ref[(*lead, at)].astype(f32)
+            total = value if total is None else total + value
+        ref, lead = target
+        ref[(*lead, at)] = total.astype(ref.dtype)
+        return carry
+
+    lax.fori_loop(0, rows // BLOCK, step, 0)
+
+
+class Reduce:
+    def __init__(self, halves, scratch, bits):
+        self.keep, self.send = halves[:2], halves[2:]
+        self.held, self.arrived = scratch[:2]
+        hops = len(bits)
+        self.hop_in = scratch[2 : 2 + hops]
+        self.sems, self.hop_send, self.hop_recv = scratch[2 + hops : 5 + hops]
+        self.orders = (bits[::-1], bits)
+        self.chips, self.rows = self.held.shape[1:3]
+        self.me = lax.axis_index("fsdp")
+
+    def load(self, stream):
+        return pltpu.make_async_copy(self.keep[stream], self.held.at[stream], self.sems.at[0, stream])
+
+    def core_copy(self, stream):
+        return pltpu.make_async_remote_copy(
+            src_ref=self.send[stream],
+            dst_ref=self.arrived.at[stream],
+            send_sem=self.sems.at[1, stream],
+            recv_sem=self.sems.at[2, stream],
+            device_id={"fsdp": flip(self.me, 1)},
+            device_id_type=pl.DeviceIdType.MESH,
+        )
+
+    def begin(self):
+        for stream in range(2):
+            self.core_copy(stream).start()
+            self.load(stream).start()
+
+    def leaving(self, stream, hop):
+        gone = [bit // 2 for bit in self.orders[stream][:hop]]
+        half = self.orders[stream][hop] // 2
+        return half, [p for p in range(self.chips) if p & half and not any(p & g for g in gone)]
+
+    def terms(self, stream, place, hops):
+        found = [(self.held, (stream, place)), (self.arrived, (stream, place))]
+        for hop in range(hops):
+            half, places = self.leaving(stream, hop)
+            found.append((self.hop_in[hop], (stream, places.index(place | half))))
+        return found
+
+    def hop_copy(self, stream, hop, slot, place):
+        return pltpu.make_async_remote_copy(
+            src_ref=self.held.at[stream, place],
+            dst_ref=self.hop_in[hop].at[stream, slot],
+            send_sem=self.hop_send.at[stream, hop, slot],
+            recv_sem=self.hop_recv.at[stream, hop, slot],
+            device_id={"fsdp": flip(self.me, self.orders[stream][hop])},
+            device_id_type=pl.DeviceIdType.MESH,
+        )
+
+    def wait_before(self, stream, hop):
+        if hop == 0:
+            self.load(stream).wait()
+            self.core_copy(stream).wait_recv()
+        else:
+            _, places = self.leaving(stream, hop - 1)
+            for slot, place in enumerate(places):
+                self.hop_copy(stream, hop - 1, slot, place).wait_recv()
+
+    def hop(self, at):
+        for stream in range(2):
+            self.wait_before(stream, at)
+            _, places = self.leaving(stream, at)
+            for place in places:
+                add_rows(self.rows, (self.held, (stream, place)), self.terms(stream, place, at))
+            for slot, place in enumerate(places):
+                self.hop_copy(stream, at, slot, place).start()
+
+    def finish(self, result):
+        hops = len(self.hop_in)
+        for stream in range(2):
+            self.wait_before(stream, hops)
+            add_rows(self.rows, (result, (stream,)), self.terms(stream, 0, hops))
+        for stream in range(2):
+            self.core_copy(stream).wait_send()
+            for hop in range(hops):
+                _, places = self.leaving(stream, hop)
+                for slot, place in enumerate(places):
+                    self.hop_copy(stream, hop, slot, place).wait_send()
+
+
+def reduce_scratch(chips, rows, width, hops):
+    return (
+        [pltpu.VMEM((2, chips, rows, width), bf16)] * 2
+        + [pltpu.VMEM((2, chips >> (hop + 1), rows, width), bf16) for hop in range(hops)]
+        + [pltpu.SemaphoreType.DMA((3, 2))]
+        + [pltpu.SemaphoreType.DMA((2, hops, chips // 2))] * 2
+    )
+
+
+class Spread:
+    def __init__(self, count, scratch):
+        self.total, self.outgoing, self.incoming, self.whole, self.load_sems, self.sems = scratch
+        self.bits = []
+        bit = 1
+        while bit < count:
+            self.bits.append(bit)
+            bit *= 2
+        self.rank = lax.axis_index("rep")
+        self.rows = self.total.shape[1]
+
+    def load(self, stream, source):
+        return pltpu.make_async_copy(source.at[stream], self.total.at[stream, pl.ds(0, source.shape[1])], self.load_sems.at[stream])
+
+    def side(self, bit):
+        return (self.rank // bit) % 2
+
+    def span(self, stage):
+        start, size = 0, self.rows
+        for bit in self.bits[:stage]:
+            size //= 2
+            start = start + self.side(bit) * size
+        return start, size
+
+    def down_copy(self, stream, stage):
+        size = self.rows >> (stage + 1)
+        at = pl.ds(self.rows - (self.rows >> stage), size)
+        return pltpu.make_async_remote_copy(
+            src_ref=self.outgoing.at[stream, at],
+            dst_ref=self.incoming.at[stream, at],
+            send_sem=self.sems.at[0, stream, stage],
+            recv_sem=self.sems.at[1, stream, stage],
+            device_id={"rep": flip(self.rank, self.bits[stage])},
+            device_id_type=pl.DeviceIdType.MESH,
+        )
+
+    def up_copy(self, stream, stage):
+        start, size = self.span(stage + 1)
+        at = pl.ds(pl.multiple_of(start, 16), size)
+        return pltpu.make_async_remote_copy(
+            src_ref=self.whole.at[stream, at],
+            dst_ref=self.whole.at[stream, at],
+            send_sem=self.sems.at[2, stream, stage],
+            recv_sem=self.sems.at[3, stream, stage],
+            device_id={"rep": flip(self.rank, self.bits[stage])},
+            device_id_type=pl.DeviceIdType.MESH,
+        )
+
+    def act(self, stream, tick):
+        stages = len(self.bits)
+        if 0 < tick <= stages:
+            stage = tick - 1
+            self.down_copy(stream, stage).wait_recv()
+            start, size = self.span(tick)
+            base = self.rows - (self.rows >> stage)
+            at = pl.ds(pl.multiple_of(start, 16), size)
+            self.total[stream, at] += self.incoming[stream, pl.ds(base, size)].astype(f32)
+        if tick < stages:
+            bit = self.bits[tick]
+            start, size = self.span(tick)
+            size //= 2
+            base = self.rows - (self.rows >> tick)
+            at = pl.ds(pl.multiple_of(start + (1 - self.side(bit)) * size, 16), size)
+            self.outgoing[stream, pl.ds(base, size)] = self.total[stream, at].astype(bf16)
+            self.down_copy(stream, tick).start()
+        elif tick == stages:
+            start, size = self.span(stages)
+            at = pl.ds(pl.multiple_of(start, 16), size)
+            self.whole[stream, at] = self.total[stream, at].astype(bf16)
+            self.up_copy(stream, stages - 1).start()
+        else:
+            stage = 2 * stages - tick
+            self.up_copy(stream, stage).wait_recv()
+            if stage:
+                self.up_copy(stream, stage - 1).start()
+
+    @property
+    def ticks(self):
+        return 2 * len(self.bits) + 2
+
+    def tick(self, tick):
+        for stream in range(2):
+            if 0 <= tick - stream <= 2 * len(self.bits):
+                self.act(stream, tick - stream)
+
+    def end(self):
+        for stream in range(2):
+            for stage in range(len(self.bits)):
+                self.down_copy(stream, stage).wait_send()
+                self.up_copy(stream, stage).wait_send()
+
+
+def padded(rows, count):
+    return -(-rows // (16 * count)) * 16 * count
+
+
+def spread_scratch(rows, width, count):
+    rows = padded(rows, count)
+    stages = count.bit_length() - 1
+    return [
+        pltpu.VMEM((2, rows, width), f32),
+        pltpu.VMEM((2, rows, width), bf16),
+        pltpu.VMEM((2, rows, width), bf16),
+        pltpu.VMEM((2, rows, width), bf16),
+        pltpu.SemaphoreType.DMA((2,)),
+        pltpu.SemaphoreType.DMA((4, 2, stages)),
+    ]
+
+
+def greet_both(n, reps, fsdp_bits, rep_bits):
+    me, rank = lax.axis_index("fsdp"), lax.axis_index("rep")
+    barrier = pltpu.get_barrier_semaphore()
+    for bit in fsdp_bits:
+        pl.semaphore_signal(barrier, inc=1, device_id={"fsdp": flip(me, bit)}, device_id_type=pl.DeviceIdType.MESH)
+    for bit in rep_bits:
+        pl.semaphore_signal(barrier, inc=1, device_id={"rep": flip(rank, bit)}, device_id_type=pl.DeviceIdType.MESH)
+    pl.semaphore_wait(barrier, len(fsdp_bits) + len(rep_bits))
+
+
+def bits_below(count, first=1):
+    bits = []
+    while first < count:
+        bits.append(first)
+        first *= 2
+    return bits
 
 
 def norm_forward(total, gain, shift):
@@ -483,7 +726,7 @@
 def shard_copies(n, me, source_of, keep_of, send_of, sems):
     def each(start):
         for owner in range(n):
-            mask = me ^ owner
+            mask = flip(me, owner)
             place = mask // 2
 
             @pl.when(mask % 2 == 0)
@@ -499,13 +742,54 @@
     return each
 
 
-def ffn_backward_kernel(n, me_ref, g_ref, valid_ref, n2_ref, r2_ref, low_ref, n1_ref, r1_ref, small_ref, act_ref, slope_ref, *refs):
-    up_ref, down_ref = refs[:2]
-    gs1_ref, ga1_ref, sums_ref, up_sum_ref, down_keep, down_send, up_keep, up_send = refs[2:10]
-    w_up, w_down, gs2, gffn, gpre, acc, low_turned, d_down, d_up, sems, out_sems = refs[10:]
+def ffn_backward_kernel(n, reps, carry, g_ref, valid_ref, n2_ref, r2_ref, low_ref, n1_ref, r1_ref, small_ref, act_ref, slope_ref, *refs):
+    up_ref, down_ref, refs = refs[0], refs[1], refs[2:]
+    if carry:
+        halves, spread_from, refs = refs[:4], refs[4], refs[5:]
+    gs1_ref, ga1_ref, sums_ref, up_sum_ref, down_keep, down_send, up_keep, up_send = refs[:8]
+    refs = refs[8:]
+    if carry:
+        reduced_ref, spread_ref, refs = refs[0], refs[1], refs[2:]
+    w_up, w_down, gs2, gffn, gpre, acc, low_turned, d_down, d_up, sems, out_sems = refs[:11]
+    if carry:
+        hops = len(bits_below(n, 2))
+        reduce = Reduce(halves, refs[11 : 16 + hops], bits_below(n, 2))
+        spread = Spread(reps, refs[16 + hops : 22 + hops])
+        spread_sem = refs[22 + hops]
     step, steps = pl.program_id(0), pl.num_programs(0)
-    me = me_ref[0]
+    me = lax.axis_index("fsdp")
     rows, width = gs2.shape
+    last_step = steps - 1
+    if carry:
+        out_copy = pltpu.make_async_copy(spread.whole, spread_ref, spread_sem)
+
+        @pl.when(step == 0)
+        def _():
+            greet_both(n, reps, bits_below(n), bits_below(reps))
+            reduce.begin()
+            for stream in range(2):
+                spread.load(stream, spread_from).start()
+            for stream in range(2):
+                spread.load(stream, spread_from).wait()
+            spread.tick(0)
+
+        @pl.when(step == 1)
+        def _():
+            reduce.hop(0)
+            spread.tick(1)
+
+        @pl.when(step == 2)
+        def _():
+            spread.tick(3)
+            for hop in range(1, hops):
+                reduce.hop(hop)
+
+        @pl.when(step == 3)
+        def _():
+            for tick in range(5, spread.ticks):
+                spread.tick(tick)
+            out_copy.start()
+            reduce.finish(reduced_ref)
     chunk = act_ref.shape[1]
     per_down = down_keep.shape[1]
     per_up = up_keep.shape[2]
@@ -567,12 +851,21 @@
         return carry
 
     lax.fori_loop(0, rows // ROWS, through, 0)
+    if carry:
+
+        @pl.when(step == 1)
+        def _():
+            spread.tick(2)
+
+        @pl.when(step == 2)
+        def _():
+            spread.tick(4)
 
     def down_out(which):
         def run(start):
             for local in range(chunk // per_down):
                 owner = which * (chunk // per_down) + local
-                mask = me ^ owner
+                mask = exclusive_or(me, owner, n)
                 source = d_down.at[pl.ds(local * per_down, per_down), :]
                 place = mask // 2
 
@@ -641,18 +934,42 @@
         lax.fori_loop(0, rows // ROWS, finish, 0)
         down_out(step)(False)
         up_out(step)(False)
-
-
-def ffn_backward(me, grad, valid, n2, r2, low, n1, r1, small, act, slope, w_up, w_down, n):
+        if carry:
+            out_copy.wait()
+            spread.end()
+
+
+def remote_params(collective_id):
+    return pltpu.CompilerParams(
+        dimension_semantics=("arbitrary",),
+        vmem_limit_bytes=VMEM_BYTES,
+        collective_id=collective_id,
+        has_side_effects=True,
+    )
+
+
+def ffn_backward(n, reps, grad, valid, n2, r2, low, n1, r1, small, act, slope, w_up, w_down, carry, collective_id):
     rows, width = grad.shape
     units = act.shape[1]
     chunk = width
     steps = units // chunk
     chips = n // 2
+    hops = len(bits_below(n, 2))
+    extra_out, extra_specs, extra_scratch = [], [], []
+    if carry:
+        reduced = (2,) + carry[0].shape[1:]
+        spread_rows = carry[4].shape[1]
+        extra_out = [
+            jax.ShapeDtypeStruct(reduced, f32),
+            jax.ShapeDtypeStruct((2, padded(spread_rows, reps), width), bf16),
+        ]
+        extra_specs = [whole(reduced), ANY]
+        extra_scratch = reduce_scratch(chips, carry[0].shape[1], width, hops)
+        extra_scratch += spread_scratch(spread_rows, width, reps) + [pltpu.SemaphoreType.DMA]
     down_half = jax.ShapeDtypeStruct((chips, units // n, width), bf16)
     up_half = jax.ShapeDtypeStruct((chips, steps, width // n, chunk), bf16)
     return pl.pallas_call(
-        functools.partial(ffn_backward_kernel, n),
+        functools.partial(ffn_backward_kernel, n, reps, bool(carry)),
         out_shape=(
             jax.ShapeDtypeStruct((rows, width), f32),
             jax.ShapeDtypeStruct((rows, width), bf16),
@@ -662,9 +979,10 @@
             down_half,
             up_half,
             up_half,
+            *extra_out,
         ),
         grid_spec=pltpu.PrefetchScalarGridSpec(
-            num_scalar_prefetch=1,
+            num_scalar_prefetch=0,
             grid=(steps,),
             in_specs=[
                 whole((rows, width)),
@@ -678,14 +996,15 @@
                 column_block(rows, chunk),
                 column_block(rows, chunk),
             ]
-            + [ANY] * 2,
+            + [ANY] * (2 + len(carry)),
             out_specs=[
                 whole((rows, width)),
                 whole((rows, width)),
                 whole((8, width)),
                 column_block(1, chunk),
             ]
-            + [ANY] * 4,
+            + [ANY] * 4
+            + extra_specs,
             scratch_shapes=[
                 pltpu.VMEM((width, units), bf16),
                 pltpu.VMEM((units, width), bf16),
@@ -698,22 +1017,54 @@
                 pltpu.VMEM((width, chunk), bf16),
                 pltpu.SemaphoreType.DMA((2,)),
                 pltpu.SemaphoreType.DMA((2, n)),
-            ],
+            ]
+            + extra_scratch,
         ),
-        compiler_params=pltpu.CompilerParams(
-            dimension_semantics=("arbitrary",), vmem_limit_bytes=VMEM_BYTES
-        ),
+        compiler_params=remote_params(collective_id)
+        if carry
+        else pltpu.CompilerParams(dimension_semantics=("arbitrary",), vmem_limit_bytes=VMEM_BYTES),
         cost_estimate=cost(10 * rows * width * units, 8 * rows * units),
         name="ffn_backward",
-    )(me, grad, valid, n2, r2, low, n1, r1, small, act, slope, w_up, w_down)
-
-
-def attend_backward_kernel(n, seqs, me_ref, ga_ref, gs_ref, base_ref, mask_ref, q_ref, k_ref, v_ref, ctx_ref, lse_ref, *refs):
-    qkv_ref, out_ref = refs[:2]
-    gh_ref, sums_ref, qkv_keep, qkv_send, out_keep, out_send = refs[2:8]
-    w_qkv, w_out, acc, base_turned, gctx, gproj, d_qkv, d_out, p_all, ds_all, sems, out_sems = refs[8:]
+    )(grad, valid, n2, r2, low, n1, r1, small, act, slope, w_up, w_down, *carry)
+
+
+def attend_backward_kernel(n, reps, seqs, spreads, ga_ref, gs_ref, base_ref, mask_ref, q_ref, k_ref, v_ref, ctx_ref, lse_ref, *refs):
+    qkv_ref, out_ref, halves, refs = refs[0], refs[1], refs[2:6], refs[6:]
+    if spreads:
+        spread_from, refs = refs[0], refs[1:]
+    gh_ref, sums_ref, a_keep, b_keep, a_send, b_send, reduced_ref = refs[:7]
+    refs = refs[7:]
+    if spreads:
+        spread_ref, refs = refs[0], refs[1:]
+    w_qkv, w_out, acc, base_turned, gctx, gproj, d_qkv, d_out, p_all, ds_all, sems, out_sems = refs[:12]
+    hops = len(bits_below(n, 2))
+    reduce = Reduce(halves, refs[12 : 17 + hops], bits_below(n, 2))
     step, steps = pl.program_id(0), pl.num_programs(0)
-    me = me_ref[0]
+    me = lax.axis_index("fsdp")
+    if spreads:
+        spread = Spread(reps, refs[17 + hops : 23 + hops])
+        spread_copy = pltpu.make_async_copy(spread.whole, spread_ref, refs[23 + hops])
+
+    @pl.when(step == 0)
+    def _():
+        greet_both(n, reps, bits_below(n), bits_below(reps) if spreads else [])
+        reduce.begin()
+        if spreads:
+            for stream in range(2):
+                spread.load(stream, spread_from).start()
+            for stream in range(2):
+                spread.load(stream, spread_from).wait()
+            spread.tick(0)
+
+    if spreads:
+
+        @pl.when(step == 1)
+        def _():
+            spread.tick(2)
+
+        @pl.when(step == 2)
+        def _():
+            spread.tick(4)
     rows, width = ga_ref.shape
     seq = rows // seqs
     heads = GROUP // HEAD
@@ -749,6 +1100,11 @@
 
     lax.fori_loop(0, rows // ROWS, through, 0)
     d_out[pl.ds(columns, GROUP), :] = dot_nn(ctx_ref[...].T, ga_ref[...]).astype(bf16)
+
+    @pl.when(step == 2)
+    def _():
+        for hop in range(1, hops):
+            reduce.hop(hop)
 
     def attend(s, carry):
         at = pl.ds(pl.multiple_of(s * seq, seq), seq)
@@ -780,6 +1136,24 @@
     lax.fori_loop(0, seqs, attend, 0)
     sums_ref[...] = jnp.zeros_like(sums_ref)
 
+    @pl.when(step == 0)
+    def _():
+        reduce.hop(0)
+        if spreads:
+            spread.tick(1)
+
+    @pl.when(step == 1)
+    def _():
+        if spreads:
+            spread.tick(3)
+
+    @pl.when(step == 2)
+    def _():
+        if spreads:
+            for tick in range(5, spread.ticks):
+                spread.tick(tick)
+            spread_copy.start()
+
     def onward(block, carry):
         at = pl.ds(pl.multiple_of(block * ROWS, ROWS), ROWS)
         term = dot_nt(gproj[at, 0:GROUP], w_qkv[:, pl.ds(columns, GROUP)])
@@ -804,6 +1178,12 @@
 
     lax.fori_loop(0, rows // ROWS, onward, 0)
 
+    def place_of(part, a_half, b_half):
+        return a_half if part < 2 else b_half
+
+    def rows_of(part):
+        return pl.ds((part % 2) * per, per)
+
     def qkv_out(which, start):
         for part in range(3):
             at = pl.ds(pl.multiple_of(which * GROUP, GROUP), GROUP)
@@ -811,8 +1191,8 @@
                 n,
                 me,
                 lambda owner: d_qkv.at[pl.ds(owner * per, per), pl.ds(part * GROUP, GROUP)],
-                lambda place: qkv_keep.at[place, part, :, at],
-                lambda place: qkv_send.at[place, part, :, at],
+                lambda place: place_of(part, a_keep, b_keep).at[place, rows_of(part), at],
+                lambda place: place_of(part, a_send, b_send).at[place, rows_of(part), at],
                 out_sems.at[part],
             )(start)
 
@@ -834,42 +1214,56 @@
             n,
             me,
             lambda owner: d_out.at[pl.ds(owner * per, per), :],
-            lambda place: out_keep.at[place],
-            lambda place: out_send.at[place],
+            lambda place: b_keep.at[place, rows_of(3)],
+            lambda place: b_send.at[place, rows_of(3)],
             out_sems.at[3],
         )
         out_copy(True)
         qkv_out(step, False)
         out_copy(False)
-
-
-def attend_backward(me, ga, gs, base, key_mask, q, k, v, ctx, lse, w_qkv, w_out, seqs, out_type, n):
+        reduce.finish(reduced_ref)
+        if spreads:
+            spread_copy.wait()
+            spread.end()
+
+
+def attend_backward(n, reps, ga, gs, base, key_mask, q, k, v, ctx, lse, w_qkv, w_out, seqs, out_type, carry, collective_id):
     rows, width = ga.shape
     steps = width // GROUP
     seq = rows // seqs
     heads = GROUP // HEAD
     chips = n // 2
-    qkv_half = jax.ShapeDtypeStruct((chips, 3, width // n, width), bf16)
-    out_half = jax.ShapeDtypeStruct((chips, width // n, width), bf16)
+    half = jax.ShapeDtypeStruct((chips, 2 * width // n, width), bf16)
+    hops = len(bits_below(n, 2))
+    reduced = (2,) + carry[0].shape[1:]
+    extra_out, extra_specs = [], []
+    extra_scratch = reduce_scratch(chips, carry[0].shape[1], width, hops)
+    if len(carry) > 4:
+        spread_rows = carry[4].shape[1]
+        extra_out = [jax.ShapeDtypeStruct((2, padded(spread_rows, reps), width), bf16)]
+        extra_specs = [ANY]
+        extra_scratch += spread_scratch(spread_rows, width, reps) + [pltpu.SemaphoreType.DMA]
     return pl.pallas_call(
-        functools.partial(attend_backward_kernel, n, seqs),
+        functools.partial(attend_backward_kernel, n, reps, seqs, len(carry) > 4),
         out_shape=(
             jax.ShapeDtypeStruct((rows, width), out_type),
             jax.ShapeDtypeStruct((8, width), f32),
-            qkv_half,
-            qkv_half,
-            out_half,
-            out_half,
+            half,
+            half,
+            half,
+            half,
+            jax.ShapeDtypeStruct(reduced, f32),
+            *extra_out,
         ),
         grid_spec=pltpu.PrefetchScalarGridSpec(
-            num_scalar_prefetch=1,
+            num_scalar_prefetch=0,
             grid=(steps,),
             in_specs=[whole((rows, width))] * 3
             + [whole((rows, 1))]
             + [column_block(rows, GROUP)] * 4
             + [pl.BlockSpec((1, seqs * heads, seq), lambda j, *_: (j, 0, 0))]
-            + [ANY] * 2,
-            out_specs=[whole((rows, width)), column_block(8, GROUP)] + [ANY] * 4,
+            + [ANY] * (2 + len(carry)),
+            out_specs=[whole((rows, width)), column_block(8, GROUP)] + [ANY] * 4 + [whole(reduced)] + extra_specs,
             scratch_shapes=[
                 pltpu.VMEM((width, 3 * width), bf16),
                 pltpu.VMEM((width, width), bf16),
@@ -883,64 +1277,122 @@
                 pltpu.VMEM((seq, heads * seq), bf16),
                 pltpu.SemaphoreType.DMA((2,)),
                 pltpu.SemaphoreType.DMA((4, n)),
-            ],
+            ]
+            + extra_scratch,
         ),
-        compiler_params=pltpu.CompilerParams(
-            dimension_semantics=("arbitrary",), vmem_limit_bytes=VMEM_BYTES
-        ),
+        compiler_params=remote_params(collective_id),
         cost_estimate=cost(16 * rows * width * width + 40 * rows * seq * width, 20 * rows * width),
         name="attend_backward",
-    )(me, ga, gs, base, key_mask, q, k, v, ctx, lse, w_qkv, w_out)
+    )(ga, gs, base, key_mask, q, k, v, ctx, lse, w_qkv, w_out, *carry)
 
 
 def cost(flops, moved):
     return pl.CostEstimate(flops=int(flops), bytes_accessed=int(moved), transcendentals=0)
 
 
+def last_sums_kernel(n, reps, a_keep, b_keep, a_send, b_send, spread_from, small_ref, spread_ref, attend_ref, total_ref, *scratch):
+    bits, rep_bits = bits_below(n, 2), bits_below(reps)
+    hops = len(bits)
+    reduce = Reduce((a_keep, b_keep, a_send, b_send), scratch[: 5 + hops], bits)
+    first = Spread(reps, scratch[5 + hops : 11 + hops])
+    second = Spread(reps, scratch[11 + hops : 17 + hops])
+    reduced, small_out, small_in, small_sems, sems = scratch[17 + hops :]
+    axes = [("fsdp", bit) for bit in bits_below(n)] + [("rep", bit) for bit in rep_bits]
+
+    def small_copy(at):
+        axis, bit = axes[at]
+        return pltpu.make_async_remote_copy(
+            src_ref=small_out.at[at],
+            dst_ref=small_in.at[at],
+            send_sem=small_sems.at[0, at],
+            recv_sem=small_sems.at[1, at],
+            device_id={axis: flip(lax.axis_index(axis), bit)},
+            device_id_type=pl.DeviceIdType.MESH,
+        )
+
+    def small_step(at):
+        small_copy(at).wait_recv()
+        if at + 1 < len(axes):
+            small_out[at + 1] = small_out[at] + small_in[at]
+            small_copy(at + 1).start()
+        else:
+            total_ref[...] = small_out[at] + small_in[at]
+
+    greet_both(n, reps, bits_below(n), rep_bits)
+    reduce.begin()
+    for stream in range(2):
+        first.load(stream, spread_from).start()
+    small_out[0] = small_ref[...]
+    small_copy(0).start()
+    for stream in range(2):
+        first.load(stream, spread_from).wait()
+    first.tick(0)
+    reduce.hop(0)
+    small_step(0)
+    first.tick(1)
+    small_step(1)
+    first.tick(2)
+    for hop in range(1, hops):
+        reduce.hop(hop)
+    small_step(2)
+    first.tick(3)
+    reduce.finish(reduced)
+    rows = reduced.shape[1]
+    for stream in range(2):
+        second.total[stream, pl.ds(0, rows)] = reduced[stream]
+    second.tick(0)
+    for at in range(3, len(axes)):
+        small_step(at)
+    for tick in range(4, first.ticks):
+        first.tick(tick)
+        second.tick(tick - 3)
+    first_copy = pltpu.make_async_copy(first.whole, spread_ref, sems.at[0])
+    first_copy.start()
+    for tick in range(first.ticks - 3, second.ticks):
+        second.tick(tick)
+    second_copy = pltpu.make_async_copy(second.whole, attend_ref, sems.at[1])
+    second_copy.start()
+    first.end()
+    second.end()
+    for at in range(len(axes)):
+        small_copy(at).wait_send()
+    first_copy.wait()
+    second_copy.wait()
+
+
+def last_sums(n, reps, halves, spread_rows, small, collective_id):
+    chips, rows, width = halves[0].shape
+    hops = len(bits_below(n, 2))
+    count = len(bits_below(n)) + len(bits_below(reps))
+    vmem = pl.BlockSpec(memory_space=pltpu.VMEM)
+    return pl.pallas_call(
+        functools.partial(last_sums_kernel, n, reps),
+        out_shape=(
+            jax.ShapeDtypeStruct((2, padded(spread_rows.shape[1], reps), width), bf16),
+            jax.ShapeDtypeStruct((2, padded(rows, reps), width), bf16),
+            jax.ShapeDtypeStruct(small.shape, f32),
+        ),
+        in_specs=[ANY] * 5 + [vmem],
+        out_specs=(ANY, ANY, vmem),
+        scratch_shapes=reduce_scratch(chips, rows, width, hops)
+        + spread_scratch(spread_rows.shape[1], width, reps)
+        + spread_scratch(rows, width, reps)
+        + [
+            pltpu.VMEM((2, rows, width), f32),
+            pltpu.VMEM((count, *small.shape), f32),
+            pltpu.VMEM((count, *small.shape), f32),
+            pltpu.SemaphoreType.DMA((2, count)),
+            pltpu.SemaphoreType.DMA((2,)),
+        ],
+        compiler_params=pltpu.CompilerParams(
+            vmem_limit_bytes=VMEM_BYTES, collective_id=collective_id, has_side_effects=True
+        ),
+        name="last_sums",
+    )(*halves, spread_rows, small)
+
+
 def swap(array, axis, count, mask):
     return lax.ppermute(array, axis, [(i, i ^ mask) for i in range(count)])
-
-
-def scatter_pieces(keep, send, n, bits):
-    other = swap(send, "fsdp", n, 1)
-    terms = {place: [keep[place], other[place]] for place in range(n // 2)}
-
-    def total(items):
-        return sum(item.astype(f32) for item in items)
-
-    for bit in bits:
-        half = bit // 2
-        leaving = [place for place in sorted(terms) if place & half]
-        packed = jnp.stack([total(terms[place]).astype(bf16) for place in leaving])
-        arrived = swap(packed, "fsdp", n, bit)
-        for slot, place in enumerate(leaving):
-            terms[place ^ half].append(arrived[slot])
-            del terms[place]
-    return total(terms[0])
-
-
-def sum_replicas(shards, rank, count):
-    def parts_of(array, index):
-        split = array.reshape((count, array.shape[0] // count) + array.shape[1:])
-        return lax.dynamic_index_in_dim(split, index, 0, keepdims=False)
-
-    def packed(index):
-        return jnp.concatenate([parts_of(array, index) for array in shards], axis=0)
-
-    total = packed(rank)
-    for mask in range(1, count):
-        total = total + swap(packed(rank ^ mask).astype(bf16), "rep", count, mask).astype(f32)
-    low = total.astype(bf16)
-    pieces = jnp.stack([low] + [swap(low, "rep", count, mask) for mask in range(1, count)])
-    ordered = [lax.dynamic_index_in_dim(pieces, rank ^ place, 0, keepdims=False) for place in range(count)]
-    results = []
-    start = 0
-    for array in shards:
-        size = array.shape[0] // count
-        rows = [piece[start : start + size] for piece in ordered]
-        results.append(jnp.concatenate(rows, axis=0).astype(f32))
-        start += size
-    return results
 
 
 def gather_small(own, n, me):
@@ -960,8 +1412,6 @@
     units = w_up.shape[2]
     per = width // n
     me = lax.axis_index("fsdp").astype(jnp.int32)
-    rank = lax.axis_index("rep").astype(jnp.int32)
-    me_row = me[None]
 
     places = jnp.arange(seq, dtype=jnp.int32)
     inside = places[None, :] < lengths[:, None]
@@ -1012,54 +1462,59 @@
 
     grad = cotangent.reshape(rows, width)
     grad_valid = valid
-    shard_sums = [None] * LAYERS
-    small_sums = [None] * LAYERS
+    small_rows = [None] * LAYERS
+    attend_halves, attend_reduced, ffn_done, attend_done = None, None, [None] * LAYERS, [None] * LAYERS
+    ffn_reduced = None
     for layer in range(LAYERS - 1, -1, -1):
+        first = layer == LAYERS - 1
         base, q, k, v, ctx, lse, low, n1, r1, act, slope, n2, r2 = saved[layer]
-        gs1, ga1, sums, up_sum, down_keep, down_send, up_keep, up_send = ffn_backward(
-            me_row, grad, grad_valid, n2, r2, low, n1, r1, smalls[layer], act, slope, up[layer], down[layer], n
+        results = ffn_backward(
+            n, reps, grad, grad_valid, n2, r2, low, n1, r1, smalls[layer], act, slope, up[layer], down[layer],
+            () if first else (*attend_halves, ffn_reduced), 10 + layer,
         )
-        grad, proj_sums, qkv_keep, qkv_send, out_keep, out_send = attend_backward(
-            me_row, ga1, gs1, base, key_mask, q, k, v, ctx, lse, qkv[layer], out[layer], seqs,
-            f32 if layer else bf16, n,
+        gs1, ga1, sums, up_sum, down_keep, down_send, up_keep, up_send = results[:8]
+        if not first:
+            attend_reduced, ffn_done[layer + 1] = results[8:]
+        ffn_halves = (
+            down_keep,
+            up_keep.reshape(n // 2, -1, width),
+            down_send,
+            up_send.reshape(n // 2, -1, width),
         )
+        results = attend_backward(
+            n, reps, ga1, gs1, base, key_mask, q, k, v, ctx, lse, qkv[layer], out[layer], seqs,
+            f32 if layer else bf16, ffn_halves + (() if first else (attend_reduced,)), 20 + layer,
+        )
+        grad, proj_sums = results[:2]
+        attend_halves, ffn_reduced = results[2:6], results[6]
+        if not first:
+            attend_done[layer + 1] = results[7]
         grad_valid = ones
-        d_down = scatter_pieces(down_keep, down_send, n, chip_bits[::-1])
-        d_up = scatter_pieces(up_keep, up_send, n, chip_bits)
-        d_down, d_up = sum_replicas([d_down, d_up.reshape(-1, width)], rank, reps)
-        d_qkv = scatter_pieces(qkv_keep, qkv_send, n, chip_bits[::-1])
-        d_out = scatter_pieces(out_keep, out_send, n, chip_bits)
-        d_qkv, d_out = sum_replicas([d_qkv.reshape(-1, width), d_out], rank, reps)
-        d_up = d_up.reshape(units // width, per, width).transpose(1, 0, 2).reshape(per, units)
-        d_qkv = d_qkv.reshape(3, per, width).transpose(1, 0, 2).reshape(per, 3 * width)
-        shard_sums[layer] = (d_qkv, d_out, d_up, d_down)
-        bias_sums = jnp.stack([proj_sums[0], proj_sums[1], sums[5], sums[2], sums[4], sums[1]])
-        gain_sums = jnp.stack([sums[3], sums[0]])
-        small_sums[layer] = (up_sum.reshape(n, units // n), bias_sums, gain_sums)
+        small_rows[layer] = jnp.concatenate(
+            [sums[:6], proj_sums[:2], up_sum.reshape(units // width, width), jnp.zeros((8 - units // width, width), f32)]
+        )
     grad_tokens = grad.reshape(seqs, seq, width)
-
-    ups = jnp.stack([small_sums[layer][0] for layer in range(LAYERS)], axis=1).reshape(n, -1)
-    bias_rows = jnp.stack([small_sums[layer][1] for layer in range(LAYERS)])
-    bias_rows = bias_rows.reshape(LAYERS * 6, n, per).transpose(1, 0, 2).reshape(n, -1)
-    gain_rows = jnp.stack([small_sums[layer][2] for layer in range(LAYERS)])
-    gain_rows = gain_rows.reshape(LAYERS * 2, n, per).transpose(1, 0, 2).reshape(n, -1)
-    small_total = jnp.concatenate([ups, bias_rows, gain_rows], axis=1)
-    bit = 1
-    while bit < n:
-        small_total = small_total + swap(small_total, "fsdp", n, bit)
-        bit *= 2
-    mine = lax.dynamic_index_in_dim(small_total, me, 0, keepdims=True)
-    bit = 1
-    while bit < reps:
-        mine = mine + swap(mine, "rep", reps, bit)
-        bit *= 2
-    mine = mine[0]
-    grad_up_bias = mine[:cut_a].reshape(LAYERS, units // n)
-    grad_biases = mine[cut_a:cut_b].reshape(LAYERS, 6, per)
-    grad_gains = mine[cut_b:].reshape(LAYERS, 2, per)
-
-    stacked = [jnp.stack([shard_sums[layer][member] for layer in range(LAYERS)]) for member in range(4)]
-    return (outputs, grad_tokens, *stacked, grad_up_bias, grad_biases, grad_gains)
+    ffn_done[0], attend_done[0], small_total = last_sums(
+        n, reps, attend_halves, ffn_reduced, jnp.concatenate(small_rows), 30
+    )
+
+    ffn_rows, attend_rows = units // n, 2 * per
+    both_ffn = jnp.stack([done[:, :ffn_rows] for done in ffn_done])
+    both_attend = jnp.stack([done[:, :attend_rows] for done in attend_done])
+    grad_down = both_ffn[:, 0].astype(f32)
+    grad_up = both_ffn[:, 1].reshape(LAYERS, units // width, per, width).transpose(0, 2, 1, 3)
+    grad_up = grad_up.reshape(LAYERS, per, units).astype(f32)
+    parts = both_attend.reshape(LAYERS, 4, per, width)
+    grad_qkv = parts[:, :3].transpose(0, 2, 1, 3).reshape(LAYERS, per, 3 * width).astype(f32)
+    grad_out = parts[:, 3].astype(f32)
+
+    small_total = small_total.reshape(LAYERS, 16, width)
+    mine = lax.dynamic_slice_in_dim(small_total[:, :8], me * per, per, axis=2)
+    grad_biases = jnp.stack([mine[:, at] for at in (6, 7, 5, 2, 4, 1)], axis=1)
+    grad_gains = jnp.stack([mine[:, at] for at in (3, 0)], axis=1)
+    up_rows = small_total[:, 8 : 8 + units // width].reshape(LAYERS, units)
+    grad_up_bias = lax.dynamic_slice_in_dim(up_rows, me * (units // n), units // n, axis=1)
+    return (outputs, grad_tokens, grad_qkv, grad_out, grad_up, grad_down, grad_up_bias, grad_biases, grad_gains)
 
 
 def solution(mesh):

time: 747 us -> 561 us (0.75)
  waiting for transfers between devices: 175 us -> 1.92 us
  Pallas kernels: 404 us -> 526 us
  starting transfers between devices: 92.5 us -> 5.56 us
  other arithmetic: 43.1 us -> 7.34 us
  local copies, waits for them, and re-layouts: 26.6 us -> 17.7 us
    ppermute x56 -> x3, waiting for transfers between devices: 175 us -> 1.92 us  [swap(): return lax.ppermute(array, axis, [(i, i ^ mask) for i in range(count)])]
    pallas_call x4 -> x5, Pallas kernels: 204 us -> 326 us  [the longest x2 130 us: attend_backward(): pl.pallas_call(functools.partial(attend_backward_kernel, n, reps, seqs, l...]
    ppermute x56 -> x3, starting transfers between devices: 92.5 us -> 5.56 us  [swap(): return lax.ppermute(array, axis, [(i, i ^ mask) for i in range(count)])]
    convert_element_type x20 -> x2, other arithmetic: 18 us -> 2.49 us  [the longest x1 1.63 us: on_device(): grad_down = both_ffn[:, 0].astype(f32)]
    add x13 -> x0, other arithmetic: 11.6 us -> none  [the longest x8 10.8 us: total(): return sum((item.astype(f32) for item in items))]
    another operation x20 -> x1, other arithmetic: 10.6 us -> 0.58 us  [on_device(): grad_gains = jnp.stack([mine[:, at] for at in (3, 0)], axis=1)]
  transfers between devices with their start and end apart: 56 -> 3, of which waited for: 27 -> 2; matrix products, arithmetic and copies ran while one was open for 7% -> 0% of each run, Pallas kernels for 4% -> 5%
where the time goes in v3:
time: 561 us; the launch traced here: 560 us
  Pallas kernels  526 us (94%)
  local copies, waits for them, and re-layouts  17.7 us (3%)
  other arithmetic  7.34 us (1%)
    pallas_call x2, Pallas kernels, attend_backward(): pl.pallas_call(functools.partial(attend_backward_kernel, n, reps, seqs, l...  130 us
    pallas_call x2, Pallas kernels, ffn_backward(): pl.pallas_call(functools.partial(ffn_backward_kernel, n, reps, bool(carry...  115 us
    pallas_call x2, Pallas kernels, attend_forward(): pl.pallas_call(functools.partial(attend_forward_kernel, n, seqs, layer, o...  104 us
    pallas_call x1, Pallas kernels, last_sums(): pl.pallas_call(functools.partial(last_sums_kernel, n, reps), out_shape=(j...  80.8 us
    pallas_call x2, Pallas kernels, ffn_forward(): pl.pallas_call(functools.partial(ffn_forward_kernel, n, last, layer, orde...  69.5 us
    pallas_call x1, Pallas kernels, gather_weights(): pl.pallas_call(functools.partial(gather_kernel, n, layer, orders), out_sh...  26.9 us
  transfers between devices with their start and end apart: 3, of which 2 were waited for; matrix products, arithmetic and copies ran while one was open for 0% of the time, Pallas kernels for 5%

profile of v3, /device:TPU:0, one launch (start us, length us, event | category | flops | bytes accessed | tf_op | source)
XLA Modules:
  0.0 559.7 jit_solution(7810194406645277948)
XLA Ops:
  0.6 0.8 reshape.169
  4.3 2.9 collective-permute-start.1
  7.2 1.7 collective-permute-done.1
  9.0 2.1 collective-permute-start.2
  11.9 1.0 copy.45
  12.9 1.0 copy.48
  13.9 26.9 %gather_weights.1 = (bf16[768,2304]{1,0:T(8,128)(2,1)}, bf16[768,768]{1,0:T(8,128)(2,1)}) custom-call(bf16[2,96,2304]{2,1,0:T(8,128)(2,1)} %refs_0_.6, bf16[2,96,768]{2,1,0:T(8,128)(2,1)} %refs_1_.6), custom_call_target="tpu_custom_call" | custom-call | tf_op jit(solution)/shard_map/gather_weights/pallas_call | solution.py:166
  43.2 52.6 %attend_forward.2 = (bf16[1024,768]{1,0:T(8,128)(2,1)}, bf16[1024,768]{1,0:T(8,128)(2,1)}, bf16[1024,768]{1,0:T(8,128)(2,1)}, bf16[1024,768]{1,0:T(8,128)(2,1)},...) custom-call(bf16[1024,768]{1,0:T(8,128)(2,1)} %bitcast.103, ...), custom_call_target="tpu_custom_call" | custom-call | flops 11274289152 | bytes 15728640 | tf_op jit(solution)/shard_map/attend_forward/pallas_call | solution.py:535
  95.8 38.5 %ffn_forward.2 = (bf16[1024,3072]{1,0:T(8,128)(2,1)}, bf16[1024,3072]{1,0:T(8,128)(2,1)}, bf16[1024,768]{1,0:T(8,128)(2,1)}, f32[1024,1]{1,0:T(8,128)}, f32[1024...) custom-call(f32[1024,768]{1,0:T(8,128)} %get-tuple-element.84.mid_ref, ...), custom_call_target="tpu_custom_call" | custom-call | flops 19327352832 | bytes 25165824 | tf_op jit(solution)/shard_map/ffn_forward/pallas_call | solution.py:697
  134.4 50.9 %attend_forward.3 = (bf16[1024,768]{1,0:T(8,128)(2,1)}, bf16[1024,768]{1,0:T(8,128)(2,1)}, bf16[1024,768]{1,0:T(8,128)(2,1)}, bf16[1024,768]{1,0:T(8,128)(2,1)},...) custom-call(f32[1024,768]{1,0:T(8,128)} %get-tuple-element.88.x_ref,, ...), custom_call_target="tpu_custom_call" | custom-call | flops 11274289152 | bytes 15728640 | tf_op jit(solution)/shard_map/attend_forward/pallas_call | solution.py:535
  185.2 31.0 %ffn_forward.3 = (bf16[1024,3072]{1,0:T(8,128)(2,1)}, bf16[1024,3072]{1,0:T(8,128)(2,1)}, bf16[1024,768]{1,0:T(8,128)(2,1)}, f32[1024,1]{1,0:T(8,128)}, bf16[1024,768]{1,0:T(8,128)(2,1)}) custom-call(f32[1024,768]{1,0:T(8,128)} %get-tuple-element.91.mid_ref, bf16[1024,768]{1,0:T(8,128)(2,1)} %get-tuple-element.92.low_ref, ...), custom_call_target="tpu_custom_call" | custom-call | flops 19327352832 | bytes 25165824 | tf_op jit(solution)/shard_map/ffn_forward/pallas_call | solution.py:697
  216.2 44.9 %ffn_backward.2 = (f32[1024,768]{1,0:T(8,128)}, bf16[1024,768]{1,0:T(8,128)(2,1)}, f32[8,768]{1,0:T(8,128)}, f32[1,3072]{1,0:T(1,128)}, bf16[4,384,768]{2,1,0:T(...) custom-call(bf16[1024,768]{1,0:T(8,128)(2,1)} %bitcast.102, ...), custom_call_target="tpu_custom_call" | custom-call | flops 24159191040 | bytes 25165824 | tf_op jit(solution)/shard_map/ffn_backward/pallas_call | solution.py:971
  261.1 64.3 %attend_backward.2 = (f32[1024,768]{1,0:T(8,128)}, f32[8,768]{1,0:T(8,128)}, bf16[4,192,768]{2,1,0:T(8,128)(2,1)}, bf16[4,192,768]{2,1,0:T(8,128)(2,1)}, bf16[4,...) custom-call(bf16[1024,768]{1,0:T(8,128)(2,1)} %get-tuple-element.102.ga_ref, ...), custom_call_target="tpu_custom_call" | custom-call | flops 25769803776 | bytes 15728640 | tf_op jit(solution)/shard_map/attend_backward/pallas_call | solution.py:1246
  325.4 0.8 broadcast_in_dim.25.valid_ref
  326.2 69.8 %ffn_backward.3 = (f32[1024,768]{1,0:T(8,128)}, bf16[1024,768]{1,0:T(8,128)(2,1)}, f32[8,768]{1,0:T(8,128)}, f32[1,3072]{1,0:T(1,128)}, bf16[4,384,768]{2,1,0:T(...) custom-call(f32[1024,768]{1,0:T(8,128)} %get-tuple-element.114.g_ref, ...), custom_call_target="tpu_custom_call" | custom-call | flops 24159191040 | bytes 25165824 | tf_op jit(solution)/shard_map/ffn_backward/pallas_call | solution.py:971
  396.0 66.0 %attend_backward.3 = (bf16[1024,768]{1,0:T(8,128)(2,1)}, f32[8,768]{1,0:T(8,128)}, bf16[4,192,768]{2,1,0:T(8,128)(2,1)}, bf16[4,192,768]{2,1,0:T(8,128)(2,1)}, b...) custom-call(bf16[1024,768]{1,0:T(8,128)(2,1)} %get-tuple-element.126, ...), custom_call_target="tpu_custom_call" | custom-call | flops 25769803776 | bytes 15728640 | tf_op jit(solution)/shard_map/attend_backward/pallas_call | solution.py:1246
  465.4 2.5 concatenate.24.small_ref
  467.9 80.8 %last_sums.1 = (bf16[2,384,768]{2,1,0:T(8,128)(2,1)}, bf16[2,192,768]{2,1,0:T(8,128)(2,1)}, f32[32,768]{1,0:T(8,128)}) custom-call(bf16[4,192,768]{2,1,0:T(8,128)(2,1)} %get-tuple-element.139.a_keep, bf16[4,192,768]{2,1,0:T(8,128)(2,1)} %get-tuple-element.140.b_keep, bf16[4,192,768]{2,1,0:T(8,128)(2,1)} %get-tuple-element.141.a_send, ...), custom_call_target="tpu_custom_call" | custom-call | tf_op jit(solution)/shard_map/last_sums/pallas_call | solution.py:1368
  548.7 1.2 convert_bitcast_fusion.1
  549.9 0.9 fusion.5
  550.8 1.3 copy.42
  553.1 1.6 fusion.2
  554.9 1.7 copy.43
  558.6 1.1 copy.53
  (68 shorter events, 11.9 us)
Async XLA Ops:
  2.9 1.4 collective-permute-start
  4.3 4.6 collective-permute-start.1
  9.0 31.8 %collective-permute-start.2 = (f32[4,2304]{1,0:T(4,128)S(1)}, f32[4,2304]{1,0:T(4,128)S(1)}, u32[]{:S(2)}, u32[]{:S(2)}) collective-permute-start(f32[4,2304]{1,0:T(4,128)S(1)} %pad_maximum_fusion.2), channel_id=1, source_target_pairs={{0,4},{1,5},{2,6},{3,7},{4,0},{5,1},{6,2},{7,3},{8,12},{9,13},{10,... | collective-permute-start | bytes 110600 | tf_op jit(solution)/shard_map/ppermute | solution.py:1395
  396.0 67.3 %copy-start.9 = (f32[1,3072]{1,0:T(1,128)S(1)}, f32[1,3072]{1,0:T(1,128)}, u32[]{:S(2)}) copy-start(f32[1,3072]{1,0:T(1,128)} %get-tuple-element.146) | copy-start | bytes 36868
  396.0 68.7 %copy-start.8 = (f32[1,3072]{1,0:T(1,128)S(1)}, f32[1,3072]{1,0:T(1,128)}, u32[]{:S(2)}) copy-start(f32[1,3072]{1,0:T(1,128)} %get-tuple-element.149) | copy-start | bytes 36868
  396.0 69.4 %copy-start.6 = (f32[8,768]{1,0:T(8,128)S(1)}, f32[8,768]{1,0:T(8,128)}, u32[]{:S(2)}) copy-start(f32[8,768]{1,0:T(8,128)} %get-tuple-element.147) | copy-start | bytes 73732
  396.0 69.4 %copy-start.7 = (f32[8,768]{1,0:T(8,128)S(1)}, f32[8,768]{1,0:T(8,128)}, u32[]{:S(2)}) copy-start(f32[8,768]{1,0:T(8,128)} %get-tuple-element.144) | copy-start | bytes 73732
  467.9 80.8 %copy-start = (bf16[2,192,768]{2,1,0:T(8,128)(2,1)S(1)}, bf16[2,192,768]{2,1,0:T(8,128)(2,1)}, u32[]{:S(2)}) copy-start(bf16[2,192,768]{2,1,0:T(8,128)(2,1)} %get-tuple-element.151) | copy-start | bytes 1769476
  548.7 1.2 copy-start.1
  549.9 0.9 copy-start.5
  550.8 1.8 copy-start.3
  550.8 2.3 copy-start.4
  554.9 3.7 copy-start.2

commit v4 on v3

--- a/solution.py
+++ b/solution.py
@@ -12,6 +12,8 @@
 GROUP = 256
 ROWS = 256
 VMEM_BYTES = 60 * 1024 * 1024
+UP_PARTS = 4
+EARLY = 2
 
 epsilon = 1e-05
 big_negative = -1000000000.0
@@ -133,12 +135,18 @@
         gather.end()
 
 
-def make_gathers(n, layer, shards, wholes, orders, sems):
+def make_gathers(layer, parts, shards, wholes, sems):
     send_sems, recv_sems, local_sems = sems
-    return [
-        Gather(own.at[layer], full, order, send_sems.at[at], recv_sems.at[at], local_sems.at[at])
-        for at, (own, full, order) in enumerate(zip(shards, wholes, orders))
-    ]
+    gathers = []
+    for at, ((which, column, width, order), full) in enumerate(zip(parts, wholes)):
+        own = shards[which].at[layer, :, pl.ds(column, width)]
+        gathers.append(Gather(own, full, order, send_sems.at[at], recv_sems.at[at], local_sems.at[at]))
+    return gathers
+
+
+def parts_of(which, shard, count, orders, first=0):
+    step = shard.shape[2] // count
+    return [(which, at * step, step, orders[at % 2]) for at in range(first, count)]
 
 
 def gather_sems(n, count):
@@ -149,29 +157,44 @@
     ]
 
 
-def whole_of(n, shard):
-    return jax.ShapeDtypeStruct((shard.shape[1] * n, shard.shape[2]), shard.dtype)
-
-
-def gather_kernel(n, layer, orders, *refs):
-    count = len(orders)
-    gathers = make_gathers(n, layer, refs[:count], refs[count : 2 * count], orders, refs[2 * count :])
+def wholes_of(n, shards, parts):
+    return tuple(
+        jax.ShapeDtypeStruct((shards[which].shape[1] * n, width), shards[which].dtype) for which, _, width, _ in parts
+    )
+
+
+def gather_kernel(n, layer, parts, shard_count, *refs):
+    shards, wholes = refs[:shard_count], refs[shard_count : shard_count + len(parts)]
+    gathers = make_gathers(layer, parts, shards, wholes, refs[shard_count + len(parts) :])
     begin_all(n, gathers)
-    for round_at in range(len(orders[0])):
+    for round_at in range(len(gathers[0].order)):
         onward_all(gathers, round_at)
     end_all(gathers)
 
 
-def gather_weights(n, layer, shards, orders, collective_id):
+def gather_weights(n, layer, shards, parts, collective_id):
     return pl.pallas_call(
-        functools.partial(gather_kernel, n, layer, orders),
-        out_shape=tuple(whole_of(n, shard) for shard in shards),
+        functools.partial(gather_kernel, n, layer, parts, len(shards)),
+        out_shape=wholes_of(n, shards, parts),
         in_specs=[ANY] * len(shards),
-        out_specs=tuple([ANY] * len(shards)),
-        scratch_shapes=gather_sems(n, len(shards)),
+        out_specs=tuple([ANY] * len(parts)),
+        scratch_shapes=gather_sems(n, len(parts)),
         compiler_params=pltpu.CompilerParams(collective_id=collective_id, has_side_effects=True),
         name="gather_weights",
     )(*shards)
+
+
+def part_copies(sources, target, sems, first=0):
+    copies, column = [], 0
+    for at, source in enumerate(sources):
+        width = source.shape[1]
+        copies.append(pltpu.make_async_copy(source, target.at[:, pl.ds(column, width)], sems.at[first + at]))
+        column += width
+    return copies
+
+
+def both_copies(sources, count, targets, sems):
+    return part_copies(sources[:count], targets[0], sems), part_copies(sources[count:], targets[1], sems, count)
 
 
 BLOCK = 96
@@ -283,7 +306,8 @@
 
 
 class Spread:
-    def __init__(self, count, scratch):
+    def __init__(self, count, scratch, first=0):
+        self.first = first
         self.total, self.outgoing, self.incoming, self.whole, self.load_sems, self.sems = scratch
         self.bits = []
         bit = 1
@@ -291,10 +315,20 @@
             self.bits.append(bit)
             bit *= 2
         self.rank = lax.axis_index("rep")
-        self.rows = self.total.shape[1]
+        self.streams, self.rows = self.total.shape[:2]
 
     def load(self, stream, source):
-        return pltpu.make_async_copy(source.at[stream], self.total.at[stream, pl.ds(0, source.shape[1])], self.load_sems.at[stream])
+        target = self.total.at[stream, pl.ds(0, source.shape[1])]
+        return pltpu.make_async_copy(source.at[self.first + stream], target, self.load_sems.at[stream])
+
+    def begin(self, source):
+        for stream in range(self.streams):
+            self.load(stream, source).start()
+
+    def loaded(self, source):
+        for stream in range(self.streams):
+            self.load(stream, source).wait()
+        self.tick(0)
 
     def side(self, bit):
         return (self.rank // bit) % 2
@@ -360,34 +394,121 @@
 
     @property
     def ticks(self):
-        return 2 * len(self.bits) + 2
+        return 2 * len(self.bits) + self.streams
 
     def tick(self, tick):
-        for stream in range(2):
+        for stream in range(self.streams):
             if 0 <= tick - stream <= 2 * len(self.bits):
                 self.act(stream, tick - stream)
 
     def end(self):
-        for stream in range(2):
+        for stream in range(self.streams):
             for stage in range(len(self.bits)):
                 self.down_copy(stream, stage).wait_send()
                 self.up_copy(stream, stage).wait_send()
 
 
+CHAIN = 4
+PIECES = 2
+
+
+class Chain(Spread):
+    def __init__(self, count, scratch, first=0):
+        super().__init__(count, scratch, first)
+        self.inner = (self.rank == 1) | (self.rank == 2)
+        self.chunks = self.streams * PIECES
+
+    def place(self, chunk):
+        size = self.rows // PIECES
+        return chunk // PIECES, pl.ds((chunk % PIECES) * size, size)
+
+    def copy(self, leg, chunk):
+        stream, at = self.place(chunk)
+        source = self.whole if leg == 2 else self.outgoing
+        target = self.whole.at[stream, at] if leg == 2 else self.incoming.at[leg * self.streams + stream, at]
+        return pltpu.make_async_remote_copy(
+            src_ref=source.at[stream, at],
+            dst_ref=target,
+            send_sem=self.sems.at[2 * leg, chunk],
+            recv_sem=self.sems.at[2 * leg + 1, chunk],
+            device_id={"rep": flip(self.rank, 3 if leg == 1 else 1)},
+            device_id_type=pl.DeviceIdType.MESH,
+        )
+
+    def act(self, chunk, tick):
+        stream, at = self.place(chunk)
+
+        if tick == 0:
+
+            @pl.when(jnp.logical_not(self.inner))
+            def _():
+                self.outgoing[stream, at] = self.total[stream, at].astype(bf16)
+                self.copy(0, chunk).start()
+
+        elif tick == 3:
+
+            @pl.when(jnp.logical_not(self.inner))
+            def _():
+                self.copy(2, chunk).wait_recv()
+
+        else:
+
+            @pl.when(self.inner)
+            def _():
+                self.copy(tick - 1, chunk).wait_recv()
+                arrived = self.incoming[(tick - 1) * self.streams + stream, at].astype(f32)
+                if tick == 1:
+                    self.outgoing[stream, at] = (self.total[stream, at] + arrived).astype(bf16)
+                else:
+                    self.whole[stream, at] = (self.outgoing[stream, at].astype(f32) + arrived).astype(bf16)
+                self.copy(tick, chunk).start()
+
+    @property
+    def ticks(self):
+        return self.chunks + 3
+
+    def tick(self, tick):
+        for chunk in range(self.chunks):
+            if tick == 0:
+                self.act(chunk, 0)
+            elif 1 <= tick - chunk <= 3:
+                self.act(chunk, tick - chunk)
+
+    def end(self):
+        for chunk in range(self.chunks):
+
+            @pl.when(self.inner)
+            def _():
+                self.copy(1, chunk).wait_send()
+                self.copy(2, chunk).wait_send()
+
+            @pl.when(jnp.logical_not(self.inner))
+            def _():
+                self.copy(0, chunk).wait_send()
+
+
+def make_spread(count, scratch, first=0):
+    return (Chain if count == CHAIN else Spread)(count, scratch, first)
+
+
+def rep_masks(count):
+    return [1, 3] if count == CHAIN else bits_below(count)
+
+
 def padded(rows, count):
     return -(-rows // (16 * count)) * 16 * count
 
 
-def spread_scratch(rows, width, count):
+def spread_scratch(rows, width, count, streams=2):
     rows = padded(rows, count)
     stages = count.bit_length() - 1
     return [
-        pltpu.VMEM((2, rows, width), f32),
-        pltpu.VMEM((2, rows, width), bf16),
-        pltpu.VMEM((2, rows, width), bf16),
-        pltpu.VMEM((2, rows, width), bf16),
-        pltpu.SemaphoreType.DMA((2,)),
-        pltpu.SemaphoreType.DMA((4, 2, stages)),
+        pltpu.VMEM((streams, rows, width), f32),
+        pltpu.VMEM((streams, rows, width), bf16),
+        pltpu.VMEM((2 * streams if count == CHAIN else streams, rows, width), bf16),
+        pltpu.VMEM((streams, rows, width), bf16),
+        pltpu.SemaphoreType.DMA((streams,)),
+        pltpu.SemaphoreType.DMA((6, streams * PIECES) if count == CHAIN else (4, streams, stages)),
     ]
 
 
@@ -430,28 +551,29 @@
     return (lanes >= head * HEAD) & (lanes < (head + 1) * HEAD)
 
 
-def attend_forward_kernel(n, seqs, layer, orders, x_ref, small_ref, mask_ref, qkv_ref, out_ref, *refs):
-    count = len(orders)
-    shards, refs = refs[:count], refs[count:]
+def attend_forward_kernel(n, seqs, layer, counts, parts, x_ref, small_ref, mask_ref, *refs):
+    first, given, taken = counts
+    sources, shards, refs = refs[:given], refs[given : given + taken], refs[given + taken :]
+    count = len(parts)
     q_ref, k_ref, v_ref, ctx_ref, lse_ref, mid_ref, low_ref, n1_ref, r1_ref = refs[:9]
     wholes, refs = refs[9 : 9 + count], refs[9 + count :]
     base, w_qkv, w_out, acc, sems = refs[:5]
-    gathers = make_gathers(n, layer, shards, wholes, orders, refs[5:])
+    gathers = make_gathers(layer, parts, shards, wholes, refs[5:])
     step, steps = pl.program_id(0), pl.num_programs(0)
     rows, width = x_ref.shape
     seq = rows // seqs
     heads = GROUP // HEAD
-    qkv_copy = pltpu.make_async_copy(qkv_ref, w_qkv, sems.at[0])
-    out_copy = pltpu.make_async_copy(out_ref, w_out, sems.at[1])
+    copies = sum(both_copies(sources, first, (w_qkv, w_out), sems), [])
 
     @pl.when(step == 0)
     def _():
-        qkv_copy.start()
-        out_copy.start()
+        for copy in copies:
+            copy.start()
         begin_all(n, gathers)
         base[...] = x_ref[...].astype(bf16)
-        qkv_copy.wait()
-        out_copy.wait()
+        acc[...] = x_ref[...].astype(f32) + small_ref[2:3, :]
+        for copy in copies:
+            copy.wait()
 
     columns = pl.multiple_of(step * GROUP, GROUP)
     q_bias = small_ref[0:1, pl.ds(columns, GROUP)]
@@ -496,44 +618,38 @@
 
     def mix(block, carry):
         at = pl.ds(pl.multiple_of(block * ROWS, ROWS), ROWS)
-        term = dot_nn(ctx_ref[at, :], w_out[pl.ds(columns, GROUP), :])
-
-        @pl.when(step == 0)
-        def _():
-            acc[at, :] = term
-
-        @pl.when(step > 0)
-        def _():
-            acc[at, :] += term
-
-        @pl.when(step == steps - 1)
-        def _():
-            total = x_ref[at, :].astype(f32) + acc[at, :] + small_ref[2:3, :]
-            mid, normed, scaling = norm_forward(total, small_ref[6:7, :], small_ref[4:5, :])
+        acc[at, :] += dot_nn(ctx_ref[at, :], w_out[pl.ds(columns, GROUP), :])
+        return carry
+
+    lax.fori_loop(0, rows // ROWS, mix, 0)
+
+    @pl.when(step == steps - 1)
+    def _():
+        def finish(block, carry):
+            at = pl.ds(pl.multiple_of(block * ROWS, ROWS), ROWS)
+            mid, normed, scaling = norm_forward(acc[at, :], small_ref[6:7, :], small_ref[4:5, :])
             mid_ref[at, :] = mid
             low_ref[at, :] = mid.astype(bf16)
             n1_ref[at, :] = normed.astype(bf16)
             r1_ref[at, :] = scaling
-
-        return carry
-
-    lax.fori_loop(0, rows // ROWS, mix, 0)
-
-    @pl.when(step == steps - 1)
-    def _():
-        for round_at in range(1, len(orders[0])):
+            return carry
+
+        lax.fori_loop(0, rows // ROWS, finish, 0)
+        for round_at in range(1, len(gathers[0].order)):
             onward_all(gathers, round_at)
         end_all(gathers)
 
 
-def attend_forward(n, x, small, key_mask, w_qkv, w_out, seqs, layer, shards, orders, collective_id):
+def attend_forward(n, x, small, key_mask, w_qkv, w_out, seqs, layer, shards, parts, collective_id):
     rows, width = x.shape
     steps = width // GROUP
     seq = rows // seqs
     wide = jax.ShapeDtypeStruct((rows, width), bf16)
     heads = GROUP // HEAD
     return pl.pallas_call(
-        functools.partial(attend_forward_kernel, n, seqs, layer, orders),
+        functools.partial(
+            attend_forward_kernel, n, seqs, layer, (len(w_qkv), len(w_qkv) + len(w_out), len(shards)), parts
+        ),
         out_shape=(
             wide,
             wide,
@@ -545,11 +661,12 @@
             wide,
             jax.ShapeDtypeStruct((rows, 1), f32),
         )
-        + tuple(whole_of(n, shard) for shard in shards),
+        + wholes_of(n, shards, parts),
         grid_spec=pltpu.PrefetchScalarGridSpec(
             num_scalar_prefetch=0,
             grid=(steps,),
-            in_specs=[whole((rows, width)), whole(small.shape), whole((rows, 1))] + [ANY] * (2 + len(shards)),
+            in_specs=[whole((rows, width)), whole(small.shape), whole((rows, 1))]
+            + [ANY] * (len(w_qkv) + len(w_out) + len(shards)),
             out_specs=[column_block(rows, GROUP)] * 4
             + [
                 pl.BlockSpec((1, seqs * heads, seq), lambda j, *_: (j, 0, 0)),
@@ -558,15 +675,15 @@
                 whole((rows, width)),
                 whole((rows, 1)),
             ]
-            + [ANY] * len(shards),
+            + [ANY] * len(parts),
             scratch_shapes=[
                 pltpu.VMEM((rows, width), bf16),
                 pltpu.VMEM((width, 3 * width), bf16),
                 pltpu.VMEM((width, width), bf16),
                 pltpu.VMEM((rows, width), f32),
-                pltpu.SemaphoreType.DMA((2,)),
+                pltpu.SemaphoreType.DMA((len(w_qkv) + len(w_out),)),
             ]
-            + gather_sems(n, len(shards)),
+            + gather_sems(n, len(parts)),
         ),
         compiler_params=pltpu.CompilerParams(
             dimension_semantics=("arbitrary",),
@@ -576,43 +693,40 @@
         ),
         cost_estimate=cost(8 * rows * width * width + 16 * rows * seq * width, 20 * rows * width),
         name="attend_forward",
-    )(x, small, key_mask, w_qkv, w_out, *shards)
-
-
-def ffn_forward_kernel(n, last, layer, orders, mid_ref, low_ref, small_ref, up_bias_ref, valid_ref, up_ref, down_ref, *refs):
-    count = len(orders)
-    shards, refs = refs[:count], refs[count:]
+    )(x, small, key_mask, *w_qkv, *w_out, *shards)
+
+
+def ffn_forward_kernel(n, last, layer, counts, parts, mid_ref, low_ref, small_ref, up_bias_ref, valid_ref, *refs):
+    first, given, taken = counts
+    sources, shards, refs = refs[:given], refs[given : given + taken], refs[given + taken :]
+    count = len(parts)
     act_ref, slope_ref, n2_ref, r2_ref, hid_ref = refs[:5]
     refs = refs[5:]
     if not last:
         hid_low_ref, refs = refs[0], refs[1:]
     wholes, refs = refs[:count], refs[count:]
     w_up, w_down, acc, sems = refs[:4]
-    gathers = make_gathers(n, layer, shards, wholes, orders, refs[4:]) if count else []
+    gathers = make_gathers(layer, parts, shards, wholes, refs[4:]) if count else []
     step, steps = pl.program_id(0), pl.num_programs(0)
     rows, width = mid_ref.shape
     chunk = act_ref.shape[1]
-    up_copy = pltpu.make_async_copy(up_ref, w_up, sems.at[0])
-    down_copy = pltpu.make_async_copy(down_ref, w_down, sems.at[1])
+    copies = sum(both_copies(sources, first, (w_up, w_down), sems), [])
 
     @pl.when(step == 0)
     def _():
-        up_copy.start()
-        down_copy.start()
+        for copy in copies:
+            copy.start()
         if gathers:
             begin_all(n, gathers)
-        up_copy.wait()
-        down_copy.wait()
+        acc[...] = mid_ref[...] + small_ref[3:4, :]
+        for copy in copies:
+            copy.wait()
 
     if gathers:
 
-        @pl.when(step == 1)
+        @pl.when(step == 2)
         def _():
             onward_all(gathers, 0)
-
-        @pl.when(step == 3)
-        def _():
-            onward_all(gathers, 1)
 
     columns = pl.multiple_of(step * chunk, chunk)
     tile = 256
@@ -620,28 +734,27 @@
     def block_step(block, carry):
         at = pl.ds(pl.multiple_of(block * ROWS, ROWS), ROWS)
         low = low_ref[at, :]
+        acts = []
         for part in range(chunk // tile):
             inside = slice(part * tile, (part + 1) * tile)
             at_units = pl.ds(pl.multiple_of(columns + part * tile, tile), tile)
             pre = dot_nn(low, w_up[:, at_units]) + up_bias_ref[:, inside]
             share = 0.5 * (1.0 + lax.erf(pre * root_half))
-            act_ref[at, inside] = (pre * share).astype(bf16)
+            act = (pre * share).astype(bf16)
+            act_ref[at, inside] = act
+            acts.append(act)
             density = inv_root_tau * jnp.exp(-0.5 * pre * pre)
             slope_ref[at, inside] = (share + pre * density).astype(bf16)
-        term = dot_nn(act_ref[at, :], w_down[pl.ds(columns, chunk), :])
-
-        @pl.when(step == 0)
-        def _():
-            acc[at, :] = term
-
-        @pl.when(step > 0)
-        def _():
-            acc[at, :] += term
-
-        @pl.when(step == steps - 1)
-        def _():
-            total = mid_ref[at, :] + acc[at, :] + small_ref[3:4, :]
-            hidden, normed, scaling = norm_forward(total, small_ref[7:8, :], small_ref[5:6, :])
+        acc[at, :] += dot_nn(jnp.concatenate(acts, axis=1), w_down[pl.ds(columns, chunk), :])
+        return carry
+
+    lax.fori_loop(0, rows // ROWS, block_step, 0)
+
+    @pl.when(step == steps - 1)
+    def _():
+        def finish(block, carry):
+            at = pl.ds(pl.multiple_of(block * ROWS, ROWS), ROWS)
+            hidden, normed, scaling = norm_forward(acc[at, :], small_ref[7:8, :], small_ref[5:6, :])
             n2_ref[at, :] = normed.astype(bf16)
             r2_ref[at, :] = scaling
             if last:
@@ -649,21 +762,20 @@
             else:
                 hid_ref[at, :] = hidden
                 hid_low_ref[at, :] = hidden.astype(bf16)
-
-        return carry
-
-    lax.fori_loop(0, rows // ROWS, block_step, 0)
+            return carry
+
+        lax.fori_loop(0, rows // ROWS, finish, 0)
 
     if gathers:
 
         @pl.when(step == steps - 1)
         def _():
-            for round_at in range(2, len(orders[0])):
+            for round_at in range(1, len(gathers[0].order)):
                 onward_all(gathers, round_at)
             end_all(gathers)
 
 
-def ffn_forward(n, mid, low, small, up_bias, valid, w_up, w_down, last, layer, shards, orders, collective_id):
+def ffn_forward(n, mid, low, small, up_bias, valid, w_up, w_down, last, layer, shards, parts, collective_id):
     rows, width = mid.shape
     units = up_bias.shape[1]
     chunk = width
@@ -683,9 +795,9 @@
     if not last:
         out_shape.append(jax.ShapeDtypeStruct((rows, width), bf16))
         out_specs.append(whole((rows, width)))
-    out_shape += [whole_of(n, shard) for shard in shards]
-    out_specs += [ANY] * len(shards)
-    if shards:
+    out_shape += wholes_of(n, shards, parts)
+    out_specs += [ANY] * len(parts)
+    if parts:
         params = pltpu.CompilerParams(
             dimension_semantics=("arbitrary",),
             vmem_limit_bytes=VMEM_BYTES,
@@ -695,7 +807,9 @@
     else:
         params = pltpu.CompilerParams(dimension_semantics=("arbitrary",), vmem_limit_bytes=VMEM_BYTES)
     return pl.pallas_call(
-        functools.partial(ffn_forward_kernel, n, last, layer, orders),
+        functools.partial(
+            ffn_forward_kernel, n, last, layer, (len(w_up), len(w_up) + len(w_down), len(shards)), parts
+        ),
         out_shape=tuple(out_shape),
         grid_spec=pltpu.PrefetchScalarGridSpec(
             num_scalar_prefetch=0,
@@ -707,20 +821,20 @@
                 column_block(1, chunk),
                 whole((rows, 1)),
             ]
-            + [ANY] * (2 + len(shards)),
+            + [ANY] * (len(w_up) + len(w_down) + len(shards)),
             out_specs=out_specs,
             scratch_shapes=[
                 pltpu.VMEM((width, units), bf16),
                 pltpu.VMEM((units, width), bf16),
                 pltpu.VMEM((rows, width), f32),
-                pltpu.SemaphoreType.DMA((2,)),
+                pltpu.SemaphoreType.DMA((len(w_up) + len(w_down),)),
             ]
-            + (gather_sems(n, len(shards)) if shards else []),
+            + (gather_sems(n, len(parts)) if parts else []),
         ),
         compiler_params=params,
         cost_estimate=cost(8 * rows * width * units, 8 * rows * units),
         name="ffn_forward",
-    )(mid, low, small, up_bias, valid, w_up, w_down, *shards)
+    )(mid, low, small, up_bias, valid, *w_up, *w_down, *shards)
 
 
 def shard_copies(n, me, source_of, keep_of, send_of, sems):
@@ -742,60 +856,52 @@
     return each
 
 
-def ffn_backward_kernel(n, reps, carry, g_ref, valid_ref, n2_ref, r2_ref, low_ref, n1_ref, r1_ref, small_ref, act_ref, slope_ref, *refs):
-    up_ref, down_ref, refs = refs[0], refs[1], refs[2:]
+def ffn_backward_kernel(n, reps, counts, carry, g_ref, valid_ref, n2_ref, r2_ref, low_ref, n1_ref, r1_ref, small_ref, act_ref, slope_ref, *refs):
+    sources, refs = refs[: counts[1]], refs[counts[1] :]
     if carry:
         halves, spread_from, refs = refs[:4], refs[4], refs[5:]
     gs1_ref, ga1_ref, sums_ref, up_sum_ref, down_keep, down_send, up_keep, up_send = refs[:8]
     refs = refs[8:]
     if carry:
         reduced_ref, spread_ref, refs = refs[0], refs[1], refs[2:]
-    w_up, w_down, gs2, gffn, gpre, acc, low_turned, d_down, d_up, sems, out_sems = refs[:11]
+    w_up, w_down, gffn, gpre, acc, low_turned, d_down, d_up, sems, out_sems = refs[:10]
     if carry:
         hops = len(bits_below(n, 2))
-        reduce = Reduce(halves, refs[11 : 16 + hops], bits_below(n, 2))
-        spread = Spread(reps, refs[16 + hops : 22 + hops])
-        spread_sem = refs[22 + hops]
+        reduce = Reduce(halves, refs[10 : 15 + hops], bits_below(n, 2))
+        spread = make_spread(reps, refs[15 + hops : 21 + hops])
+        spread_sem = refs[21 + hops]
     step, steps = pl.program_id(0), pl.num_programs(0)
     me = lax.axis_index("fsdp")
-    rows, width = gs2.shape
+    rows, width = acc.shape
     last_step = steps - 1
     if carry:
         out_copy = pltpu.make_async_copy(spread.whole, spread_ref, spread_sem)
 
         @pl.when(step == 0)
         def _():
-            greet_both(n, reps, bits_below(n), bits_below(reps))
+            greet_both(n, reps, bits_below(n), rep_masks(reps))
+            spread.begin(spread_from)
             reduce.begin()
-            for stream in range(2):
-                spread.load(stream, spread_from).start()
-            for stream in range(2):
-                spread.load(stream, spread_from).wait()
-            spread.tick(0)
+            spread.loaded(spread_from)
 
         @pl.when(step == 1)
         def _():
-            reduce.hop(0)
             spread.tick(1)
 
         @pl.when(step == 2)
         def _():
-            spread.tick(3)
+            spread.tick(2)
             for hop in range(1, hops):
                 reduce.hop(hop)
 
         @pl.when(step == 3)
         def _():
-            for tick in range(5, spread.ticks):
-                spread.tick(tick)
-            out_copy.start()
             reduce.finish(reduced_ref)
     chunk = act_ref.shape[1]
     per_down = down_keep.shape[1]
     per_up = up_keep.shape[2]
     tile = 256
-    up_copies = [pltpu.make_async_copy(up_ref, w_up, sems.at[0])]
-    down_copies = [pltpu.make_async_copy(down_ref, w_down, sems.at[1])]
+    up_copies, down_copies = both_copies(sources, counts[0], (w_up, w_down), sems)
 
     @pl.when(step == 0)
     def _():
@@ -810,7 +916,7 @@
             grad = g_ref[at, :].astype(f32) * valid_ref[at, :]
             normed = n2_ref[at, :].astype(f32)
             summed = norm_backward(grad, normed, r2_ref[at, :], small_ref[7:8, :])
-            gs2[at, :] = summed
+            acc[at, :] = summed
             low = summed.astype(bf16)
             gffn[at, :] = low
             sums_ref[0:1, :] += jnp.sum(grad * normed, axis=0, keepdims=True)
@@ -831,35 +937,34 @@
     def through(block, carry):
         at = pl.ds(pl.multiple_of(block * ROWS, ROWS), ROWS)
         grad = gffn[at, :]
+        lows = []
         for part in range(chunk // tile):
             inside = slice(part * tile, (part + 1) * tile)
             at_units = pl.ds(pl.multiple_of(columns + part * tile, tile), tile)
             grad_act = dot_nt(grad, w_down[at_units, :])
             low = (grad_act * slope_ref[at, inside].astype(f32)).astype(bf16)
             gpre[at, inside] = low
+            lows.append(low)
             up_sum_ref[:, inside] += jnp.sum(low.astype(f32), axis=0, keepdims=True)
-        term = dot_nt(gpre[at, :], w_up[:, pl.ds(columns, chunk)])
+        acc[at, :] += dot_nt(jnp.concatenate(lows, axis=1), w_up[:, pl.ds(columns, chunk)])
+        return carry
+
+    lax.fori_loop(0, rows // ROWS, through, 0)
+    if carry:
 
         @pl.when(step == 0)
         def _():
-            acc[at, :] = term
-
-        @pl.when(step > 0)
-        def _():
-            acc[at, :] += term
-
-        return carry
-
-    lax.fori_loop(0, rows // ROWS, through, 0)
-    if carry:
-
-        @pl.when(step == 1)
-        def _():
-            spread.tick(2)
+            reduce.hop(0)
 
         @pl.when(step == 2)
         def _():
-            spread.tick(4)
+            spread.tick(3)
+
+        @pl.when(step == 3)
+        def _():
+            for tick in range(4, spread.ticks):
+                spread.tick(tick)
+            out_copy.start()
 
     def down_out(which):
         def run(start):
@@ -920,7 +1025,7 @@
     def _():
         def finish(block, carry):
             at = pl.ds(pl.multiple_of(block * ROWS, ROWS), ROWS)
-            grad = gs2[at, :] + acc[at, :]
+            grad = acc[at, :]
             normed = n1_ref[at, :].astype(f32)
             summed = norm_backward(grad, normed, r1_ref[at, :], small_ref[6:7, :])
             gs1_ref[at, :] = summed
@@ -961,15 +1066,15 @@
         spread_rows = carry[4].shape[1]
         extra_out = [
             jax.ShapeDtypeStruct(reduced, f32),
-            jax.ShapeDtypeStruct((2, padded(spread_rows, reps), width), bf16),
+            jax.ShapeDtypeStruct((1, padded(spread_rows, reps), width), bf16),
         ]
         extra_specs = [whole(reduced), ANY]
         extra_scratch = reduce_scratch(chips, carry[0].shape[1], width, hops)
-        extra_scratch += spread_scratch(spread_rows, width, reps) + [pltpu.SemaphoreType.DMA]
+        extra_scratch += spread_scratch(spread_rows, width, reps, 1) + [pltpu.SemaphoreType.DMA]
     down_half = jax.ShapeDtypeStruct((chips, units // n, width), bf16)
     up_half = jax.ShapeDtypeStruct((chips, steps, width // n, chunk), bf16)
     return pl.pallas_call(
-        functools.partial(ffn_backward_kernel, n, reps, bool(carry)),
+        functools.partial(ffn_backward_kernel, n, reps, (len(w_up), len(w_up) + len(w_down)), bool(carry)),
         out_shape=(
             jax.ShapeDtypeStruct((rows, width), f32),
             jax.ShapeDtypeStruct((rows, width), bf16),
@@ -996,7 +1101,7 @@
                 column_block(rows, chunk),
                 column_block(rows, chunk),
             ]
-            + [ANY] * (2 + len(carry)),
+            + [ANY] * (len(w_up) + len(w_down) + len(carry)),
             out_specs=[
                 whole((rows, width)),
                 whole((rows, width)),
@@ -1008,14 +1113,13 @@
             scratch_shapes=[
                 pltpu.VMEM((width, units), bf16),
                 pltpu.VMEM((units, width), bf16),
-                pltpu.VMEM((rows, width), f32),
                 pltpu.VMEM((rows, width), bf16),
                 pltpu.VMEM((rows, chunk), bf16),
                 pltpu.VMEM((rows, width), f32),
                 pltpu.VMEM((width, rows), bf16),
                 pltpu.VMEM((chunk, width), bf16),
                 pltpu.VMEM((width, chunk), bf16),
-                pltpu.SemaphoreType.DMA((2,)),
+                pltpu.SemaphoreType.DMA((len(w_up) + len(w_down),)),
                 pltpu.SemaphoreType.DMA((2, n)),
             ]
             + extra_scratch,
@@ -1025,53 +1129,66 @@
         else pltpu.CompilerParams(dimension_semantics=("arbitrary",), vmem_limit_bytes=VMEM_BYTES),
         cost_estimate=cost(10 * rows * width * units, 8 * rows * units),
         name="ffn_backward",
-    )(grad, valid, n2, r2, low, n1, r1, small, act, slope, w_up, w_down, *carry)
-
-
-def attend_backward_kernel(n, reps, seqs, spreads, ga_ref, gs_ref, base_ref, mask_ref, q_ref, k_ref, v_ref, ctx_ref, lse_ref, *refs):
-    qkv_ref, out_ref, halves, refs = refs[0], refs[1], refs[2:6], refs[6:]
+    )(grad, valid, n2, r2, low, n1, r1, small, act, slope, *w_up, *w_down, *carry)
+
+
+def attend_backward_kernel(n, reps, seqs, counts, spreads, ga_ref, gs_ref, base_ref, mask_ref, q_ref, k_ref, v_ref, ctx_ref, lse_ref, *refs):
+    sources, refs = refs[: counts[1]], refs[counts[1] :]
+    halves, refs = refs[:4], refs[4:]
     if spreads:
-        spread_from, refs = refs[0], refs[1:]
+        spread_from, refs = refs[:2], refs[2:]
     gh_ref, sums_ref, a_keep, b_keep, a_send, b_send, reduced_ref = refs[:7]
     refs = refs[7:]
     if spreads:
-        spread_ref, refs = refs[0], refs[1:]
+        spread_refs, refs = refs[:2], refs[2:]
     w_qkv, w_out, acc, base_turned, gctx, gproj, d_qkv, d_out, p_all, ds_all, sems, out_sems = refs[:12]
     hops = len(bits_below(n, 2))
     reduce = Reduce(halves, refs[12 : 17 + hops], bits_below(n, 2))
     step, steps = pl.program_id(0), pl.num_programs(0)
     me = lax.axis_index("fsdp")
     if spreads:
-        spread = Spread(reps, refs[17 + hops : 23 + hops])
-        spread_copy = pltpu.make_async_copy(spread.whole, spread_ref, refs[23 + hops])
+        rest = refs[17 + hops :]
+        spread_list = [make_spread(reps, rest[:6]), make_spread(reps, rest[6:12], 1)]
+        spread_copies = [
+            pltpu.make_async_copy(spread.whole, ref, rest[12].at[at])
+            for at, (spread, ref) in enumerate(zip(spread_list, spread_refs))
+        ]
+
+    def spread_tick(tick):
+        if spreads:
+            for spread, copy in zip(spread_list, spread_copies):
+                if tick < spread.ticks:
+                    spread.tick(tick)
+                if tick == spread.ticks - 1:
+                    copy.start()
 
     @pl.when(step == 0)
     def _():
-        greet_both(n, reps, bits_below(n), bits_below(reps) if spreads else [])
+        greet_both(n, reps, bits_below(n), rep_masks(reps) if spreads else [])
+        if spreads:
+            for spread, source in zip(spread_list, spread_from):
+                spread.begin(source)
         reduce.begin()
         if spreads:
-            for stream in range(2):
-                spread.load(stream, spread_from).start()
-            for stream in range(2):
-                spread.load(stream, spread_from).wait()
-            spread.tick(0)
+            for spread, source in zip(spread_list, spread_from):
+                spread.loaded(source)
 
     if spreads:
 
         @pl.when(step == 1)
         def _():
-            spread.tick(2)
+            spread_tick(2)
 
         @pl.when(step == 2)
         def _():
-            spread.tick(4)
+            spread_tick(4)
+
     rows, width = ga_ref.shape
     seq = rows // seqs
     heads = GROUP // HEAD
     per = width // n
     tile = 256
-    qkv_copies = [pltpu.make_async_copy(qkv_ref, w_qkv, sems.at[0])]
-    out_copies = [pltpu.make_async_copy(out_ref, w_out, sems.at[1])]
+    qkv_copies, out_copies = both_copies(sources, counts[0], (w_qkv, w_out), sems)
 
     @pl.when(step == 0)
     def _():
@@ -1082,6 +1199,7 @@
 
         def turn(block, carry):
             at = pl.ds(pl.multiple_of(block * ROWS, ROWS), ROWS)
+            acc[at, :] = gs_ref[at, :]
             base_turned[:, at] = base_ref[at, :].T
             return carry
 
@@ -1139,20 +1257,18 @@
     @pl.when(step == 0)
     def _():
         reduce.hop(0)
-        if spreads:
-            spread.tick(1)
-
-    @pl.when(step == 1)
-    def _():
-        if spreads:
-            spread.tick(3)
-
-    @pl.when(step == 2)
-    def _():
-        if spreads:
-            for tick in range(5, spread.ticks):
-                spread.tick(tick)
-            spread_copy.start()
+        spread_tick(1)
+
+    if spreads:
+
+        @pl.when(step == 1)
+        def _():
+            spread_tick(3)
+
+        @pl.when(step == 2)
+        def _():
+            for tick in range(5, spread_list[0].ticks):
+                spread_tick(tick)
 
     def onward(block, carry):
         at = pl.ds(pl.multiple_of(block * ROWS, ROWS), ROWS)
@@ -1161,22 +1277,14 @@
         term += dot_nt(gproj[at, 2 * GROUP : 3 * GROUP], w_qkv[:, pl.ds(pl.multiple_of(2 * width + columns, GROUP), GROUP)])
         sums_ref[0:1, :] += jnp.sum(gproj[at, 0:GROUP].astype(f32), axis=0, keepdims=True)
         sums_ref[1:2, :] += jnp.sum(gproj[at, 2 * GROUP : 3 * GROUP].astype(f32), axis=0, keepdims=True)
-
-        @pl.when(step == 0)
-        def _():
-            acc[at, :] = gs_ref[at, :] + term
-
-        @pl.when(step > 0)
-        def _():
-            acc[at, :] += term
-
-        @pl.when(step == steps - 1)
-        def _():
-            gh_ref[at, :] = acc[at, :].astype(gh_ref.dtype)
-
+        acc[at, :] += term
         return carry
 
     lax.fori_loop(0, rows // ROWS, onward, 0)
+
+    @pl.when(step == steps - 1)
+    def _():
+        gh_ref[...] = acc[...].astype(gh_ref.dtype)
 
     def place_of(part, a_half, b_half):
         return a_half if part < 2 else b_half
@@ -1223,8 +1331,9 @@
         out_copy(False)
         reduce.finish(reduced_ref)
         if spreads:
-            spread_copy.wait()
-            spread.end()
+            for spread, copy in zip(spread_list, spread_copies):
+                copy.wait()
+                spread.end()
 
 
 def attend_backward(n, reps, ga, gs, base, key_mask, q, k, v, ctx, lse, w_qkv, w_out, seqs, out_type, carry, collective_id):
@@ -1239,12 +1348,15 @@
     extra_out, extra_specs = [], []
     extra_scratch = reduce_scratch(chips, carry[0].shape[1], width, hops)
     if len(carry) > 4:
-        spread_rows = carry[4].shape[1]
-        extra_out = [jax.ShapeDtypeStruct((2, padded(spread_rows, reps), width), bf16)]
-        extra_specs = [ANY]
-        extra_scratch += spread_scratch(spread_rows, width, reps) + [pltpu.SemaphoreType.DMA]
+        for source, streams in zip(carry[4:], (2, 1)):
+            extra_out.append(jax.ShapeDtypeStruct((streams, padded(source.shape[1], reps), width), bf16))
+            extra_specs.append(ANY)
+            extra_scratch += spread_scratch(source.shape[1], width, reps, streams)
+        extra_scratch.append(pltpu.SemaphoreType.DMA((2,)))
     return pl.pallas_call(
-        functools.partial(attend_backward_kernel, n, reps, seqs, len(carry) > 4),
+        functools.partial(
+            attend_backward_kernel, n, reps, seqs, (len(w_qkv), len(w_qkv) + len(w_out)), len(carry) > 4
+        ),
         out_shape=(
             jax.ShapeDtypeStruct((rows, width), out_type),
             jax.ShapeDtypeStruct((8, width), f32),
@@ -1262,7 +1374,7 @@
             + [whole((rows, 1))]
             + [column_block(rows, GROUP)] * 4
             + [pl.BlockSpec((1, seqs * heads, seq), lambda j, *_: (j, 0, 0))]
-            + [ANY] * (2 + len(carry)),
+            + [ANY] * (len(w_qkv) + len(w_out) + len(carry)),
             out_specs=[whole((rows, width)), column_block(8, GROUP)] + [ANY] * 4 + [whole(reduced)] + extra_specs,
             scratch_shapes=[
                 pltpu.VMEM((width, 3 * width), bf16),
@@ -1275,7 +1387,7 @@
                 pltpu.VMEM((width, width), bf16),
                 pltpu.VMEM((seq, heads * seq), bf16),
                 pltpu.VMEM((seq, heads * seq), bf16),
-                pltpu.SemaphoreType.DMA((2,)),
+                pltpu.SemaphoreType.DMA((len(w_qkv) + len(w_out),)),
                 pltpu.SemaphoreType.DMA((4, n)),
             ]
             + extra_scratch,
@@ -1283,19 +1395,21 @@
         compiler_params=remote_params(collective_id),
         cost_estimate=cost(16 * rows * width * width + 40 * rows * seq * width, 20 * rows * width),
         name="attend_backward",
-    )(ga, gs, base, key_mask, q, k, v, ctx, lse, w_qkv, w_out, *carry)
+    )(ga, gs, base, key_mask, q, k, v, ctx, lse, *w_qkv, *w_out, *carry)
 
 
 def cost(flops, moved):
     return pl.CostEstimate(flops=int(flops), bytes_accessed=int(moved), transcendentals=0)
 
 
-def last_sums_kernel(n, reps, a_keep, b_keep, a_send, b_send, spread_from, small_ref, spread_ref, attend_ref, total_ref, *scratch):
+def last_sums_kernel(n, reps, a_keep, b_keep, a_send, b_send, spread_from, *refs):
+    sums, refs = refs[: 3 * LAYERS], refs[3 * LAYERS :]
+    spread_ref, attend_ref, total_ref, *scratch = refs
     bits, rep_bits = bits_below(n, 2), bits_below(reps)
     hops = len(bits)
     reduce = Reduce((a_keep, b_keep, a_send, b_send), scratch[: 5 + hops], bits)
-    first = Spread(reps, scratch[5 + hops : 11 + hops])
-    second = Spread(reps, scratch[11 + hops : 17 + hops])
+    first = make_spread(reps, scratch[5 + hops : 11 + hops])
+    second = make_spread(reps, scratch[11 + hops : 17 + hops])
     reduced, small_out, small_in, small_sems, sems = scratch[17 + hops :]
     axes = [("fsdp", bit) for bit in bits_below(n)] + [("rep", bit) for bit in rep_bits]
 
@@ -1318,38 +1432,45 @@
         else:
             total_ref[...] = small_out[at] + small_in[at]
 
-    greet_both(n, reps, bits_below(n), rep_bits)
+    greet_both(n, reps, bits_below(n), sorted({*rep_bits, *rep_masks(reps)}))
+    first.begin(spread_from)
+    width = small_out.shape[2]
+    small_out[0] = jnp.zeros(small_out.shape[1:], f32)
+    for layer in range(LAYERS):
+        ffn_sums, proj_sums, up_sums = sums[3 * layer : 3 * layer + 3]
+        small_out[0, 16 * layer : 16 * layer + 6] = ffn_sums[0:6]
+        small_out[0, 16 * layer + 6 : 16 * layer + 8] = proj_sums[0:2]
+        for at in range(up_sums.shape[1] // width):
+            small_out[0, 16 * layer + 8 + at : 16 * layer + 9 + at] = up_sums[:, at * width : (at + 1) * width]
+    small_copy(0).start()
     reduce.begin()
-    for stream in range(2):
-        first.load(stream, spread_from).start()
-    small_out[0] = small_ref[...]
-    small_copy(0).start()
-    for stream in range(2):
-        first.load(stream, spread_from).wait()
-    first.tick(0)
+    first.loaded(spread_from)
+    small_step(0)
     reduce.hop(0)
-    small_step(0)
+    small_step(1)
     first.tick(1)
-    small_step(1)
     first.tick(2)
     for hop in range(1, hops):
         reduce.hop(hop)
-    small_step(2)
+    for at in range(2, len(bits) + 1):
+        small_step(at)
     first.tick(3)
     reduce.finish(reduced)
     rows = reduced.shape[1]
     for stream in range(2):
         second.total[stream, pl.ds(0, rows)] = reduced[stream]
     second.tick(0)
-    for at in range(3, len(axes)):
-        small_step(at)
     for tick in range(4, first.ticks):
         first.tick(tick)
         second.tick(tick - 3)
+        if len(bits) + tick - 3 < len(axes):
+            small_step(len(bits) + tick - 3)
     first_copy = pltpu.make_async_copy(first.whole, spread_ref, sems.at[0])
     first_copy.start()
     for tick in range(first.ticks - 3, second.ticks):
         second.tick(tick)
+    for at in range(len(bits) + max(first.ticks - 3, 1), len(axes)):
+        small_step(at)
     second_copy = pltpu.make_async_copy(second.whole, attend_ref, sems.at[1])
     second_copy.start()
     first.end()
@@ -1360,7 +1481,7 @@
     second_copy.wait()
 
 
-def last_sums(n, reps, halves, spread_rows, small, collective_id):
+def last_sums(n, reps, halves, spread_rows, sums, collective_id):
     chips, rows, width = halves[0].shape
     hops = len(bits_below(n, 2))
     count = len(bits_below(n)) + len(bits_below(reps))
@@ -1370,17 +1491,17 @@
         out_shape=(
             jax.ShapeDtypeStruct((2, padded(spread_rows.shape[1], reps), width), bf16),
             jax.ShapeDtypeStruct((2, padded(rows, reps), width), bf16),
-            jax.ShapeDtypeStruct(small.shape, f32),
+            jax.ShapeDtypeStruct((16 * LAYERS, width), f32),
         ),
-        in_specs=[ANY] * 5 + [vmem],
+        in_specs=[ANY] * 5 + [vmem] * len(sums),
         out_specs=(ANY, ANY, vmem),
         scratch_shapes=reduce_scratch(chips, rows, width, hops)
         + spread_scratch(spread_rows.shape[1], width, reps)
         + spread_scratch(rows, width, reps)
         + [
             pltpu.VMEM((2, rows, width), f32),
-            pltpu.VMEM((count, *small.shape), f32),
-            pltpu.VMEM((count, *small.shape), f32),
+            pltpu.VMEM((count, 16 * LAYERS, width), f32),
+            pltpu.VMEM((count, 16 * LAYERS, width), f32),
             pltpu.SemaphoreType.DMA((2, count)),
             pltpu.SemaphoreType.DMA((2,)),
         ],
@@ -1388,22 +1509,7 @@
             vmem_limit_bytes=VMEM_BYTES, collective_id=collective_id, has_side_effects=True
         ),
         name="last_sums",
-    )(*halves, spread_rows, small)
-
-
-def swap(array, axis, count, mask):
-    return lax.ppermute(array, axis, [(i, i ^ mask) for i in range(count)])
-
-
-def gather_small(own, n, me):
-    array = own[None]
-    bit = 1
-    while bit < n:
-        other = swap(array, "fsdp", n, bit)
-        upper = (me // bit) % 2 == 1
-        array = jnp.concatenate([jnp.where(upper, other, array), jnp.where(upper, array, other)], axis=0)
-        bit *= 2
-    return array
+    )(*halves, spread_rows, *sums)
 
 
 def on_device(n, reps, tokens, cotangent, lengths, live_batches, w_qkv, w_out, w_up, w_down, up_bias, biases, norm_gains):
@@ -1420,8 +1526,20 @@
     valid = jnp.where(inside & alive[:, None], 1.0, 0.0).astype(f32).reshape(rows, 1)
     ones = jnp.ones((rows, 1), f32)
 
+    chip_bits = bits_below(n, 2)
+    orders = (tuple(chip_bits + [1]), tuple(chip_bits[::-1] + [1]))
+
+    qkv, out, up, down = ([[] for _ in range(LAYERS)] for _ in range(4))
+    attend_parts = parts_of(0, w_qkv, 2, orders) + parts_of(1, w_out, 2, orders)
+
     own_small = jnp.concatenate([up_bias.reshape(-1), biases.reshape(-1), norm_gains.reshape(-1)])
-    small_all = gather_small(own_small, n, me)
+    small_count = own_small.shape[0]
+    small_rows = -(-small_count // 2048) * 16
+    own_small = jnp.pad(own_small, (0, small_rows * 128 - small_count)).reshape(1, small_rows, 128)
+    small_parts = [(2, 0, 128, orders[0])]
+    gathered = gather_weights(n, 0, (w_qkv, w_out, own_small), small_parts + attend_parts, 0)
+    small_all = gathered[0].reshape(n, small_rows * 128)[:, :small_count]
+    qkv[0], out[0] = gathered[1:3], gathered[3:5]
     cut_a = LAYERS * units // n
     cut_b = cut_a + LAYERS * 6 * per
     up_bias_all = small_all[:, :cut_a].reshape(n, LAYERS, units // n).transpose(1, 0, 2).reshape(LAYERS, 1, units)
@@ -1429,41 +1547,37 @@
     gain_all = small_all[:, cut_b:].reshape(n, LAYERS, 2, per).transpose(1, 2, 0, 3).reshape(LAYERS, 2, width)
     smalls = jnp.concatenate([bias_all, gain_all], axis=1)
 
-    chip_bits = []
-    bit = 2
-    while bit < n:
-        chip_bits.append(bit)
-        bit *= 2
-    upward = tuple(chip_bits + [1])
-    downward = tuple(chip_bits[::-1] + [1])
-
-    attend_orders, ffn_orders = (upward, downward), (downward, upward)
-    qkv, out, up, down = [None] * LAYERS, [None] * LAYERS, [None] * LAYERS, [None] * LAYERS
-    qkv[0], out[0] = gather_weights(n, 0, (w_qkv, w_out), attend_orders, 0)
-
     current = tokens.reshape(rows, width)
     base = current
     saved = []
     for layer in range(LAYERS):
         last = layer == LAYERS - 1
-        q, k, v, ctx, lse, mid, low, n1, r1, up[layer], down[layer] = attend_forward(
+        begun = EARLY if layer else 0
+        parts = parts_of(0, w_up, UP_PARTS, orders, begun) + parts_of(1, w_down, 2, orders)
+        results = attend_forward(
             n, current, smalls[layer], key_mask, qkv[layer], out[layer], seqs,
-            layer, (w_up, w_down), ffn_orders, 1 + 2 * layer,
+            layer, (w_up, w_down), parts, 1 + 2 * layer,
         )
+        q, k, v, ctx, lse, mid, low, n1, r1 = results[:9]
+        up[layer] = [*up[layer], *results[9:-2]]
+        down[layer] = results[-2:]
+        parts = [] if last else attend_parts + parts_of(2, w_up, UP_PARTS, orders)[:EARLY]
         results = ffn_forward(
             n, mid, low, smalls[layer], up_bias_all[layer], valid, up[layer], down[layer], last,
-            layer + 1, () if last else (w_qkv, w_out), () if last else attend_orders, 2 + 2 * layer,
+            layer + 1, () if last else (w_qkv, w_out, w_up), parts, 2 + 2 * layer,
         )
         act, slope, n2, r2, current = results[:5]
         saved.append((base, q, k, v, ctx, lse, low, n1, r1, act, slope, n2, r2))
         if not last:
-            base, qkv[layer + 1], out[layer + 1] = results[5:]
+            base = results[5]
+            qkv[layer + 1], out[layer + 1], up[layer + 1] = results[6:8], results[8:10], list(results[10:])
     outputs = current.reshape(seqs, seq, width)
 
     grad = cotangent.reshape(rows, width)
     grad_valid = valid
-    small_rows = [None] * LAYERS
-    attend_halves, attend_reduced, ffn_done, attend_done = None, None, [None] * LAYERS, [None] * LAYERS
+    sum_rows = [None] * LAYERS
+    attend_halves, attend_reduced = None, None
+    down_done, up_done, attend_done = [None] * LAYERS, [None] * LAYERS, [None] * LAYERS
     ffn_reduced = None
     for layer in range(LAYERS - 1, -1, -1):
         first = layer == LAYERS - 1
@@ -1474,7 +1588,7 @@
         )
         gs1, ga1, sums, up_sum, down_keep, down_send, up_keep, up_send = results[:8]
         if not first:
-            attend_reduced, ffn_done[layer + 1] = results[8:]
+            attend_reduced, down_done[layer + 1] = results[8:]
         ffn_halves = (
             down_keep,
             up_keep.reshape(n // 2, -1, width),
@@ -1483,26 +1597,25 @@
         )
         results = attend_backward(
             n, reps, ga1, gs1, base, key_mask, q, k, v, ctx, lse, qkv[layer], out[layer], seqs,
-            f32 if layer else bf16, ffn_halves + (() if first else (attend_reduced,)), 20 + layer,
+            f32 if layer else bf16, ffn_halves + (() if first else (attend_reduced, ffn_reduced)), 20 + layer,
         )
         grad, proj_sums = results[:2]
         attend_halves, ffn_reduced = results[2:6], results[6]
         if not first:
-            attend_done[layer + 1] = results[7]
+            attend_done[layer + 1], up_done[layer + 1] = results[7:]
         grad_valid = ones
-        small_rows[layer] = jnp.concatenate(
-            [sums[:6], proj_sums[:2], up_sum.reshape(units // width, width), jnp.zeros((8 - units // width, width), f32)]
-        )
+        sum_rows[layer] = (sums, proj_sums, up_sum)
     grad_tokens = grad.reshape(seqs, seq, width)
-    ffn_done[0], attend_done[0], small_total = last_sums(
-        n, reps, attend_halves, ffn_reduced, jnp.concatenate(small_rows), 30
+    ffn_last, attend_done[0], small_total = last_sums(
+        n, reps, attend_halves, ffn_reduced, [array for arrays in sum_rows for array in arrays], 30
     )
+    down_done[0], up_done[0] = ffn_last[:1], ffn_last[1:]
 
     ffn_rows, attend_rows = units // n, 2 * per
-    both_ffn = jnp.stack([done[:, :ffn_rows] for done in ffn_done])
     both_attend = jnp.stack([done[:, :attend_rows] for done in attend_done])
-    grad_down = both_ffn[:, 0].astype(f32)
-    grad_up = both_ffn[:, 1].reshape(LAYERS, units // width, per, width).transpose(0, 2, 1, 3)
+    grad_down = jnp.stack([done[0, :ffn_rows] for done in down_done]).astype(f32)
+    grad_up = jnp.stack([done[0, :ffn_rows] for done in up_done])
+    grad_up = grad_up.reshape(LAYERS, units // width, per, width).transpose(0, 2, 1, 3)
     grad_up = grad_up.reshape(LAYERS, per, units).astype(f32)
     parts = both_attend.reshape(LAYERS, 4, per, width)
     grad_qkv = parts[:, :3].transpose(0, 2, 1, 3).reshape(LAYERS, per, 3 * width).astype(f32)

time: 561 us -> 524 us (0.934); the launches traced: 560 us -> 514 us
  Pallas kernels: 526 us -> 492 us
    pallas_call x9, Pallas kernels: 445 us -> 423 us  [the longest x2 139 us: attend_backward(): pl.pallas_call(functools.partial(attend_backward_kernel, n, reps, seqs, (...]
    pallas_call x1, Pallas kernels: 80.8 us -> 68.8 us  [last_sums(): pl.pallas_call(functools.partial(last_sums_kernel, n, reps), out_shape=(j...]
  transfers between devices with their start and end apart: 3 -> 0, of which waited for: 2 -> 0; matrix products, arithmetic and copies ran while one was open for 0% -> 0% of each run, Pallas kernels for 5% -> 0%
where the time goes in v4:
time: 524 us; the launch traced here: 514 us
  Pallas kernels  492 us (94%)
  local copies, waits for them, and re-layouts  14.5 us (3%)
  other arithmetic  5.74 us (1%)
    pallas_call x2, Pallas kernels, attend_backward(): pl.pallas_call(functools.partial(attend_backward_kernel, n, reps, seqs, (...  139 us
    pallas_call x2, Pallas kernels, ffn_backward(): pl.pallas_call(functools.partial(ffn_backward_kernel, n, reps, (len(w_up)...  96.6 us
    pallas_call x2, Pallas kernels, attend_forward(): pl.pallas_call(functools.partial(attend_forward_kernel, n, seqs, layer, (...  90.9 us
    pallas_call x2, Pallas kernels, ffn_forward(): pl.pallas_call(functools.partial(ffn_forward_kernel, n, last, layer, (len...  69.2 us
    pallas_call x1, Pallas kernels, last_sums(): pl.pallas_call(functools.partial(last_sums_kernel, n, reps), out_shape=(j...  68.8 us
    pallas_call x1, Pallas kernels, gather_weights(): pl.pallas_call(functools.partial(gather_kernel, n, layer, parts, len(shar...  27.7 us

profile of v4, /device:TPU:0, one launch (start us, length us, event | category | flops | bytes accessed | tf_op | source)
XLA Modules:
  0.0 514.4 jit_solution(84974312091988335)
XLA Ops:
  0.7 0.8 reshape.168
  1.4 0.7 copy.24
  2.2 0.7 reshape.166
  3.5 27.7 %gather_weights.1 = (f32[256,128]{1,0:T(8,128)}, bf16[768,1152]{1,0:T(8,128)(2,1)}, bf16[768,1152]{1,0:T(8,128)(2,1)}, bf16[768,384]{1,0:T(8,128)(2,1)}, bf16[768,384]{1,0:T(8,128)(2,1)}) custom-call(bf16[2,96,2304]{2,1,0:T(8,128)(2,1)} %refs_6_.1, bf16[2,96,768]{2,1,0:T(8,128)(2,1)} %refs_7_.1, f32[1,32,128]{2,1,0:T(8,128)} %fusion.6.refs_2_), custom_call_target="tpu_custom_call" | custom-call | tf_op jit(solution)/shard_map/gather_weights/pallas_call | solution.py:176
  31.2 0.9 reshape.170
  32.5 0.6 fusion.5
  33.9 1.0 copy.45
  34.9 50.1 %attend_forward.2 = (bf16[1024,768]{1,0:T(8,128)(2,1)}, bf16[1024,768]{1,0:T(8,128)(2,1)}, bf16[1024,768]{1,0:T(8,128)(2,1)}, bf16[1024,768]{1,0:T(8,128)(2,1)},...) custom-call(bf16[1024,768]{1,0:T(8,128)(2,1)} %bitcast.92, ...), custom_call_target="tpu_custom_call" | custom-call | flops 11274289152 | bytes 15728640 | tf_op jit(solution)/shard_map/attend_forward/pallas_call | solution.py:649
  85.6 1.0 copy.48
  86.6 41.1 %ffn_forward.2 = (bf16[1024,3072]{1,0:T(8,128)(2,1)}, bf16[1024,3072]{1,0:T(8,128)(2,1)}, bf16[1024,768]{1,0:T(8,128)(2,1)}, f32[1024,1]{1,0:T(8,128)}, f32[1024...) custom-call(f32[1024,768]{1,0:T(8,128)} %get-tuple-element.101.mid_r, ...), custom_call_target="tpu_custom_call" | custom-call | flops 19327352832 | bytes 25165824 | tf_op jit(solution)/shard_map/ffn_forward/pallas_call | solution.py:809
  127.7 40.9 %attend_forward.3 = (bf16[1024,768]{1,0:T(8,128)(2,1)}, bf16[1024,768]{1,0:T(8,128)(2,1)}, bf16[1024,768]{1,0:T(8,128)(2,1)}, bf16[1024,768]{1,0:T(8,128)(2,1)},...) custom-call(f32[1024,768]{1,0:T(8,128)} %get-tuple-element.109.x_ref, ...), custom_call_target="tpu_custom_call" | custom-call | flops 11274289152 | bytes 15728640 | tf_op jit(solution)/shard_map/attend_forward/pallas_call | solution.py:649
  169.2 28.1 %ffn_forward.3 = (bf16[1024,3072]{1,0:T(8,128)(2,1)}, bf16[1024,3072]{1,0:T(8,128)(2,1)}, bf16[1024,768]{1,0:T(8,128)(2,1)}, f32[1024,1]{1,0:T(8,128)}, bf16[1024,768]{1,0:T(8,128)(2,1)}) custom-call(f32[1024,768]{1,0:T(8,128)} %get-tuple-element.114.mid_ref, bf16[1024,768]{1,0:T(8,128)(2,1)} %get-tuple-element.115.low_ref, ...), custom_call_target="tpu_custom_call" | custom-call | flops 19327352832 | bytes 25165824 | tf_op jit(solution)/shard_map/ffn_forward/pallas_call | solution.py:809
  197.3 43.8 %ffn_backward.2 = (f32[1024,768]{1,0:T(8,128)}, bf16[1024,768]{1,0:T(8,128)(2,1)}, f32[8,768]{1,0:T(8,128)}, f32[1,3072]{1,0:T(1,128)}, bf16[4,384,768]{2,1,0:T(...) custom-call(bf16[1024,768]{1,0:T(8,128)(2,1)} %bitcast.91, ...), custom_call_target="tpu_custom_call" | custom-call | flops 24159191040 | bytes 25165824 | tf_op jit(solution)/shard_map/ffn_backward/pallas_call | solution.py:1076
  241.1 63.9 %attend_backward.2 = (f32[1024,768]{1,0:T(8,128)}, f32[8,768]{1,0:T(8,128)}, bf16[4,192,768]{2,1,0:T(8,128)(2,1)}, bf16[4,192,768]{2,1,0:T(8,128)(2,1)}, bf16[4,...) custom-call(bf16[1024,768]{1,0:T(8,128)(2,1)} %get-tuple-element.129.ga_ref, ...), custom_call_target="tpu_custom_call" | custom-call | flops 25769803776 | bytes 15728640 | tf_op jit(solution)/shard_map/attend_backward/pallas_call | solution.py:1356
  305.0 0.8 broadcast_in_dim.21.valid_ref
  305.8 52.8 %ffn_backward.3 = (f32[1024,768]{1,0:T(8,128)}, bf16[1024,768]{1,0:T(8,128)(2,1)}, f32[8,768]{1,0:T(8,128)}, f32[1,3072]{1,0:T(1,128)}, bf16[4,384,768]{2,1,0:T(...) custom-call(f32[1024,768]{1,0:T(8,128)} %get-tuple-element.141.g_ref, ...), custom_call_target="tpu_custom_call" | custom-call | flops 24159191040 | bytes 25165824 | tf_op jit(solution)/shard_map/ffn_backward/pallas_call | solution.py:1076
  358.6 75.2 %attend_backward.3 = (bf16[1024,768]{1,0:T(8,128)(2,1)}, f32[8,768]{1,0:T(8,128)}, bf16[4,192,768]{2,1,0:T(8,128)(2,1)}, bf16[4,192,768]{2,1,0:T(8,128)(2,1)}, b...) custom-call(bf16[1024,768]{1,0:T(8,128)(2,1)} %get-tuple-element.153, ...), custom_call_target="tpu_custom_call" | custom-call | flops 25769803776 | bytes 15728640 | tf_op jit(solution)/shard_map/attend_backward/pallas_call | solution.py:1356
  433.8 68.8 %last_sums.1 = (bf16[2,384,768]{2,1,0:T(8,128)(2,1)}, bf16[2,192,768]{2,1,0:T(8,128)(2,1)}, f32[32,768]{1,0:T(8,128)}) custom-call(bf16[4,192,768]{2,1,0:T(8,128)(2,1)} %get-tuple-element.166.a_keep, bf16[4,192,768]{2,1,0:T(8,128)(2,1)} %get-tuple-element.167.b_keep, bf16[4,192,768]{2,1,0:T(8,128)(2,1)} %get-tuple-element.168.a_send, ...), custom_call_target="tpu_custom_call" | custom-call | tf_op jit(solution)/shard_map/last_sums/pallas_call | solution.py:1489
  502.6 1.1 convert_bitcast_fusion.1
  503.8 1.3 copy.42
  505.1 0.9 fusion.2
  507.3 1.6 pad_maximum_fusion
  509.1 1.7 copy.43
  512.8 1.1 copy.53
  (45 shorter events, 5.9 us)
Async XLA Ops:
  0.6 33.2 %copy-start.7 = (s32[2]{0:T(128)S(1)}, s32[2]{0:T(128)}, u32[]{:S(2)}) copy-start(s32[2]{0:T(128)} %param.13) | copy-start | bytes 28
  433.8 68.8 %copy-start = (bf16[2,192,768]{2,1,0:T(8,128)(2,1)S(1)}, bf16[2,192,768]{2,1,0:T(8,128)(2,1)}, u32[]{:S(2)}) copy-start(bf16[2,192,768]{2,1,0:T(8,128)(2,1)} %get-tuple-element.178) | copy-start | bytes 1769476
  503.7 1.3 copy-start.1
  505.1 1.5 copy-start.3
  505.9 1.2 copy-start.4
  505.9 1.3 copy-start.5
  509.1 1.7 copy-start.6
  509.1 3.7 copy-start.2

commit v5 on v4

--- a/solution.py
+++ b/solution.py
@@ -34,6 +34,10 @@
 def whole(shape):
     zeros = (0,) * len(shape)
     return pl.BlockSpec(shape, lambda *_: zeros, pipeline_mode=pl.Buffered(1))
+
+
+def layer_of(array, layer):
+    return pl.BlockSpec((None, *array.shape[1:]), lambda *_: (layer, 0, 0), pipeline_mode=pl.Buffered(1))
 
 
 def column_block(rows, width):
@@ -102,8 +106,8 @@
             pltpu.make_async_copy(self.own, self.rows(0), self.local_sem).start()
         self.copy(self.order[round_at]).start()
 
-    def onward(self, round_at):
-        masks = self.round_masks(round_at)
+    def onward(self, round_at, which=slice(None)):
+        masks = self.round_masks(round_at)[which]
         for mask in masks:
             self.copy(mask).wait_recv()
         for bit in self.order[round_at + 1 :]:
@@ -125,9 +129,15 @@
             gather.begin(round_at)
 
 
-def onward_all(gathers, round_at):
+def onward_all(gathers, round_at, which=slice(None)):
     for gather in gathers:
-        gather.onward(round_at)
+        gather.onward(round_at, which)
+
+
+def onward_rest(gathers):
+    onward_all(gathers, 1, slice(1, None))
+    for round_at in range(2, len(gathers[0].order)):
+        onward_all(gathers, round_at)
 
 
 def end_all(gathers):
@@ -413,8 +423,9 @@
 
 
 class Chain(Spread):
-    def __init__(self, count, scratch, first=0):
+    def __init__(self, count, scratch, first=0, lag=1):
         super().__init__(count, scratch, first)
+        self.lag = lag
         self.inner = (self.rank == 1) | (self.rank == 2)
         self.chunks = self.streams * PIECES
 
@@ -465,14 +476,16 @@
 
     @property
     def ticks(self):
-        return self.chunks + 3
+        return (self.chunks - 1) * self.lag + 4
 
     def tick(self, tick):
-        for chunk in range(self.chunks):
-            if tick == 0:
+        if tick == 0:
+            for chunk in range(self.chunks):
                 self.act(chunk, 0)
-            elif 1 <= tick - chunk <= 3:
-                self.act(chunk, tick - chunk)
+            return
+        for chunk in range(self.chunks - 1, -1, -1) if self.lag else range(self.chunks):
+            if 1 <= tick - chunk * self.lag <= 3:
+                self.act(chunk, tick - chunk * self.lag)
 
     def end(self):
         for chunk in range(self.chunks):
@@ -487,8 +500,8 @@
                 self.copy(0, chunk).wait_send()
 
 
-def make_spread(count, scratch, first=0):
-    return (Chain if count == CHAIN else Spread)(count, scratch, first)
+def make_spread(count, scratch, first=0, lag=1):
+    return Chain(count, scratch, first, lag) if count == CHAIN else Spread(count, scratch, first)
 
 
 def rep_masks(count):
@@ -557,8 +570,12 @@
     count = len(parts)
     q_ref, k_ref, v_ref, ctx_ref, lse_ref, mid_ref, low_ref, n1_ref, r1_ref = refs[:9]
     wholes, refs = refs[9 : 9 + count], refs[9 + count :]
-    base, w_qkv, w_out, acc, sems = refs[:5]
-    gathers = make_gathers(layer, parts, shards, wholes, refs[5:])
+    base, w_qkv, w_out, acc, sems, mid_buffer, low_buffer, n1_buffer, out_sems = refs[:9]
+    gathers = make_gathers(layer, parts, shards, wholes, refs[9:])
+    out_copies = [
+        pltpu.make_async_copy(source, target, out_sems.at[at])
+        for at, (source, target) in enumerate(((mid_buffer, mid_ref), (low_buffer, low_ref), (n1_buffer, n1_ref)))
+    ]
     step, steps = pl.program_id(0), pl.num_programs(0)
     rows, width = x_ref.shape
     seq = rows // seqs
@@ -570,8 +587,14 @@
         for copy in copies:
             copy.start()
         begin_all(n, gathers)
-        base[...] = x_ref[...].astype(bf16)
-        acc[...] = x_ref[...].astype(f32) + small_ref[2:3, :]
+
+        def prepare(block, carry):
+            at = pl.ds(pl.multiple_of(block * ROWS, ROWS), ROWS)
+            base[at, :] = x_ref[at, :].astype(bf16)
+            acc[at, :] = x_ref[at, :].astype(f32) + small_ref[2:3, :]
+            return carry
+
+        lax.fori_loop(0, rows // ROWS, prepare, 0)
         for copy in copies:
             copy.wait()
 
@@ -616,6 +639,10 @@
     def _():
         onward_all(gathers, 0)
 
+    @pl.when(step == steps - 1)
+    def _():
+        onward_all(gathers, 1, slice(1))
+
     def mix(block, carry):
         at = pl.ds(pl.multiple_of(block * ROWS, ROWS), ROWS)
         acc[at, :] += dot_nn(ctx_ref[at, :], w_out[pl.ds(columns, GROUP), :])
@@ -628,16 +655,19 @@
         def finish(block, carry):
             at = pl.ds(pl.multiple_of(block * ROWS, ROWS), ROWS)
             mid, normed, scaling = norm_forward(acc[at, :], small_ref[6:7, :], small_ref[4:5, :])
-            mid_ref[at, :] = mid
-            low_ref[at, :] = mid.astype(bf16)
-            n1_ref[at, :] = normed.astype(bf16)
+            mid_buffer[at, :] = mid
+            low_buffer[at, :] = mid.astype(bf16)
+            n1_buffer[at, :] = normed.astype(bf16)
             r1_ref[at, :] = scaling
             return carry
 
         lax.fori_loop(0, rows // ROWS, finish, 0)
-        for round_at in range(1, len(gathers[0].order)):
-            onward_all(gathers, round_at)
+        for copy in out_copies:
+            copy.start()
+        onward_rest(gathers)
         end_all(gathers)
+        for copy in out_copies:
+            copy.wait()
 
 
 def attend_forward(n, x, small, key_mask, w_qkv, w_out, seqs, layer, shards, parts, collective_id):
@@ -665,14 +695,14 @@
         grid_spec=pltpu.PrefetchScalarGridSpec(
             num_scalar_prefetch=0,
             grid=(steps,),
-            in_specs=[whole((rows, width)), whole(small.shape), whole((rows, 1))]
+            in_specs=[whole((rows, width)), layer_of(small, layer), whole((rows, 1))]
             + [ANY] * (len(w_qkv) + len(w_out) + len(shards)),
             out_specs=[column_block(rows, GROUP)] * 4
             + [
                 pl.BlockSpec((1, seqs * heads, seq), lambda j, *_: (j, 0, 0)),
-                whole((rows, width)),
-                whole((rows, width)),
-                whole((rows, width)),
+                ANY,
+                ANY,
+                ANY,
                 whole((rows, 1)),
             ]
             + [ANY] * len(parts),
@@ -682,6 +712,10 @@
                 pltpu.VMEM((width, width), bf16),
                 pltpu.VMEM((rows, width), f32),
                 pltpu.SemaphoreType.DMA((len(w_qkv) + len(w_out),)),
+                pltpu.VMEM((rows, width), f32),
+                pltpu.VMEM((rows, width), bf16),
+                pltpu.VMEM((rows, width), bf16),
+                pltpu.SemaphoreType.DMA((3,)),
             ]
             + gather_sems(n, len(parts)),
         ),
@@ -705,8 +739,12 @@
     if not last:
         hid_low_ref, refs = refs[0], refs[1:]
     wholes, refs = refs[:count], refs[count:]
-    w_up, w_down, acc, sems = refs[:4]
-    gathers = make_gathers(layer, parts, shards, wholes, refs[4:]) if count else []
+    w_up, w_down, acc, sems, n2_buffer, hid_buffer, low_buffer, out_sems = refs[:8]
+    gathers = make_gathers(layer, parts, shards, wholes, refs[8:]) if count else []
+    out_pairs = [(n2_buffer, n2_ref), (hid_buffer, hid_ref)] + ([] if last else [(low_buffer, hid_low_ref)])
+    out_copies = [
+        pltpu.make_async_copy(source, target, out_sems.at[at]) for at, (source, target) in enumerate(out_pairs)
+    ]
     step, steps = pl.program_id(0), pl.num_programs(0)
     rows, width = mid_ref.shape
     chunk = act_ref.shape[1]
@@ -718,7 +756,13 @@
             copy.start()
         if gathers:
             begin_all(n, gathers)
-        acc[...] = mid_ref[...] + small_ref[3:4, :]
+
+        def prepare(block, carry):
+            at = pl.ds(pl.multiple_of(block * ROWS, ROWS), ROWS)
+            acc[at, :] = mid_ref[at, :] + small_ref[3:4, :]
+            return carry
+
+        lax.fori_loop(0, rows // ROWS, prepare, 0)
         for copy in copies:
             copy.wait()
 
@@ -727,6 +771,10 @@
         @pl.when(step == 2)
         def _():
             onward_all(gathers, 0)
+
+        @pl.when(step == 3)
+        def _():
+            onward_all(gathers, 1, slice(1))
 
     columns = pl.multiple_of(step * chunk, chunk)
     tile = 256
@@ -755,29 +803,35 @@
         def finish(block, carry):
             at = pl.ds(pl.multiple_of(block * ROWS, ROWS), ROWS)
             hidden, normed, scaling = norm_forward(acc[at, :], small_ref[7:8, :], small_ref[5:6, :])
-            n2_ref[at, :] = normed.astype(bf16)
+            n2_buffer[at, :] = normed.astype(bf16)
             r2_ref[at, :] = scaling
             if last:
-                hid_ref[at, :] = (hidden * valid_ref[at, :]).astype(bf16)
+                hid_buffer[at, :] = (hidden * valid_ref[at, :]).astype(bf16)
             else:
-                hid_ref[at, :] = hidden
-                hid_low_ref[at, :] = hidden.astype(bf16)
+                hid_buffer[at, :] = hidden
+                low_buffer[at, :] = hidden.astype(bf16)
             return carry
 
         lax.fori_loop(0, rows // ROWS, finish, 0)
+        for copy in out_copies:
+            copy.start()
 
     if gathers:
 
         @pl.when(step == steps - 1)
         def _():
-            for round_at in range(1, len(gathers[0].order)):
-                onward_all(gathers, round_at)
+            onward_rest(gathers)
             end_all(gathers)
+
+    @pl.when(step == steps - 1)
+    def _():
+        for copy in out_copies:
+            copy.wait()
 
 
 def ffn_forward(n, mid, low, small, up_bias, valid, w_up, w_down, last, layer, shards, parts, collective_id):
     rows, width = mid.shape
-    units = up_bias.shape[1]
+    units = up_bias.shape[2]
     chunk = width
     steps = units // chunk
     out_shape = [
@@ -787,14 +841,10 @@
         jax.ShapeDtypeStruct((rows, 1), f32),
         jax.ShapeDtypeStruct((rows, width), bf16 if last else f32),
     ]
-    out_specs = [column_block(rows, chunk)] * 2 + [
-        whole((rows, width)),
-        whole((rows, 1)),
-        whole((rows, width)),
-    ]
+    out_specs = [column_block(rows, chunk)] * 2 + [ANY, whole((rows, 1)), ANY]
     if not last:
         out_shape.append(jax.ShapeDtypeStruct((rows, width), bf16))
-        out_specs.append(whole((rows, width)))
+        out_specs.append(ANY)
     out_shape += wholes_of(n, shards, parts)
     out_specs += [ANY] * len(parts)
     if parts:
@@ -808,7 +858,7 @@
         params = pltpu.CompilerParams(dimension_semantics=("arbitrary",), vmem_limit_bytes=VMEM_BYTES)
     return pl.pallas_call(
         functools.partial(
-            ffn_forward_kernel, n, last, layer, (len(w_up), len(w_up) + len(w_down), len(shards)), parts
+            ffn_forward_kernel, n, last, layer + 1, (len(w_up), len(w_up) + len(w_down), len(shards)), parts
         ),
         out_shape=tuple(out_shape),
         grid_spec=pltpu.PrefetchScalarGridSpec(
@@ -817,8 +867,8 @@
             in_specs=[
                 whole((rows, width)),
                 whole((rows, width)),
-                whole(small.shape),
-                column_block(1, chunk),
+                layer_of(small, layer),
+                pl.BlockSpec((None, 1, chunk), lambda j, *_: (layer, 0, j)),
                 whole((rows, 1)),
             ]
             + [ANY] * (len(w_up) + len(w_down) + len(shards)),
@@ -828,6 +878,10 @@
                 pltpu.VMEM((units, width), bf16),
                 pltpu.VMEM((rows, width), f32),
                 pltpu.SemaphoreType.DMA((len(w_up) + len(w_down),)),
+                pltpu.VMEM((rows, width), bf16),
+                pltpu.VMEM((rows, width), bf16 if last else f32),
+                pltpu.VMEM((rows, width), bf16),
+                pltpu.SemaphoreType.DMA((3,)),
             ]
             + (gather_sems(n, len(parts)) if parts else []),
         ),
@@ -870,6 +924,7 @@
         reduce = Reduce(halves, refs[10 : 15 + hops], bits_below(n, 2))
         spread = make_spread(reps, refs[15 + hops : 21 + hops])
         spread_sem = refs[21 + hops]
+    carry_in = carry
     step, steps = pl.program_id(0), pl.num_programs(0)
     me = lax.axis_index("fsdp")
     rows, width = acc.shape
@@ -913,7 +968,9 @@
 
         def prepare(block, carry):
             at = pl.ds(pl.multiple_of(block * ROWS, ROWS), ROWS)
-            grad = g_ref[at, :].astype(f32) * valid_ref[at, :]
+            grad = g_ref[at, :].astype(f32)
+            if not carry_in:
+                grad = grad * valid_ref[at, :]
             normed = n2_ref[at, :].astype(f32)
             summed = norm_backward(grad, normed, r2_ref[at, :], small_ref[7:8, :])
             acc[at, :] = summed
@@ -1053,7 +1110,7 @@
     )
 
 
-def ffn_backward(n, reps, grad, valid, n2, r2, low, n1, r1, small, act, slope, w_up, w_down, carry, collective_id):
+def ffn_backward(n, reps, grad, valid, n2, r2, low, n1, r1, small, act, slope, w_up, w_down, layer, carry, collective_id):
     rows, width = grad.shape
     units = act.shape[1]
     chunk = width
@@ -1097,7 +1154,7 @@
                 whole((rows, width)),
                 whole((rows, width)),
                 whole((rows, 1)),
-                whole(small.shape),
+                layer_of(small, layer),
                 column_block(rows, chunk),
                 column_block(rows, chunk),
             ]
@@ -1141,26 +1198,18 @@
     refs = refs[7:]
     if spreads:
         spread_refs, refs = refs[:2], refs[2:]
-    w_qkv, w_out, acc, base_turned, gctx, gproj, d_qkv, d_out, p_all, ds_all, sems, out_sems = refs[:12]
+    w_qkv, w_out, acc, base_turned, gctx, gproj, d_qkv, d_out, p_all, ds_all, ctx_turned, sems, out_sems = refs[:13]
     hops = len(bits_below(n, 2))
-    reduce = Reduce(halves, refs[12 : 17 + hops], bits_below(n, 2))
+    reduce = Reduce(halves, refs[13 : 18 + hops], bits_below(n, 2))
     step, steps = pl.program_id(0), pl.num_programs(0)
     me = lax.axis_index("fsdp")
     if spreads:
-        rest = refs[17 + hops :]
-        spread_list = [make_spread(reps, rest[:6]), make_spread(reps, rest[6:12], 1)]
+        rest = refs[18 + hops :]
+        spread_list = [make_spread(reps, rest[:6], 0, 0), make_spread(reps, rest[6:12], 1, 0)]
         spread_copies = [
             pltpu.make_async_copy(spread.whole, ref, rest[12].at[at])
             for at, (spread, ref) in enumerate(zip(spread_list, spread_refs))
         ]
-
-    def spread_tick(tick):
-        if spreads:
-            for spread, copy in zip(spread_list, spread_copies):
-                if tick < spread.ticks:
-                    spread.tick(tick)
-                if tick == spread.ticks - 1:
-                    copy.start()
 
     @pl.when(step == 0)
     def _():
@@ -1170,18 +1219,16 @@
                 spread.begin(source)
         reduce.begin()
         if spreads:
-            for spread, source in zip(spread_list, spread_from):
+            for spread, source in zip(spread_list[::-1], spread_from[::-1]):
                 spread.loaded(source)
 
     if spreads:
 
-        @pl.when(step == 1)
-        def _():
-            spread_tick(2)
-
-        @pl.when(step == 2)
-        def _():
-            spread_tick(4)
+        for at in (1, 2):
+
+            @pl.when(step == at)
+            def _():
+                spread_list[1].tick(at)
 
     rows, width = ga_ref.shape
     seq = rows // seqs
@@ -1217,7 +1264,14 @@
         return carry
 
     lax.fori_loop(0, rows // ROWS, through, 0)
-    d_out[pl.ds(columns, GROUP), :] = dot_nn(ctx_ref[...].T, ga_ref[...]).astype(bf16)
+    ctx_turned[...] = ctx_ref[...].T
+
+    def out_part(part, carry):
+        at = pl.ds(pl.multiple_of(part * tile, tile), tile)
+        d_out[pl.ds(columns, GROUP), at] = dot_nn(ctx_turned[...], ga_ref[:, at]).astype(bf16)
+        return carry
+
+    lax.fori_loop(0, width // tile, out_part, 0)
 
     @pl.when(step == 2)
     def _():
@@ -1225,6 +1279,10 @@
             reduce.hop(hop)
 
     def attend(s, carry):
+        @pl.when((step == 0) & (s == seqs - 1))
+        def _():
+            reduce.hop(0)
+
         at = pl.ds(pl.multiple_of(s * seq, seq), seq)
         q, k, v, grad = q_ref[at, :], k_ref[at, :], v_ref[at, :], gctx[at, :]
         k_turned = k.T
@@ -1254,21 +1312,14 @@
     lax.fori_loop(0, seqs, attend, 0)
     sums_ref[...] = jnp.zeros_like(sums_ref)
 
-    @pl.when(step == 0)
-    def _():
-        reduce.hop(0)
-        spread_tick(1)
-
     if spreads:
 
-        @pl.when(step == 1)
-        def _():
-            spread_tick(3)
-
-        @pl.when(step == 2)
-        def _():
-            for tick in range(5, spread_list[0].ticks):
-                spread_tick(tick)
+        for at in (1, 2):
+
+            @pl.when(step == at)
+            def _():
+                spread_list[0].tick(at)
+
 
     def onward(block, carry):
         at = pl.ds(pl.multiple_of(block * ROWS, ROWS), ROWS)
@@ -1284,7 +1335,12 @@
 
     @pl.when(step == steps - 1)
     def _():
-        gh_ref[...] = acc[...].astype(gh_ref.dtype)
+        def finish(block, carry):
+            at = pl.ds(pl.multiple_of(block * ROWS, ROWS), ROWS)
+            gh_ref[at, :] = acc[at, :].astype(gh_ref.dtype)
+            return carry
+
+        lax.fori_loop(0, rows // ROWS, finish, 0)
 
     def place_of(part, a_half, b_half):
         return a_half if part < 2 else b_half
@@ -1331,6 +1387,10 @@
         out_copy(False)
         reduce.finish(reduced_ref)
         if spreads:
+            for spread, copy in zip(spread_list[::-1], spread_copies[::-1]):
+                for tick in range(3, spread.ticks):
+                    spread.tick(tick)
+                copy.start()
             for spread, copy in zip(spread_list, spread_copies):
                 copy.wait()
                 spread.end()
@@ -1387,6 +1447,7 @@
                 pltpu.VMEM((width, width), bf16),
                 pltpu.VMEM((seq, heads * seq), bf16),
                 pltpu.VMEM((seq, heads * seq), bf16),
+                pltpu.VMEM((GROUP, rows), bf16),
                 pltpu.SemaphoreType.DMA((len(w_qkv) + len(w_out),)),
                 pltpu.SemaphoreType.DMA((4, n)),
             ]
@@ -1524,7 +1585,6 @@
     alive = jnp.arange(seqs, dtype=jnp.int32) < live_batches[0]
     key_mask = jnp.where(inside, 0.0, big_negative).astype(f32).reshape(rows, 1)
     valid = jnp.where(inside & alive[:, None], 1.0, 0.0).astype(f32).reshape(rows, 1)
-    ones = jnp.ones((rows, 1), f32)
 
     chip_bits = bits_below(n, 2)
     orders = (tuple(chip_bits + [1]), tuple(chip_bits[::-1] + [1]))
@@ -1555,7 +1615,7 @@
         begun = EARLY if layer else 0
         parts = parts_of(0, w_up, UP_PARTS, orders, begun) + parts_of(1, w_down, 2, orders)
         results = attend_forward(
-            n, current, smalls[layer], key_mask, qkv[layer], out[layer], seqs,
+            n, current, smalls, key_mask, qkv[layer], out[layer], seqs,
             layer, (w_up, w_down), parts, 1 + 2 * layer,
         )
         q, k, v, ctx, lse, mid, low, n1, r1 = results[:9]
@@ -1563,8 +1623,8 @@
         down[layer] = results[-2:]
         parts = [] if last else attend_parts + parts_of(2, w_up, UP_PARTS, orders)[:EARLY]
         results = ffn_forward(
-            n, mid, low, smalls[layer], up_bias_all[layer], valid, up[layer], down[layer], last,
-            layer + 1, () if last else (w_qkv, w_out, w_up), parts, 2 + 2 * layer,
+            n, mid, low, smalls, up_bias_all, valid, up[layer], down[layer], last,
+            layer, () if last else (w_qkv, w_out, w_up), parts, 2 + 2 * layer,
         )
         act, slope, n2, r2, current = results[:5]
         saved.append((base, q, k, v, ctx, lse, low, n1, r1, act, slope, n2, r2))
@@ -1574,7 +1634,6 @@
     outputs = current.reshape(seqs, seq, width)
 
     grad = cotangent.reshape(rows, width)
-    grad_valid = valid
     sum_rows = [None] * LAYERS
     attend_halves, attend_reduced = None, None
     down_done, up_done, attend_done = [None] * LAYERS, [None] * LAYERS, [None] * LAYERS
@@ -1583,7 +1642,7 @@
         first = layer == LAYERS - 1
         base, q, k, v, ctx, lse, low, n1, r1, act, slope, n2, r2 = saved[layer]
         results = ffn_backward(
-            n, reps, grad, grad_valid, n2, r2, low, n1, r1, smalls[layer], act, slope, up[layer], down[layer],
+            n, reps, grad, valid, n2, r2, low, n1, r1, smalls, act, slope, up[layer], down[layer], layer,
             () if first else (*attend_halves, ffn_reduced), 10 + layer,
         )
         gs1, ga1, sums, up_sum, down_keep, down_send, up_keep, up_send = results[:8]
@@ -1603,7 +1662,6 @@
         attend_halves, ffn_reduced = results[2:6], results[6]
         if not first:
             attend_done[layer + 1], up_done[layer + 1] = results[7:]
-        grad_valid = ones
         sum_rows[layer] = (sums, proj_sums, up_sum)
     grad_tokens = grad.reshape(seqs, seq, width)
     ffn_last, attend_done[0], small_total = last_sums(

time: 524 us -> 493 us (0.941); the launches traced: 514 us -> 493 us
  Pallas kernels: 492 us -> 473 us
    pallas_call x2, Pallas kernels: 139 us -> 131 us  [attend_backward(): pl.pallas_call(functools.partial(attend_backward_kernel, n, reps, seqs, (...]
    pallas_call x2, Pallas kernels: 90.9 us -> 85.5 us  [attend_forward(): pl.pallas_call(functools.partial(attend_forward_kernel, n, seqs, layer, (...]
where the time goes in v5:
time: 493 us
  Pallas kernels  473 us (96%)
  local copies, waits for them, and re-layouts  13.1 us (3%)
  other arithmetic  5.73 us (1%)
    pallas_call x2, Pallas kernels, attend_backward(): pl.pallas_call(functools.partial(attend_backward_kernel, n, reps, seqs, (...  131 us
    pallas_call x2, Pallas kernels, ffn_backward(): pl.pallas_call(functools.partial(ffn_backward_kernel, n, reps, (len(w_up)...  96.8 us
    pallas_call x2, Pallas kernels, attend_forward(): pl.pallas_call(functools.partial(attend_forward_kernel, n, seqs, layer, (...  85.5 us
    pallas_call x2, Pallas kernels, ffn_forward(): pl.pallas_call(functools.partial(ffn_forward_kernel, n, last, layer + 1,...  67.7 us
    pallas_call x1, Pallas kernels, last_sums(): pl.pallas_call(functools.partial(last_sums_kernel, n, reps), out_shape=(j...  64.2 us
    pallas_call x1, Pallas kernels, gather_weights(): pl.pallas_call(functools.partial(gather_kernel, n, layer, parts, len(shar...  27.7 us

profile of v5, /device:TPU:0, one launch (start us, length us, event | category | flops | bytes accessed | tf_op | source)
XLA Modules:
  0.0 492.9 jit_solution(4376705979823805225)
XLA Ops:
  0.7 0.8 reshape.166
  1.4 0.7 copy.24
  2.2 0.7 reshape.164
  3.5 27.7 %gather_weights.1 = (f32[256,128]{1,0:T(8,128)}, bf16[768,1152]{1,0:T(8,128)(2,1)}, bf16[768,1152]{1,0:T(8,128)(2,1)}, bf16[768,384]{1,0:T(8,128)(2,1)}, bf16[768,384]{1,0:T(8,128)(2,1)}) custom-call(bf16[2,96,2304]{2,1,0:T(8,128)(2,1)} %refs_6_.1, bf16[2,96,768]{2,1,0:T(8,128)(2,1)} %refs_7_.1, f32[1,32,128]{2,1,0:T(8,128)} %fusion.3.refs_2_), custom_call_target="tpu_custom_call" | custom-call | tf_op jit(solution)/shard_map/gather_weights/pallas_call | solution.py:186
  31.2 0.9 reshape.168
  32.5 0.6 pad_maximum_fusion.2.small_ref
  33.9 1.0 copy.46
  34.9 47.3 %attend_forward.2 = (bf16[1024,768]{1,0:T(8,128)(2,1)}, bf16[1024,768]{1,0:T(8,128)(2,1)}, bf16[1024,768]{1,0:T(8,128)(2,1)}, bf16[1024,768]{1,0:T(8,128)(2,1)},...) custom-call(bf16[1024,768]{1,0:T(8,128)(2,1)} %bitcast.81, ...), custom_call_target="tpu_custom_call" | custom-call | flops 11274289152 | bytes 15728640 | tf_op jit(solution)/shard_map/attend_forward/pallas_call | solution.py:679
  82.3 0.6 reshape.174.up_bias_ref
  82.9 1.0 copy.48
  83.9 38.8 %ffn_forward.2 = (bf16[1024,3072]{1,0:T(8,128)(2,1)}, bf16[1024,3072]{1,0:T(8,128)(2,1)}, bf16[1024,768]{1,0:T(8,128)(2,1)}, f32[1024,1]{1,0:T(8,128)}, f32[1024...) custom-call(f32[1024,768]{1,0:T(8,128)} %get-tuple-element.101.mid_r, ...), custom_call_target="tpu_custom_call" | custom-call | flops 19327352832 | bytes 25165824 | tf_op jit(solution)/shard_map/ffn_forward/pallas_call | solution.py:859
  122.8 38.2 %attend_forward.3 = (bf16[1024,768]{1,0:T(8,128)(2,1)}, bf16[1024,768]{1,0:T(8,128)(2,1)}, bf16[1024,768]{1,0:T(8,128)(2,1)}, bf16[1024,768]{1,0:T(8,128)(2,1)},...) custom-call(f32[1024,768]{1,0:T(8,128)} %get-tuple-element.109.x_ref, ...), custom_call_target="tpu_custom_call" | custom-call | flops 11274289152 | bytes 15728640 | tf_op jit(solution)/shard_map/attend_forward/pallas_call | solution.py:679
  161.0 28.8 %ffn_forward.3 = (bf16[1024,3072]{1,0:T(8,128)(2,1)}, bf16[1024,3072]{1,0:T(8,128)(2,1)}, bf16[1024,768]{1,0:T(8,128)(2,1)}, f32[1024,1]{1,0:T(8,128)}, bf16[1024,768]{1,0:T(8,128)(2,1)}) custom-call(f32[1024,768]{1,0:T(8,128)} %get-tuple-element.114.mid_ref, bf16[1024,768]{1,0:T(8,128)(2,1)} %get-tuple-element.115.low_ref, ...), custom_call_target="tpu_custom_call" | custom-call | flops 19327352832 | bytes 25165824 | tf_op jit(solution)/shard_map/ffn_forward/pallas_call | solution.py:859
  189.8 43.8 %ffn_backward.2 = (f32[1024,768]{1,0:T(8,128)}, bf16[1024,768]{1,0:T(8,128)(2,1)}, f32[8,768]{1,0:T(8,128)}, f32[1,3072]{1,0:T(1,128)}, bf16[4,384,768]{2,1,0:T(...) custom-call(bf16[1024,768]{1,0:T(8,128)(2,1)} %bitcast.80, ...), custom_call_target="tpu_custom_call" | custom-call | flops 24159191040 | bytes 25165824 | tf_op jit(solution)/shard_map/ffn_backward/pallas_call | solution.py:1133
  233.6 60.4 %attend_backward.2 = (f32[1024,768]{1,0:T(8,128)}, f32[8,768]{1,0:T(8,128)}, bf16[4,192,768]{2,1,0:T(8,128)(2,1)}, bf16[4,192,768]{2,1,0:T(8,128)(2,1)}, bf16[4,...) custom-call(bf16[1024,768]{1,0:T(8,128)(2,1)} %get-tuple-element.129.ga_ref, ...), custom_call_target="tpu_custom_call" | custom-call | flops 25769803776 | bytes 15728640 | tf_op jit(solution)/shard_map/attend_backward/pallas_call | solution.py:1416
  294.1 53.0 %ffn_backward.3 = (f32[1024,768]{1,0:T(8,128)}, bf16[1024,768]{1,0:T(8,128)(2,1)}, f32[8,768]{1,0:T(8,128)}, f32[1,3072]{1,0:T(1,128)}, bf16[4,384,768]{2,1,0:T(...) custom-call(f32[1024,768]{1,0:T(8,128)} %get-tuple-element.141.g_ref, ...), custom_call_target="tpu_custom_call" | custom-call | flops 24159191040 | bytes 25165824 | tf_op jit(solution)/shard_map/ffn_backward/pallas_call | solution.py:1133
  347.0 70.4 %attend_backward.3 = (bf16[1024,768]{1,0:T(8,128)(2,1)}, f32[8,768]{1,0:T(8,128)}, bf16[4,192,768]{2,1,0:T(8,128)(2,1)}, bf16[4,192,768]{2,1,0:T(8,128)(2,1)}, b...) custom-call(bf16[1024,768]{1,0:T(8,128)(2,1)} %get-tuple-element.153, ...), custom_call_target="tpu_custom_call" | custom-call | flops 25769803776 | bytes 15728640 | tf_op jit(solution)/shard_map/attend_backward/pallas_call | solution.py:1416
  417.4 64.2 %last_sums.1 = (bf16[2,384,768]{2,1,0:T(8,128)(2,1)}, bf16[2,192,768]{2,1,0:T(8,128)(2,1)}, f32[32,768]{1,0:T(8,128)}) custom-call(bf16[4,192,768]{2,1,0:T(8,128)(2,1)} %get-tuple-element.166.a_keep, bf16[4,192,768]{2,1,0:T(8,128)(2,1)} %get-tuple-element.167.b_keep, bf16[4,192,768]{2,1,0:T(8,128)(2,1)} %get-tuple-element.168.a_send, ...), custom_call_target="tpu_custom_call" | custom-call | tf_op jit(solution)/shard_map/last_sums/pallas_call | solution.py:1550
  481.6 1.1 convert_bitcast_fusion.1
  482.7 1.3 copy.43
  484.1 0.9 fusion.2
  486.3 1.6 pad_maximum_fusion
  488.1 1.7 copy.44
  491.8 1.1 copy.52
  (42 shorter events, 4.7 us)
Async XLA Ops:
  0.6 33.2 %copy-start.7 = (s32[2]{0:T(128)S(1)}, s32[2]{0:T(128)}, u32[]{:S(2)}) copy-start(s32[2]{0:T(128)} %param.13) | copy-start | bytes 28
  417.4 64.2 %copy-start = (bf16[2,192,768]{2,1,0:T(8,128)(2,1)S(1)}, bf16[2,192,768]{2,1,0:T(8,128)(2,1)}, u32[]{:S(2)}) copy-start(bf16[2,192,768]{2,1,0:T(8,128)(2,1)} %get-tuple-element.178) | copy-start | bytes 1769476
  482.7 1.3 copy-start.1
  484.1 1.5 copy-start.3
  484.9 1.2 copy-start.4
  484.9 1.3 copy-start.5
  488.1 1.7 copy-start.6
  488.1 3.7 copy-start.2

commit v6 on v5

--- a/solution.py
+++ b/solution.py
@@ -951,6 +951,7 @@
 
         @pl.when(step == 3)
         def _():
+            spread.tick(4)
             reduce.finish(reduced_ref)
     chunk = act_ref.shape[1]
     per_down = down_keep.shape[1]
@@ -1013,15 +1014,11 @@
         def _():
             reduce.hop(0)
 
-        @pl.when(step == 2)
-        def _():
-            spread.tick(3)
-
-        @pl.when(step == 3)
-        def _():
-            for tick in range(4, spread.ticks):
-                spread.tick(tick)
-            out_copy.start()
+        for at in (2, 3):
+
+            @pl.when(step == at)
+            def _():
+                spread.tick(2 * at - 1)
 
     def down_out(which):
         def run(start):
@@ -1097,6 +1094,9 @@
         down_out(step)(False)
         up_out(step)(False)
         if carry:
+            for tick in range(6, spread.ticks):
+                spread.tick(tick)
+            out_copy.start()
             out_copy.wait()
             spread.end()
 
@@ -1123,11 +1123,11 @@
         spread_rows = carry[4].shape[1]
         extra_out = [
             jax.ShapeDtypeStruct(reduced, f32),
-            jax.ShapeDtypeStruct((1, padded(spread_rows, reps), width), bf16),
+            jax.ShapeDtypeStruct((2, padded(spread_rows, reps), width), bf16),
         ]
         extra_specs = [whole(reduced), ANY]
         extra_scratch = reduce_scratch(chips, carry[0].shape[1], width, hops)
-        extra_scratch += spread_scratch(spread_rows, width, reps, 1) + [pltpu.SemaphoreType.DMA]
+        extra_scratch += spread_scratch(spread_rows, width, reps) + [pltpu.SemaphoreType.DMA]
     down_half = jax.ShapeDtypeStruct((chips, units // n, width), bf16)
     up_half = jax.ShapeDtypeStruct((chips, steps, width // n, chunk), bf16)
     return pl.pallas_call(
@@ -1193,34 +1193,28 @@
     sources, refs = refs[: counts[1]], refs[counts[1] :]
     halves, refs = refs[:4], refs[4:]
     if spreads:
-        spread_from, refs = refs[:2], refs[2:]
+        spread_from, refs = refs[0], refs[1:]
     gh_ref, sums_ref, a_keep, b_keep, a_send, b_send, reduced_ref = refs[:7]
     refs = refs[7:]
     if spreads:
-        spread_refs, refs = refs[:2], refs[2:]
+        spread_ref, refs = refs[0], refs[1:]
     w_qkv, w_out, acc, base_turned, gctx, gproj, d_qkv, d_out, p_all, ds_all, ctx_turned, sems, out_sems = refs[:13]
     hops = len(bits_below(n, 2))
     reduce = Reduce(halves, refs[13 : 18 + hops], bits_below(n, 2))
     step, steps = pl.program_id(0), pl.num_programs(0)
     me = lax.axis_index("fsdp")
     if spreads:
-        rest = refs[18 + hops :]
-        spread_list = [make_spread(reps, rest[:6], 0, 0), make_spread(reps, rest[6:12], 1, 0)]
-        spread_copies = [
-            pltpu.make_async_copy(spread.whole, ref, rest[12].at[at])
-            for at, (spread, ref) in enumerate(zip(spread_list, spread_refs))
-        ]
+        spread = make_spread(reps, refs[18 + hops : 24 + hops], 0, 0)
+        spread_copy = pltpu.make_async_copy(spread.whole, spread_ref, refs[24 + hops])
 
     @pl.when(step == 0)
     def _():
         greet_both(n, reps, bits_below(n), rep_masks(reps) if spreads else [])
         if spreads:
-            for spread, source in zip(spread_list, spread_from):
-                spread.begin(source)
+            spread.begin(spread_from)
         reduce.begin()
         if spreads:
-            for spread, source in zip(spread_list[::-1], spread_from[::-1]):
-                spread.loaded(source)
+            spread.loaded(spread_from)
 
     if spreads:
 
@@ -1228,7 +1222,7 @@
 
             @pl.when(step == at)
             def _():
-                spread_list[1].tick(at)
+                spread.tick(at)
 
     rows, width = ga_ref.shape
     seq = rows // seqs
@@ -1312,14 +1306,6 @@
     lax.fori_loop(0, seqs, attend, 0)
     sums_ref[...] = jnp.zeros_like(sums_ref)
 
-    if spreads:
-
-        for at in (1, 2):
-
-            @pl.when(step == at)
-            def _():
-                spread_list[0].tick(at)
-
 
     def onward(block, carry):
         at = pl.ds(pl.multiple_of(block * ROWS, ROWS), ROWS)
@@ -1387,13 +1373,11 @@
         out_copy(False)
         reduce.finish(reduced_ref)
         if spreads:
-            for spread, copy in zip(spread_list[::-1], spread_copies[::-1]):
-                for tick in range(3, spread.ticks):
-                    spread.tick(tick)
-                copy.start()
-            for spread, copy in zip(spread_list, spread_copies):
-                copy.wait()
-                spread.end()
+            for tick in range(3, spread.ticks):
+                spread.tick(tick)
+            spread_copy.start()
+            spread_copy.wait()
+            spread.end()
 
 
 def attend_backward(n, reps, ga, gs, base, key_mask, q, k, v, ctx, lse, w_qkv, w_out, seqs, out_type, carry, collective_id):
@@ -1408,11 +1392,10 @@
     extra_out, extra_specs = [], []
     extra_scratch = reduce_scratch(chips, carry[0].shape[1], width, hops)
     if len(carry) > 4:
-        for source, streams in zip(carry[4:], (2, 1)):
-            extra_out.append(jax.ShapeDtypeStruct((streams, padded(source.shape[1], reps), width), bf16))
-            extra_specs.append(ANY)
-            extra_scratch += spread_scratch(source.shape[1], width, reps, streams)
-        extra_scratch.append(pltpu.SemaphoreType.DMA((2,)))
+        spread_rows = carry[4].shape[1]
+        extra_out = [jax.ShapeDtypeStruct((2, padded(spread_rows, reps), width), bf16)]
+        extra_specs = [ANY]
+        extra_scratch += spread_scratch(spread_rows, width, reps) + [pltpu.SemaphoreType.DMA]
     return pl.pallas_call(
         functools.partial(
             attend_backward_kernel, n, reps, seqs, (len(w_qkv), len(w_qkv) + len(w_out)), len(carry) > 4
@@ -1636,7 +1619,7 @@
     grad = cotangent.reshape(rows, width)
     sum_rows = [None] * LAYERS
     attend_halves, attend_reduced = None, None
-    down_done, up_done, attend_done = [None] * LAYERS, [None] * LAYERS, [None] * LAYERS
+    ffn_done, attend_done = [None] * LAYERS, [None] * LAYERS
     ffn_reduced = None
     for layer in range(LAYERS - 1, -1, -1):
         first = layer == LAYERS - 1
@@ -1647,7 +1630,7 @@
         )
         gs1, ga1, sums, up_sum, down_keep, down_send, up_keep, up_send = results[:8]
         if not first:
-            attend_reduced, down_done[layer + 1] = results[8:]
+            attend_reduced, ffn_done[layer + 1] = results[8:]
         ffn_halves = (
             down_keep,
             up_keep.reshape(n // 2, -1, width),
@@ -1656,23 +1639,22 @@
         )
         results = attend_backward(
             n, reps, ga1, gs1, base, key_mask, q, k, v, ctx, lse, qkv[layer], out[layer], seqs,
-            f32 if layer else bf16, ffn_halves + (() if first else (attend_reduced, ffn_reduced)), 20 + layer,
+            f32 if layer else bf16, ffn_halves + (() if first else (attend_reduced,)), 20 + layer,
         )
         grad, proj_sums = results[:2]
         attend_halves, ffn_reduced = results[2:6], results[6]
         if not first:
-            attend_done[layer + 1], up_done[layer + 1] = results[7:]
+            attend_done[layer + 1] = results[7]
         sum_rows[layer] = (sums, proj_sums, up_sum)
     grad_tokens = grad.reshape(seqs, seq, width)
-    ffn_last, attend_done[0], small_total = last_sums(
+    ffn_done[0], attend_done[0], small_total = last_sums(
         n, reps, attend_halves, ffn_reduced, [array for arrays in sum_rows for array in arrays], 30
     )
-    down_done[0], up_done[0] = ffn_last[:1], ffn_last[1:]
 
     ffn_rows, attend_rows = units // n, 2 * per
     both_attend = jnp.stack([done[:, :attend_rows] for done in attend_done])
-    grad_down = jnp.stack([done[0, :ffn_rows] for done in down_done]).astype(f32)
-    grad_up = jnp.stack([done[0, :ffn_rows] for done in up_done])
+    grad_down = jnp.stack([done[0, :ffn_rows] for done in ffn_done]).astype(f32)
+    grad_up = jnp.stack([done[1, :ffn_rows] for done in ffn_done])
     grad_up = grad_up.reshape(LAYERS, units // width, per, width).transpose(0, 2, 1, 3)
     grad_up = grad_up.reshape(LAYERS, per, units).astype(f32)
     parts = both_attend.reshape(LAYERS, 4, per, width)

time: 493 us -> 493 us (level)
    pallas_call x2, Pallas kernels: 131 us -> 122 us  [attend_backward(): pl.pallas_call(functools.partial(attend_backward_kernel, n, reps, seqs, (...]
    pallas_call x2, Pallas kernels: 96.8 us -> 104 us  [ffn_backward(): pl.pallas_call(functools.partial(ffn_backward_kernel, n, reps, (len(w_up)...]
where the time goes in v6:
time: 493 us; the launch traced here: 492 us
  Pallas kernels  472 us (96%)
  local copies, waits for them, and re-layouts  13.2 us (3%)
  other arithmetic  5.73 us (1%)
    pallas_call x2, Pallas kernels, attend_backward(): pl.pallas_call(functools.partial(attend_backward_kernel, n, reps, seqs, (...  122 us
    pallas_call x2, Pallas kernels, ffn_backward(): pl.pallas_call(functools.partial(ffn_backward_kernel, n, reps, (len(w_up)...  104 us
    pallas_call x2, Pallas kernels, attend_forward(): pl.pallas_call(functools.partial(attend_forward_kernel, n, seqs, layer, (...  85.5 us
    pallas_call x2, Pallas kernels, ffn_forward(): pl.pallas_call(functools.partial(ffn_forward_kernel, n, last, layer + 1,...  67.7 us
    pallas_call x1, Pallas kernels, last_sums(): pl.pallas_call(functools.partial(last_sums_kernel, n, reps), out_shape=(j...  65 us
    pallas_call x1, Pallas kernels, gather_weights(): pl.pallas_call(functools.partial(gather_kernel, n, layer, parts, len(shar...  27.7 us

profile of v6, /device:TPU:0, one launch (start us, length us, event | category | flops | bytes accessed | tf_op | source)
XLA Modules:
  0.0 492.2 jit_solution(5656022383051188644)
XLA Ops:
  0.7 0.8 reshape.166
  1.4 0.7 copy.24
  2.2 0.7 reshape.164
  3.5 27.7 %gather_weights.1 = (f32[256,128]{1,0:T(8,128)}, bf16[768,1152]{1,0:T(8,128)(2,1)}, bf16[768,1152]{1,0:T(8,128)(2,1)}, bf16[768,384]{1,0:T(8,128)(2,1)}, bf16[768,384]{1,0:T(8,128)(2,1)}) custom-call(bf16[2,96,2304]{2,1,0:T(8,128)(2,1)} %refs_6_.1, bf16[2,96,768]{2,1,0:T(8,128)(2,1)} %refs_7_.1, f32[1,32,128]{2,1,0:T(8,128)} %fusion.3.refs_2_), custom_call_target="tpu_custom_call" | custom-call | tf_op jit(solution)/shard_map/gather_weights/pallas_call | solution.py:186
  31.2 0.9 reshape.168
  33.9 1.0 copy.46
  34.9 47.3 %attend_forward.2 = (bf16[1024,768]{1,0:T(8,128)(2,1)}, bf16[1024,768]{1,0:T(8,128)(2,1)}, bf16[1024,768]{1,0:T(8,128)(2,1)}, bf16[1024,768]{1,0:T(8,128)(2,1)},...) custom-call(bf16[1024,768]{1,0:T(8,128)(2,1)} %bitcast.81, ...), custom_call_target="tpu_custom_call" | custom-call | flops 11274289152 | bytes 15728640 | tf_op jit(solution)/shard_map/attend_forward/pallas_call | solution.py:679
  82.3 0.6 reshape.174.up_bias_ref
  82.9 1.0 copy.48
  83.9 38.8 %ffn_forward.2 = (bf16[1024,3072]{1,0:T(8,128)(2,1)}, bf16[1024,3072]{1,0:T(8,128)(2,1)}, bf16[1024,768]{1,0:T(8,128)(2,1)}, f32[1024,1]{1,0:T(8,128)}, f32[1024...) custom-call(f32[1024,768]{1,0:T(8,128)} %get-tuple-element.100.mid_r, ...), custom_call_target="tpu_custom_call" | custom-call | flops 19327352832 | bytes 25165824 | tf_op jit(solution)/shard_map/ffn_forward/pallas_call | solution.py:859
  122.8 38.2 %attend_forward.3 = (bf16[1024,768]{1,0:T(8,128)(2,1)}, bf16[1024,768]{1,0:T(8,128)(2,1)}, bf16[1024,768]{1,0:T(8,128)(2,1)}, bf16[1024,768]{1,0:T(8,128)(2,1)},...) custom-call(f32[1024,768]{1,0:T(8,128)} %get-tuple-element.108.x_ref, ...), custom_call_target="tpu_custom_call" | custom-call | flops 11274289152 | bytes 15728640 | tf_op jit(solution)/shard_map/attend_forward/pallas_call | solution.py:679
  161.0 28.8 %ffn_forward.3 = (bf16[1024,3072]{1,0:T(8,128)(2,1)}, bf16[1024,3072]{1,0:T(8,128)(2,1)}, bf16[1024,768]{1,0:T(8,128)(2,1)}, f32[1024,1]{1,0:T(8,128)}, bf16[1024,768]{1,0:T(8,128)(2,1)}) custom-call(f32[1024,768]{1,0:T(8,128)} %get-tuple-element.113.mid_ref, bf16[1024,768]{1,0:T(8,128)(2,1)} %get-tuple-element.114.low_ref, ...), custom_call_target="tpu_custom_call" | custom-call | flops 19327352832 | bytes 25165824 | tf_op jit(solution)/shard_map/ffn_forward/pallas_call | solution.py:859
  189.8 43.8 %ffn_backward.2 = (f32[1024,768]{1,0:T(8,128)}, bf16[1024,768]{1,0:T(8,128)(2,1)}, f32[8,768]{1,0:T(8,128)}, f32[1,3072]{1,0:T(1,128)}, bf16[4,384,768]{2,1,0:T(...) custom-call(bf16[1024,768]{1,0:T(8,128)(2,1)} %bitcast.80, ...), custom_call_target="tpu_custom_call" | custom-call | flops 24159191040 | bytes 25165824 | tf_op jit(solution)/shard_map/ffn_backward/pallas_call | solution.py:1133
  233.6 60.5 %attend_backward.2 = (f32[1024,768]{1,0:T(8,128)}, f32[8,768]{1,0:T(8,128)}, bf16[4,192,768]{2,1,0:T(8,128)(2,1)}, bf16[4,192,768]{2,1,0:T(8,128)(2,1)}, bf16[4,...) custom-call(bf16[1024,768]{1,0:T(8,128)(2,1)} %get-tuple-element.128.ga_ref, ...), custom_call_target="tpu_custom_call" | custom-call | flops 25769803776 | bytes 15728640 | tf_op jit(solution)/shard_map/attend_backward/pallas_call | solution.py:1399
  294.1 60.5 %ffn_backward.3 = (f32[1024,768]{1,0:T(8,128)}, bf16[1024,768]{1,0:T(8,128)(2,1)}, f32[8,768]{1,0:T(8,128)}, f32[1,3072]{1,0:T(1,128)}, bf16[4,384,768]{2,1,0:T(...) custom-call(f32[1024,768]{1,0:T(8,128)} %get-tuple-element.140.g_ref, ...), custom_call_target="tpu_custom_call" | custom-call | flops 24159191040 | bytes 25165824 | tf_op jit(solution)/shard_map/ffn_backward/pallas_call | solution.py:1133
  354.6 61.1 %attend_backward.3 = (bf16[1024,768]{1,0:T(8,128)(2,1)}, f32[8,768]{1,0:T(8,128)}, bf16[4,192,768]{2,1,0:T(8,128)(2,1)}, bf16[4,192,768]{2,1,0:T(8,128)(2,1)}, b...) custom-call(bf16[1024,768]{1,0:T(8,128)(2,1)} %get-tuple-element.152, ...), custom_call_target="tpu_custom_call" | custom-call | flops 25769803776 | bytes 15728640 | tf_op jit(solution)/shard_map/attend_backward/pallas_call | solution.py:1399
  415.7 65.0 %last_sums.1 = (bf16[2,384,768]{2,1,0:T(8,128)(2,1)}, bf16[2,192,768]{2,1,0:T(8,128)(2,1)}, f32[32,768]{1,0:T(8,128)}) custom-call(bf16[4,192,768]{2,1,0:T(8,128)(2,1)} %get-tuple-element.165.a_keep, bf16[4,192,768]{2,1,0:T(8,128)(2,1)} %get-tuple-element.166.b_keep, bf16[4,192,768]{2,1,0:T(8,128)(2,1)} %get-tuple-element.167.a_send, ...), custom_call_target="tpu_custom_call" | custom-call | tf_op jit(solution)/shard_map/last_sums/pallas_call | solution.py:1533
  480.8 1.1 convert_bitcast_fusion.1
  481.9 1.3 copy.43
  483.2 0.9 fusion.2
  484.8 0.7 copy-done.4
  485.5 1.6 pad_maximum_fusion
  487.4 1.7 copy.44
  491.1 1.1 copy.52
  (41 shorter events, 4.8 us)
Async XLA Ops:
  0.6 33.2 %copy-start.6 = (s32[2]{0:T(128)S(1)}, s32[2]{0:T(128)}, u32[]{:S(2)}) copy-start(s32[2]{0:T(128)} %param.13) | copy-start | bytes 28
  415.7 65.1 %copy-start = (bf16[2,192,768]{2,1,0:T(8,128)(2,1)S(1)}, bf16[2,192,768]{2,1,0:T(8,128)(2,1)}, u32[]{:S(2)}) copy-start(bf16[2,192,768]{2,1,0:T(8,128)(2,1)} %get-tuple-element.177) | copy-start | bytes 1769476
  481.9 1.3 copy-start.1
  483.2 1.5 copy-start.3
  484.1 1.4 copy-start.4
  487.4 1.7 copy-start.5
  487.4 3.7 copy-start.2
